TPU v7x, 128 devices: a whole 4x4x4 slice. The times are simulated.
128 devices in a mesh: dp: 4 (over x), ctx: 8 (over y, core), head: 4 (over z).
Axes of the slice: x: 4, y: 4, z: 4, core: 2. Of those that a mesh axis runs over, the one named last changes fastest.
Arguments:
- x_rows: bfloat16 [16384, 8192], P(('dp', 'ctx', 'head')), may hold values from -6 to 6
- b_rows: bfloat16 [16384, 1024], P(('dp', 'ctx', 'head')), may hold values from -3 to 3
- c_rows: bfloat16 [16384, 1024], P(('dp', 'ctx', 'head')), may hold values from -3 to 3
- dt_rows: bfloat16 [16384, 128], P(('dp', 'ctx', 'head')), may hold values from -5 to 5
- length_plan: int32 [8192], replicated, may hold values from 0 to 8191, as said below
- trace_lengths: int32 [4, 6], P('dp'), may hold values from 1 to 2048, 4096 in all within a row
- x_taps: float32 [4, 8192], P(None, 'head'), may hold values from -3 to 3
- bc_taps: float32 [2, 4, 1024], P(None, None, 'head'), may hold values from -3 to 3
- x_bias: float32 [8192], P('head'), may hold values from -3 to 3
- bc_bias: float32 [2, 1024], P(None, 'head'), may hold values from -1.5 to 1.5
- dt_bias: float32 [128], P('head'), may hold values from -1.5 to 0.5
- decay_rate: float32 [128], P('head'), may hold values from 0.00012207031 to 0.05
- skip_gain: float32 [128], P('head'), may hold values from 0.25 to 4
- out_grad: bfloat16 [16384, 8192], P(('dp', 'ctx'), 'head'), may hold values from -6 to 6
Outputs:
- mixer_out: bfloat16 [16384, 8192], P(('dp', 'ctx'), 'head')
- x_rows_grad: bfloat16 [16384, 8192], P(('dp', 'ctx', 'head'))
- b_rows_grad: bfloat16 [16384, 1024], P(('dp', 'ctx', 'head'))
- c_rows_grad: bfloat16 [16384, 1024], P(('dp', 'ctx', 'head'))
- dt_rows_grad: bfloat16 [16384, 128], P(('dp', 'ctx', 'head'))
- x_taps_grad: float32 [4, 8192], P(None, 'head')
- bc_taps_grad: float32 [2, 4, 1024], P(None, None, 'head')
- x_bias_grad: float32 [8192], P('head')
- bc_bias_grad: float32 [2, 1024], P(None, 'head')
- dt_bias_grad: float32 [128], P('head')
- decay_rate_grad: float32 [128], P('head')
- skip_gain_grad: float32 [128], P('head')
Inputs may be any that keep to these rules, and one draw needn't show every extreme that they name: A permutation: each loader block fills exactly one packed block. Packed block g belongs to owner g // 256; loader block b sits on loader device b // 64 of owner b // 256 and head index b // 64 % 4. The head index of length_plan[g] is g % 256 // 64. One loader device sends at most 4 blocks to one owner, and some loader device sends exactly 4 blocks to some owner.
All inputs are finite; a program needn't handle non-finite values.
Results may differ from a plain program's by a relative error of at most 0.015.
Values may be sent and summed in bfloat16 or wider, within the bound.
A program may use at most 128 MiB of HBM per device.

v0:
```python
import jax
import jax.numpy as jnp
from jax import lax
from jax.sharding import PartitionSpec as P

HEADS = 128
HEAD_DIM = 64
GROUPS = 8
STATE = 128
KERNEL = 4
STRETCH = 256
BLK = 2


head_batch = 4


def passed_along(value, axis, steps):
    count = lax.axis_size(axis)
    first, last = (max(0, -steps), min(count, count - steps))
    return lax.ppermute(value, axis, [(source, source + steps) for source in range(first, last)])


def segment_of(ends, positions):
    return jnp.sum((positions[:, None] >= ends[None, :]).astype(jnp.int32), axis=1)


def mask_parts(lengths_row, start, count):
    ends = jnp.cumsum(lengths_row)
    positions = start + jnp.arange(count, dtype=jnp.int32)
    labels = segment_of(ends, positions)
    behind = positions[:, None] - (KERNEL - 1) + jnp.arange(KERNEL, dtype=jnp.int32)[None, :]
    behind_labels = segment_of(ends, behind.reshape(-1)).reshape(count, KERNEL)
    conv_keep = ((behind >= 0) & (behind_labels == labels[:, None])).astype(jnp.float32)
    earlier = segment_of(ends, jnp.reshape(start - 1, (1,)))[0]
    before = jnp.where(start > 0, earlier, -1)
    stretches = count // STRETCH
    grid = labels.reshape(stretches, STRETCH)
    prior = jnp.concatenate([jnp.reshape(before, (1,)), grid[:-1, -1]])
    lower = (
        jnp.arange(STRETCH, dtype=jnp.int32)[:, None]
        >= jnp.arange(STRETCH, dtype=jnp.int32)[None, :]
    )
    same = (grid[:, :, None] == grid[:, None, :]) & lower[None]
    last_keep = (grid == grid[:, -1:]).astype(jnp.float32)
    first_keep = (grid == prior[:, None]).astype(jnp.float32)
    carry_keep = (grid[:, -1] == prior).astype(jnp.float32)
    return (conv_keep, same, last_keep, first_keep, carry_keep)


def convolve(padded, weight, bias, keep):
    count = keep.shape[0]
    total = jnp.broadcast_to(bias, (count, bias.shape[0]))
    for tap_at in range(KERNEL):
        total = (
            total + weight[tap_at] * padded[tap_at : tap_at + count] * keep[:, tap_at : tap_at + 1]
        )
    return jax.nn.silu(total).astype(jnp.bfloat16)


def contract(form, left, right):
    return jnp.einsum(form, left, right, preferred_element_type=jnp.float32)


def decay_parts(dt_raw, shift_part, rate_part):
    step_size = jax.nn.softplus(dt_raw.astype(jnp.float32) + shift_part)
    count = step_size.shape[0]
    folded = step_size.reshape(count // STRETCH, STRETCH, -1)
    log_decay = jnp.cumsum(-rate_part * folded, axis=1)
    return (folded, log_decay)


def stretch_states(inner_f, b_low, step_size, log_decay, last_keep, carry_keep):
    to_end = jnp.exp(log_decay[:, -1:, :] - log_decay) * last_keep[:, :, None]
    weighted = ((step_size * to_end)[:, :, :, None] * inner_f).astype(jnp.bfloat16)
    e_stretch = contract("kqhp,kqn->khpn", weighted, b_low)
    g_stretch = jnp.exp(log_decay[:, -1, :]) * carry_keep[:, None]
    return (e_stretch, g_stretch)


def ssd_local(
    x_part,
    b_full,
    c_full,
    dt_raw,
    shift_part,
    rate_part,
    skip_part,
    same,
    last_keep,
    first_keep,
    carry_keep,
    h_in,
):
    count = x_part.shape[0]
    stretches = count // STRETCH
    width = h_in.shape[0]
    step_size, log_decay = decay_parts(dt_raw, shift_part, rate_part)
    inner_f = x_part.astype(jnp.float32).reshape(stretches, STRETCH, width, HEAD_DIM)
    b_low = b_full.astype(jnp.bfloat16).reshape(stretches, STRETCH, STATE)
    c_low = c_full.astype(jnp.bfloat16).reshape(stretches, STRETCH, STATE)
    x_step = (step_size[:, :, :, None] * inner_f).astype(jnp.bfloat16)
    intersections = contract("kqn,ksn->kqs", c_low, b_low)
    decay_h = jnp.swapaxes(log_decay, 1, 2)
    gaps = jnp.where(same[:, None], decay_h[:, :, :, None] - decay_h[:, :, None, :], -jnp.inf)
    mixing = (intersections[:, None] * jnp.exp(gaps)).astype(jnp.bfloat16)
    inner = contract("khqs,kshp->kqhp", mixing, x_step)
    e_stretch, g_stretch = stretch_states(
        inner_f, b_low, step_size, log_decay, last_keep, carry_keep
    )
    state = h_in
    entering = []
    for stretch_at in range(stretches):
        entering.append(state)
        state = g_stretch[stretch_at][:, None, None] * state + e_stretch[stretch_at]
    entering = jnp.stack(entering)
    gains = jnp.exp(log_decay) * first_keep[:, :, None]
    carried = jnp.einsum(
        "kqn,khpn->kqhp",
        c_full.reshape(stretches, STRETCH, STATE),
        entering,
        precision=lax.Precision.HIGHEST,
    )
    total = inner + carried * gains[:, :, :, None] + skip_part[:, None] * inner_f
    return (total.astype(jnp.bfloat16).reshape(count, width * HEAD_DIM), state)


def bucket(targets, groups, depth):
    count = targets.shape[0]
    order = jnp.arange(count, dtype=jnp.int32)
    ranks = jnp.sum(
        ((targets[:, None] == targets[None, :]) & (order[None, :] < order[:, None])).astype(
            jnp.int32
        ),
        axis=1,
    )
    table = jnp.full((groups * depth,), -1, jnp.int32).at[targets * depth + ranks].set(order)
    return table.reshape(groups, depth)


def place(rows, table):
    picked = rows[jnp.maximum(table, 0)]
    return jnp.where((table >= 0)[:, :, None, None], picked, jnp.zeros((), rows.dtype))


def unplace(rows, spots, count):
    total = rows.shape[0]
    source = (
        jnp.full((count,), total, jnp.int32)
        .at[jnp.where(spots >= 0, spots, count)]
        .set(jnp.arange(total, dtype=jnp.int32), mode="drop")
    )
    padded = jnp.concatenate([rows, jnp.zeros((1,) + rows.shape[1:], rows.dtype)])
    return padded[source]


def route_tables(length_plan, holders, sender, owner, groups, depth, span):
    every = length_plan.shape[0]
    slot_of = jnp.zeros((every,), jnp.int32).at[length_plan].set(jnp.arange(every, dtype=jnp.int32))
    targets = slot_of[holders] // span
    tables = jax.vmap(lambda row: bucket(row, groups, depth))(targets)
    mine = tables[sender]
    incoming = tables[:, owner]
    names = jnp.where(
        incoming >= 0, jnp.take_along_axis(holders, jnp.maximum(incoming, 0), axis=1), -1
    )
    return (mine, names.reshape(-1))


def locate(names, wanted, every):
    where_is = (
        jnp.zeros((every,), jnp.int32)
        .at[jnp.where(names >= 0, names, every)]
        .set(jnp.arange(names.shape[0], dtype=jnp.int32), mode="drop")
    )
    return where_is[wanted]


def flatten_slots(block):
    return block.reshape((-1,) + block.shape[2:])


def on_device(
    x_rows,
    b_rows,
    c_rows,
    dt_rows,
    length_plan,
    trace_lengths,
    x_taps,
    bc_taps,
    x_bias,
    bc_bias,
    dt_bias,
    decay_rate,
    skip_gain,
    out_grad,
):
    context_size = lax.axis_size("ctx")
    head_ways = lax.axis_size("head")
    owner_count = lax.axis_size("dp") * context_size
    owner = lax.axis_index("dp") * context_size + lax.axis_index("ctx")
    head_at = lax.axis_index("head")
    every = length_plan.shape[0]
    lblocks = x_rows.shape[0] // BLK
    oblocks = lblocks * head_ways
    rows_dev = oblocks * BLK
    depth = 2 * (lblocks // owner_count)
    sources = jnp.arange(owner_count, dtype=jnp.int32)
    holders = (sources[:, None] * head_ways + head_at) * lblocks + jnp.arange(
        lblocks, dtype=jnp.int32
    )[None, :]
    mine, names = route_tables(length_plan, holders, owner, owner, owner_count, depth, oblocks)
    loaded = [
        part.reshape(lblocks, BLK, part.shape[1]) for part in (x_rows, b_rows, c_rows, dt_rows)
    ]
    landed = (
        lax.all_to_all(
            place(loaded[0], mine), ("dp", "ctx"), split_axis=0, concat_axis=0, tiled=True
        ),
        lax.all_to_all(
            place(loaded[1], mine), ("dp", "ctx"), split_axis=0, concat_axis=0, tiled=True
        ),
        lax.all_to_all(
            place(loaded[2], mine), ("dp", "ctx"), split_axis=0, concat_axis=0, tiled=True
        ),
        lax.all_to_all(
            place(loaded[3], mine), ("dp", "ctx"), split_axis=0, concat_axis=0, tiled=True
        ),
    )
    flat = [flatten_slots(part) for part in landed]
    wanted = lax.dynamic_slice_in_dim(length_plan, owner * oblocks + head_at * lblocks, lblocks)
    spots = locate(names, wanted, every)
    quarter = [part[spots].reshape(lblocks * BLK, part.shape[2]) for part in flat]
    x_pack, b_pack, c_pack, dt_pack = (
        lax.all_to_all(quarter[0], "head", split_axis=1, concat_axis=0, tiled=True),
        lax.all_to_all(quarter[1], "head", split_axis=1, concat_axis=0, tiled=True),
        lax.all_to_all(quarter[2], "head", split_axis=1, concat_axis=0, tiled=True),
        lax.all_to_all(quarter[3], "head", split_axis=1, concat_axis=0, tiled=True),
    )
    start = lax.axis_index("ctx") * rows_dev
    conv_keep, same, last_keep, first_keep, carry_keep = mask_parts(
        trace_lengths[0], start, rows_dev
    )
    tail = KERNEL - 1
    rim_x, rim_b, rim_c = passed_along((x_pack[-tail:], b_pack[-tail:], c_pack[-tail:]), "ctx", 1)
    pads = (
        jnp.concatenate([rim_x, x_pack]).astype(jnp.float32),
        jnp.concatenate([rim_b, b_pack]).astype(jnp.float32),
        jnp.concatenate([rim_c, c_pack]).astype(jnp.float32),
    )
    weights = (x_taps, bc_taps[0], bc_taps[1], x_bias, bc_bias[0], bc_bias[1])

    def conv_all(pads, weights):
        return (
            convolve(pads[0], weights[0], weights[3], conv_keep),
            convolve(pads[1], weights[1], weights[4], conv_keep),
            convolve(pads[2], weights[2], weights[5], conv_keep),
        )

    (x_conv, b_conv, c_conv), conv_pull = jax.vjp(conv_all, pads, weights)
    b_wide = b_conv.astype(jnp.float32)
    c_wide = c_conv.astype(jnp.float32)
    heads_dev = dt_pack.shape[1]
    batches = heads_dev // head_batch
    per_group = HEADS // GROUPS // head_batch
    groups_dev = batches // per_group

    def batch_inputs(batch_at):
        group = batch_at // per_group
        return (
            lax.dynamic_slice_in_dim(
                x_conv, batch_at * head_batch * HEAD_DIM, head_batch * HEAD_DIM, 1
            ),
            lax.dynamic_slice_in_dim(b_wide, group * STATE, STATE, 1),
            lax.dynamic_slice_in_dim(c_wide, group * STATE, STATE, 1),
            lax.dynamic_slice_in_dim(dt_pack, batch_at * head_batch, head_batch, 1),
            lax.dynamic_slice_in_dim(dt_bias, batch_at * head_batch, head_batch),
            lax.dynamic_slice_in_dim(decay_rate, batch_at * head_batch, head_batch),
            lax.dynamic_slice_in_dim(skip_gain, batch_at * head_batch, head_batch),
            lax.dynamic_slice_in_dim(
                out_grad, batch_at * head_batch * HEAD_DIM, head_batch * HEAD_DIM, 1
            ),
        )

    def summary(batch_at):
        x_part, b_full, c_full, dt_raw, shift_part, rate_part, skip_part, grad_part = batch_inputs(
            batch_at
        )
        step_size, log_decay = decay_parts(dt_raw, shift_part, rate_part)
        stretches = log_decay.shape[0]
        inner_f = x_part.astype(jnp.float32).reshape(stretches, STRETCH, head_batch, HEAD_DIM)
        b_low = b_full.astype(jnp.bfloat16).reshape(stretches, STRETCH, STATE)
        e_stretch, g_stretch = stretch_states(
            inner_f, b_low, step_size, log_decay, last_keep, carry_keep
        )
        gains = jnp.exp(log_decay) * first_keep[:, :, None]
        grad_f = (
            grad_part.astype(jnp.float32).reshape(stretches, STRETCH, head_batch, HEAD_DIM)
            * gains[:, :, :, None]
        )
        touched = jnp.einsum(
            "kqhp,kqn->khpn",
            grad_f,
            c_full.reshape(stretches, STRETCH, STATE),
            precision=lax.Precision.HIGHEST,
        )
        state = jnp.zeros((head_batch, HEAD_DIM, STATE), jnp.float32)
        pulled = jnp.zeros((head_batch, HEAD_DIM, STATE), jnp.float32)
        factor = jnp.ones((head_batch,), jnp.float32)
        for stretch_at in range(stretches):
            state = g_stretch[stretch_at][:, None, None] * state + e_stretch[stretch_at]
            pulled = pulled + factor[:, None, None] * touched[stretch_at]
            factor = factor * g_stretch[stretch_at]
        return (factor, state, pulled)

    g_parts, e_parts, pull_parts = lax.map(summary, jnp.arange(batches, dtype=jnp.int32))
    g_all = g_parts.reshape(heads_dev)
    e_all = e_parts.reshape(heads_dev, HEAD_DIM, STATE)
    pull_all = pull_parts.reshape(heads_dev, HEAD_DIM, STATE)

    def forward_turn(turn, entering):
        return passed_along(g_all[:, None, None] * entering + e_all, "ctx", 1)

    entering = lax.fori_loop(0, context_size - 1, forward_turn, jnp.zeros_like(e_all))

    def backward_turn(turn, leaving):
        return passed_along(pull_all + g_all[:, None, None] * leaving, "ctx", -1)

    leaving = lax.fori_loop(0, context_size - 1, backward_turn, jnp.zeros_like(e_all))

    def backward_batch(batch_at):
        x_part, b_full, c_full, dt_raw, shift_part, rate_part, skip_part, grad_part = batch_inputs(
            batch_at
        )
        start_state = lax.dynamic_slice_in_dim(entering, batch_at * head_batch, head_batch, 0)
        end_grad = lax.dynamic_slice_in_dim(leaving, batch_at * head_batch, head_batch, 0)

        def local(x_in, b_in, c_in, dt_in, shift_in, rate_in, skip_in):
            return ssd_local(
                x_in,
                b_in,
                c_in,
                dt_in,
                shift_in,
                rate_in,
                skip_in,
                same,
                last_keep,
                first_keep,
                carry_keep,
                start_state,
            )

        (mixed, _), pull_fn = jax.vjp(
            local, x_part, b_full, c_full, dt_raw, shift_part, rate_part, skip_part
        )
        return (mixed,) + tuple(pull_fn((grad_part, end_grad)))

    mixed, grad_xc, grad_bc, grad_cc, grad_dt, grad_shift, grad_rate, grad_skip = lax.map(
        backward_batch, jnp.arange(batches, dtype=jnp.int32)
    )
    mixer_out = jnp.swapaxes(mixed, 0, 1).reshape(rows_dev, heads_dev * HEAD_DIM)
    x_conv_grad = jnp.swapaxes(grad_xc, 0, 1).reshape(rows_dev, heads_dev * HEAD_DIM)
    b_conv_grad = jnp.swapaxes(
        grad_bc.reshape(groups_dev, per_group, rows_dev, STATE).sum(axis=1), 0, 1
    ).reshape(rows_dev, groups_dev * STATE)
    c_conv_grad = jnp.swapaxes(
        grad_cc.reshape(groups_dev, per_group, rows_dev, STATE).sum(axis=1), 0, 1
    ).reshape(rows_dev, groups_dev * STATE)
    dt_pack_grad = jnp.swapaxes(grad_dt, 0, 1).reshape(rows_dev, heads_dev)
    pad_grads, weight_grads = conv_pull(
        (x_conv_grad, b_conv_grad.astype(jnp.bfloat16), c_conv_grad.astype(jnp.bfloat16))
    )
    back_x, back_b, back_c = passed_along(
        (pad_grads[0][:tail], pad_grads[1][:tail], pad_grads[2][:tail]), "ctx", -1
    )
    x_pack_grad = pad_grads[0][tail:].at[-tail:].add(back_x).astype(jnp.bfloat16)
    b_pack_grad = pad_grads[1][tail:].at[-tail:].add(back_b).astype(jnp.bfloat16)
    c_pack_grad = pad_grads[2][tail:].at[-tail:].add(back_c).astype(jnp.bfloat16)
    summed = lax.psum(
        (
            weight_grads[0],
            jnp.stack([weight_grads[1], weight_grads[2]]),
            weight_grads[3],
            jnp.stack([weight_grads[4], weight_grads[5]]),
            grad_shift.reshape(-1),
            grad_rate.reshape(-1),
            grad_skip.reshape(-1),
        ),
        ("dp", "ctx"),
    )
    homeward = (
        lax.all_to_all(x_pack_grad, "head", split_axis=0, concat_axis=1, tiled=True),
        lax.all_to_all(b_pack_grad, "head", split_axis=0, concat_axis=1, tiled=True),
        lax.all_to_all(c_pack_grad, "head", split_axis=0, concat_axis=1, tiled=True),
        lax.all_to_all(dt_pack_grad, "head", split_axis=0, concat_axis=1, tiled=True),
    )
    blocks = [part.reshape(lblocks, BLK, part.shape[1]) for part in homeward]
    slotted = [
        unplace(part, spots, owner_count * depth).reshape((owner_count, depth) + part.shape[1:])
        for part in blocks
    ]
    returned = (
        lax.all_to_all(slotted[0], ("dp", "ctx"), split_axis=0, concat_axis=0, tiled=True),
        lax.all_to_all(slotted[1], ("dp", "ctx"), split_axis=0, concat_axis=0, tiled=True),
        lax.all_to_all(slotted[2], ("dp", "ctx"), split_axis=0, concat_axis=0, tiled=True),
        lax.all_to_all(slotted[3], ("dp", "ctx"), split_axis=0, concat_axis=0, tiled=True),
    )
    results = [
        unplace(flatten_slots(part), mine.reshape(-1), lblocks).reshape(
            lblocks * BLK, part.shape[3]
        )
        for part in returned
    ]
    return (
        mixer_out,
        results[0],
        results[1],
        results[2],
        results[3],
        summed[0],
        summed[1],
        summed[2],
        summed[3],
        summed[4],
        summed[5],
        summed[6],
    )


def solution(mesh):
    return jax.shard_map(
        on_device,
        mesh=mesh,
        in_specs=(
            P(("dp", "ctx", "head"), None),
            P(("dp", "ctx", "head"), None),
            P(("dp", "ctx", "head"), None),
            P(("dp", "ctx", "head"), None),
            P(),
            P("dp", None),
            P(None, "head"),
            P(None, None, "head"),
            P("head"),
            P(None, "head"),
            P("head"),
            P("head"),
            P("head"),
            P(("dp", "ctx"), "head"),
        ),
        out_specs=(
            P(("dp", "ctx"), "head"),
            P(("dp", "ctx", "head"), None),
            P(("dp", "ctx", "head"), None),
            P(("dp", "ctx", "head"), None),
            P(("dp", "ctx", "head"), None),
            P(None, "head"),
            P(None, None, "head"),
            P("head"),
            P(None, "head"),
            P("head"),
            P("head"),
            P("head"),
        ),
        check_vma=False,
    )
```

profile of v0, /device:TPU:1, one launch (start us, length us, event | category | flops | bytes accessed | tf_op | source)
XLA Modules:
  0.0 1435.8 jit_solution(15854344978462429324)
XLA Ops:
  1.6 30.5 %scatter_custom_fusion = s32[8192]{0:T(1024)S(1)} fusion(s32[8192]{0:T(1024)S(1)} %compare_select_fusion.4, s32[8192]{0:T(1024)S(1)} %iota.77, s32[]{:T(128)} %constant.344.clone.1), kind=kCustom, calls=%fused_computation.267 | custom fusion | bytes 32772 | tf_op jit(solution)/shard_map/scatter | solution.py:159
  32.1 11.8 gather_fusion
  84.2 20.2 %all_to_all.180 = bf16[32,4,2,1024]{3,2,1,0:T(2,128)(2,1)S(1)} all-to-all(bf16[32,4,2,1024]{3,2,1,0:T(2,128)(2,1)S(1)} %get-tuple-element.1171), channel_id=1, replica_groups=mesh['dp'=4,'ctx'=8,'head'=4] {'dp','ctx'}, dimensions={0} | all-to-all | bytes 1048576 | tf_op jit(solution)/shard_map/all_to_all | solution.py:224
  111.8 11.8 gather_fusion.4
  152.3 44.6 %all-to-all-done.2 = bf16[32,4,2,8192]{3,2,1,0:T(2,128)(2,1)} async-done(((bf16[32,4,2,8192]{3,2,1,0:T(2,128)(2,1)}), bf16[32,4,2,8192]{3,2,1,0:T(2,128)(2,1)}, u32[]{:S(2)}, u32[]{:S(2)}) %all-to-all-start.2) | async-done | bytes 4194336 | tf_op jit(solution)/shard_map/all_to_all | solution.py:218
  236.3 10.1 all-to-all-done.3
  267.2 104.1 %while.68 = (s32[]{:T(128)}, f32[8,4]{1,0:T(8,128)S(1)}, f32[8,4,64,128]{3,2,1,0:T(8,128)}, f32[8,4,64,128]{3,2,1,0:T(8,128)S(1)}, s32[8]{0:T(128)S(1)}, /*index...) while((s32[]{:T(128)}, f32[8,4]{1,0:T(8,128)S(1)}, ...), condition=%wide.region_11.12_spmd, body=%wide.region_8.11_spmd.sunk | while | flops 235989056 | bytes 8997585 | solution.py:317
  372.2 122.4 %while.71 = (s32[]{:T(128)}, f32[32,64,128]{2,1,0:T(8,128)S(1)}, f32[8,4]{1,0:T(8,128)}, f32[32,64,128]{2,1,0:T(8,128)S(1)}, f32[32]{0:T(128)S(1)}, /*index=5*/s32[]{:T(128)}) while((s32[]{:T(128)}, f32[32,64,128]{2,1,0:T(8,128)S(1)}, f32[8,4]{1,0:T(8,128)}, f32[32,64,128]{2,1,0:T(8,128)S(1)}, f32[32]{0:T(128)S(1)}, ...), condition=%wide.wide.region_15.16_spmd, body=%wide.wide.region_14.15_spmd.sunk | while | flops 524290 | bytes 7340269 | solution.py:330
  375.3 14.5 %collective-permute-done.1 = f32[32,64,128]{2,1,0:T(8,128)S(1)} collective-permute-done((f32[32,64,128]{2,1,0:T(8,128)}, f32[32,64,128]{2,1,0:T(8,128)S(1)}, u32[]{:S(2)}, u32[]{:S(2)}) %collective-permute-start.1) | collective-permute-done | bytes 1048608 | tf_op jit(solution)/shard_map/while/body/eval_jaxpr/ppermute | solution.py:21
  392.9 14.4 %collective-permute-done.1 = f32[32,64,128]{2,1,0:T(8,128)S(1)} collective-permute-done((f32[32,64,128]{2,1,0:T(8,128)}, f32[32,64,128]{2,1,0:T(8,128)S(1)}, u32[]{:S(2)}, u32[]{:S(2)}) %collective-permute-start.1) | collective-permute-done | bytes 1048608 | tf_op jit(solution)/shard_map/while/body/eval_jaxpr/ppermute | solution.py:21
  410.3 14.4 %collective-permute-done.1 = f32[32,64,128]{2,1,0:T(8,128)S(1)} collective-permute-done((f32[32,64,128]{2,1,0:T(8,128)}, f32[32,64,128]{2,1,0:T(8,128)S(1)}, u32[]{:S(2)}, u32[]{:S(2)}) %collective-permute-start.1) | collective-permute-done | bytes 1048608 | tf_op jit(solution)/shard_map/while/body/eval_jaxpr/ppermute | solution.py:21
  427.8 14.4 %collective-permute-done.1 = f32[32,64,128]{2,1,0:T(8,128)S(1)} collective-permute-done((f32[32,64,128]{2,1,0:T(8,128)}, f32[32,64,128]{2,1,0:T(8,128)S(1)}, u32[]{:S(2)}, u32[]{:S(2)}) %collective-permute-start.1) | collective-permute-done | bytes 1048608 | tf_op jit(solution)/shard_map/while/body/eval_jaxpr/ppermute | solution.py:21
  445.3 14.4 %collective-permute-done.1 = f32[32,64,128]{2,1,0:T(8,128)S(1)} collective-permute-done((f32[32,64,128]{2,1,0:T(8,128)}, f32[32,64,128]{2,1,0:T(8,128)S(1)}, u32[]{:S(2)}, u32[]{:S(2)}) %collective-permute-start.1) | collective-permute-done | bytes 1048608 | tf_op jit(solution)/shard_map/while/body/eval_jaxpr/ppermute | solution.py:21
  462.7 14.4 %collective-permute-done.1 = f32[32,64,128]{2,1,0:T(8,128)S(1)} collective-permute-done((f32[32,64,128]{2,1,0:T(8,128)}, f32[32,64,128]{2,1,0:T(8,128)S(1)}, u32[]{:S(2)}, u32[]{:S(2)}) %collective-permute-start.1) | collective-permute-done | bytes 1048608 | tf_op jit(solution)/shard_map/while/body/eval_jaxpr/ppermute | solution.py:21
  480.2 14.4 %collective-permute-done.1 = f32[32,64,128]{2,1,0:T(8,128)S(1)} collective-permute-done((f32[32,64,128]{2,1,0:T(8,128)}, f32[32,64,128]{2,1,0:T(8,128)S(1)}, u32[]{:S(2)}, u32[]{:S(2)}) %collective-permute-start.1) | collective-permute-done | bytes 1048608 | tf_op jit(solution)/shard_map/while/body/eval_jaxpr/ppermute | solution.py:21
  494.7 119.9 %while.70 = (s32[]{:T(128)}, f32[32,64,128]{2,1,0:T(8,128)S(1)}, f32[8,4]{1,0:T(8,128)}, f32[32,64,128]{2,1,0:T(8,128)S(1)}, f32[32]{0:T(128)S(1)}, /*index=5*/s32[]{:T(128)}) while((s32[]{:T(128)}, f32[32,64,128]{2,1,0:T(8,128)S(1)}, f32[8,4]{1,0:T(8,128)}, f32[32,64,128]{2,1,0:T(8,128)S(1)}, f32[32]{0:T(128)S(1)}, ...), condition=%wide.wide.region_13.14_spmd, body=%wide.wide.region_12.13_spmd.sunk | while | flops 524290 | bytes 7340269 | solution.py:325
  497.8 12.0 collective-permute-done
  515.3 12.0 collective-permute-done
  532.7 12.0 collective-permute-done
  550.2 12.0 collective-permute-done
  567.7 12.0 collective-permute-done
  585.1 12.0 collective-permute-done
  602.6 12.0 collective-permute-done
  616.9 453.9 %while.69 = (s32[]{:T(128)}, bf16[8,512,256]{1,2,0:T(8,128)(2,1)}, bf16[8,512,256]{1,2,0:T(8,128)(2,1)}, f32[8,512,128]{2,1,0:T(8,128)}, f32[8,512,128]{2,1,0:T(...) while((s32[]{:T(128)}, bf16[8,512,256]{1,2,0:T(8,128)(2,1)}, ...), condition=%wide.region_34.35_spmd.clone, body=%wide.region_16.34_spmd.clone.sunk | while | flops 905941056 | bytes 34788684 | solution.py:360
  646.1 10.1 reduce-window.68
  702.8 10.1 reduce-window.68
  759.5 10.1 reduce-window.68
  1096.0 10.9 multiply_reduce_fusion.8
  1185.5 23.3 %all-to-all-done.8 = bf16[4,128,2048]{2,1,0:T(8,128)(2,1)S(1)} async-done(((bf16[4,128,2048]{2,1,0:T(8,128)(2,1)}), bf16[4,128,2048]{2,1,0:T(8,128)(2,1)S(1)}, u32[]{:S(2)}, u32[]{:S(2)}) %all-to-all-start.8) | async-done | bytes 2097184 | tf_op jit(solution)/shard_map/all_to_all | solution.py:394
  1228.3 11.8 gather_fusion.10
  1251.7 155.4 %all-reduce.38 = (f32[4,2048]{1,0:T(4,128)}, f32[2,4,256]{2,1,0:T(4,128)}, f32[2048]{0:T(1024)}, f32[2,256]{1,0:T(2,128)}, f32[32]{0:T(128)}, /*index=5*/f32[32]{0:T(128)}, f32[32]{0:T(128)}) all-reduce(f32[4,2048]{1,0:T(4,128)S(1)} %pad_add_fusion.8, ...), channel_id=1, replica_groups=mesh['dp'=4,'ctx'=8,'head'=4] {'dp','ctx'}, use_global_device_ids=true, to_apply=%region_43.44 | all-reduce | flops 12896 | bytes 103168 | tf_op jit(solution)/shard_map/psum | solution.py:381
  1413.1 11.7 concatenate.47
  (1553 shorter events, 807.8 us)
Async XLA Ops:
  55.9 17.4 %all-to-all-start = ((bf16[32,4,2,128]{3,2,1,0:T(2,128)(2,1)}), bf16[32,4,2,128]{3,2,1,0:T(2,128)(2,1)S(1)}, u32[]{:S(2)}, u32[]{:S(2)}) async-start(bf16[32,4,2,128]{3,2,1,0:T(2,128)(2,1)} %broadcast_select_fusion.3), calls=%async_computation | async-start | bytes 131072 | tf_op jit(solution)/shard_map/all_to_all | solution.py:227
  74.9 9.3 all-to-all-start.1
  104.4 21.2 %all-to-all-start.6 = ((bf16[32,4,2,1024]{3,2,1,0:T(2,128)(2,1)}), bf16[32,4,2,1024]{3,2,1,0:T(2,128)(2,1)S(1)}, u32[]{:S(2)}, u32[]{:S(2)}) async-start(bf16[32,4,2,1024]{3,2,1,0:T(2,128)(2,1)} %get-tuple-element.1170), calls=%async_computation.6 | async-start | bytes 1048576 | tf_op jit(solution)/shard_map/all_to_all | solution.py:221
  125.5 11.1 all-to-all-start.5
  137.3 59.5 %all-to-all-start.2 = ((bf16[32,4,2,8192]{3,2,1,0:T(2,128)(2,1)}), bf16[32,4,2,8192]{3,2,1,0:T(2,128)(2,1)}, u32[]{:S(2)}, u32[]{:S(2)}) async-start(bf16[32,4,2,8192]{3,2,1,0:T(2,128)(2,1)} %broadcast_select_fusion), calls=%async_computation.2 | async-start | bytes 8388608 | tf_op jit(solution)/shard_map/all_to_all | solution.py:218
  196.9 19.7 %all-to-all-start.7 = ((bf16[128,4,256]{2,0,1:T(8,128)(2,1)}), bf16[128,4,256]{2,0,1:T(8,128)(2,1)S(1)}, u32[]{:S(2)}, u32[]{:S(2)}) async-start(bf16[128,4,256]{2,0,1:T(8,128)(2,1)} %copy.404), calls=%async_computation.7 | async-start | bytes 524288 | tf_op jit(solution)/shard_map/all_to_all | solution.py:237
  216.6 29.8 %all-to-all-start.3 = ((bf16[128,4,2048]{2,0,1:T(8,128)(2,1)}), bf16[128,4,2048]{2,0,1:T(8,128)(2,1)}, u32[]{:S(2)}, u32[]{:S(2)}) async-start(bf16[128,4,2048]{2,0,1:T(8,128)(2,1)} %copy.401), calls=%async_computation.3 | async-start | bytes 4194304 | tf_op jit(solution)/shard_map/all_to_all | solution.py:236
  373.4 16.4 %collective-permute-start.1 = (f32[32,64,128]{2,1,0:T(8,128)}, f32[32,64,128]{2,1,0:T(8,128)S(1)}, u32[]{:S(2)}, u32[]{:S(2)}) collective-permute-start(f32[32,64,128]{2,1,0:T(8,128)} %multiply_add_fusion.13), channel_id=1, source_target_pairs={{4,0},{8,4},{12,8},{16,12},{20,16},{24,20},{28,24},{5,1},{9,5},{13... | collective-permute-start | bytes 3145736 | tf_op jit(solution)/shard_map/while/body/eval_jaxpr/ppermute | solution.py:21
  390.9 16.3 %collective-permute-start.1 = (f32[32,64,128]{2,1,0:T(8,128)}, f32[32,64,128]{2,1,0:T(8,128)S(1)}, u32[]{:S(2)}, u32[]{:S(2)}) collective-permute-start(f32[32,64,128]{2,1,0:T(8,128)} %multiply_add_fusion.13), channel_id=1, source_target_pairs={{4,0},{8,4},{12,8},{16,12},{20,16},{24,20},{28,24},{5,1},{9,5},{13... | collective-permute-start | bytes 3145736 | tf_op jit(solution)/shard_map/while/body/eval_jaxpr/ppermute | solution.py:21
  408.4 16.3 %collective-permute-start.1 = (f32[32,64,128]{2,1,0:T(8,128)}, f32[32,64,128]{2,1,0:T(8,128)S(1)}, u32[]{:S(2)}, u32[]{:S(2)}) collective-permute-start(f32[32,64,128]{2,1,0:T(8,128)} %multiply_add_fusion.13), channel_id=1, source_target_pairs={{4,0},{8,4},{12,8},{16,12},{20,16},{24,20},{28,24},{5,1},{9,5},{13... | collective-permute-start | bytes 3145736 | tf_op jit(solution)/shard_map/while/body/eval_jaxpr/ppermute | solution.py:21
  425.9 16.3 %collective-permute-start.1 = (f32[32,64,128]{2,1,0:T(8,128)}, f32[32,64,128]{2,1,0:T(8,128)S(1)}, u32[]{:S(2)}, u32[]{:S(2)}) collective-permute-start(f32[32,64,128]{2,1,0:T(8,128)} %multiply_add_fusion.13), channel_id=1, source_target_pairs={{4,0},{8,4},{12,8},{16,12},{20,16},{24,20},{28,24},{5,1},{9,5},{13... | collective-permute-start | bytes 3145736 | tf_op jit(solution)/shard_map/while/body/eval_jaxpr/ppermute | solution.py:21
  443.3 16.3 %collective-permute-start.1 = (f32[32,64,128]{2,1,0:T(8,128)}, f32[32,64,128]{2,1,0:T(8,128)S(1)}, u32[]{:S(2)}, u32[]{:S(2)}) collective-permute-start(f32[32,64,128]{2,1,0:T(8,128)} %multiply_add_fusion.13), channel_id=1, source_target_pairs={{4,0},{8,4},{12,8},{16,12},{20,16},{24,20},{28,24},{5,1},{9,5},{13... | collective-permute-start | bytes 3145736 | tf_op jit(solution)/shard_map/while/body/eval_jaxpr/ppermute | solution.py:21
  460.8 16.3 %collective-permute-start.1 = (f32[32,64,128]{2,1,0:T(8,128)}, f32[32,64,128]{2,1,0:T(8,128)S(1)}, u32[]{:S(2)}, u32[]{:S(2)}) collective-permute-start(f32[32,64,128]{2,1,0:T(8,128)} %multiply_add_fusion.13), channel_id=1, source_target_pairs={{4,0},{8,4},{12,8},{16,12},{20,16},{24,20},{28,24},{5,1},{9,5},{13... | collective-permute-start | bytes 3145736 | tf_op jit(solution)/shard_map/while/body/eval_jaxpr/ppermute | solution.py:21
  478.3 16.3 %collective-permute-start.1 = (f32[32,64,128]{2,1,0:T(8,128)}, f32[32,64,128]{2,1,0:T(8,128)S(1)}, u32[]{:S(2)}, u32[]{:S(2)}) collective-permute-start(f32[32,64,128]{2,1,0:T(8,128)} %multiply_add_fusion.13), channel_id=1, source_target_pairs={{4,0},{8,4},{12,8},{16,12},{20,16},{24,20},{28,24},{5,1},{9,5},{13... | collective-permute-start | bytes 3145736 | tf_op jit(solution)/shard_map/while/body/eval_jaxpr/ppermute | solution.py:21
  495.9 14.0 collective-permute-start
  511.0 16.3 %collective-permute-start = (f32[32,64,128]{2,1,0:T(8,128)}, f32[32,64,128]{2,1,0:T(8,128)S(1)}, u32[]{:S(2)}, u32[]{:S(2)}) collective-permute-start(f32[32,64,128]{2,1,0:T(8,128)} %multiply_add_fusion.12), channel_id=1, source_target_pairs={{0,4},{4,8},{8,12},{12,16},{16,20},{20,24},{24,28},{1,5},{5,9},{9,... | collective-permute-start | bytes 3145736 | tf_op jit(solution)/shard_map/while/body/eval_jaxpr/ppermute | solution.py:21
  528.5 16.3 %collective-permute-start = (f32[32,64,128]{2,1,0:T(8,128)}, f32[32,64,128]{2,1,0:T(8,128)S(1)}, u32[]{:S(2)}, u32[]{:S(2)}) collective-permute-start(f32[32,64,128]{2,1,0:T(8,128)} %multiply_add_fusion.12), channel_id=1, source_target_pairs={{0,4},{4,8},{8,12},{12,16},{16,20},{20,24},{24,28},{1,5},{5,9},{9,... | collective-permute-start | bytes 3145736 | tf_op jit(solution)/shard_map/while/body/eval_jaxpr/ppermute | solution.py:21
  545.9 16.3 %collective-permute-start = (f32[32,64,128]{2,1,0:T(8,128)}, f32[32,64,128]{2,1,0:T(8,128)S(1)}, u32[]{:S(2)}, u32[]{:S(2)}) collective-permute-start(f32[32,64,128]{2,1,0:T(8,128)} %multiply_add_fusion.12), channel_id=1, source_target_pairs={{0,4},{4,8},{8,12},{12,16},{16,20},{20,24},{24,28},{1,5},{5,9},{9,... | collective-permute-start | bytes 3145736 | tf_op jit(solution)/shard_map/while/body/eval_jaxpr/ppermute | solution.py:21
  563.4 16.3 %collective-permute-start = (f32[32,64,128]{2,1,0:T(8,128)}, f32[32,64,128]{2,1,0:T(8,128)S(1)}, u32[]{:S(2)}, u32[]{:S(2)}) collective-permute-start(f32[32,64,128]{2,1,0:T(8,128)} %multiply_add_fusion.12), channel_id=1, source_target_pairs={{0,4},{4,8},{8,12},{12,16},{16,20},{20,24},{24,28},{1,5},{5,9},{9,... | collective-permute-start | bytes 3145736 | tf_op jit(solution)/shard_map/while/body/eval_jaxpr/ppermute | solution.py:21
  580.9 16.3 %collective-permute-start = (f32[32,64,128]{2,1,0:T(8,128)}, f32[32,64,128]{2,1,0:T(8,128)S(1)}, u32[]{:S(2)}, u32[]{:S(2)}) collective-permute-start(f32[32,64,128]{2,1,0:T(8,128)} %multiply_add_fusion.12), channel_id=1, source_target_pairs={{0,4},{4,8},{8,12},{12,16},{16,20},{20,24},{24,28},{1,5},{5,9},{9,... | collective-permute-start | bytes 3145736 | tf_op jit(solution)/shard_map/while/body/eval_jaxpr/ppermute | solution.py:21
  598.3 16.3 %collective-permute-start = (f32[32,64,128]{2,1,0:T(8,128)}, f32[32,64,128]{2,1,0:T(8,128)S(1)}, u32[]{:S(2)}, u32[]{:S(2)}) collective-permute-start(f32[32,64,128]{2,1,0:T(8,128)} %multiply_add_fusion.12), channel_id=1, source_target_pairs={{0,4},{4,8},{8,12},{12,16},{16,20},{20,24},{24,28},{1,5},{5,9},{9,... | collective-permute-start | bytes 3145736 | tf_op jit(solution)/shard_map/while/body/eval_jaxpr/ppermute | solution.py:21
  1091.5 40.4 %collective-permute-start.7 = (f32[3,256]{1,0:T(4,128)}, f32[3,256]{1,0:T(4,128)}, u32[]{:S(2)}, u32[]{:S(2)}) collective-permute-start(f32[3,256]{1,0:T(4,128)} %pad_add_fusion.9), channel_id=1, source_target_pairs={{4,0},{8,4},{12,8},{16,12},{20,16},{24,20},{28,24},{5,1},{9,5},{13... | collective-permute-start | bytes 9224 | tf_op jit(solution)/shard_map/ppermute | solution.py:21
  1094.0 48.6 %collective-permute-start.6 = (f32[3,256]{1,0:T(4,128)}, f32[3,256]{1,0:T(4,128)}, u32[]{:S(2)}, u32[]{:S(2)}) collective-permute-start(f32[3,256]{1,0:T(4,128)} %pad_add_fusion.10), channel_id=1, source_target_pairs={{4,0},{8,4},{12,8},{16,12},{20,16},{24,20},{28,24},{5,1},{9,5},{13... | collective-permute-start | bytes 9224 | tf_op jit(solution)/shard_map/ppermute | solution.py:21
  1114.1 7.5 all-to-all-start.14
  1123.3 15.9 %all-to-all-start.15 = ((bf16[32,4,2,128]{3,2,1,0:T(2,128)(2,1)}), bf16[32,4,2,128]{3,2,1,0:T(2,128)(2,1)S(1)}, u32[]{:S(2)}, u32[]{:S(2)}) async-start(bf16[32,4,2,128]{3,2,1,0:T(2,128)(2,1)} %bitcast.83), calls=%async_computation.15 | async-start | bytes 131072 | tf_op jit(solution)/shard_map/all_to_all | solution.py:408
  1139.2 9.5 all-to-all-start.12
  1148.7 10.7 all-to-all-start.10
  1153.0 24.0 %collective-permute-start.5 = (f32[3,2048]{1,0:T(4,128)S(1)}, f32[3,2048]{1,0:T(4,128)S(1)}, u32[]{:S(2)}, u32[]{:S(2)}) collective-permute-start(f32[3,2048]{1,0:T(4,128)S(1)} %pad_add_fusion.6), channel_id=1, source_target_pairs={{4,0},{8,4},{12,8},{16,12},{20,16},{24,20},{28,24},{5,1},{9,5},{13... | collective-permute-start | bytes 73736 | tf_op jit(solution)/shard_map/ppermute | solution.py:21
  1159.4 19.1 %all-to-all-start.13 = ((bf16[32,4,2,1024]{3,2,1,0:T(2,128)(2,1)}), bf16[32,4,2,1024]{3,2,1,0:T(2,128)(2,1)S(1)}, u32[]{:S(2)}, u32[]{:S(2)}) async-start(bf16[32,4,2,1024]{3,2,1,0:T(2,128)(2,1)} %bitcast.79), calls=%async_computation.13 | async-start | bytes 1048576 | tf_op jit(solution)/shard_map/all_to_all | solution.py:407
  1178.6 30.2 %all-to-all-start.8 = ((bf16[4,128,2048]{2,1,0:T(8,128)(2,1)}), bf16[4,128,2048]{2,1,0:T(8,128)(2,1)S(1)}, u32[]{:S(2)}, u32[]{:S(2)}) async-start(bf16[4,128,2048]{2,1,0:T(8,128)(2,1)} %bitcast.428), calls=%async_computation.8 | async-start | bytes 4194304 | tf_op jit(solution)/shard_map/all_to_all | solution.py:394
  1208.8 31.2 %all-to-all-start.11 = ((bf16[32,4,2,1024]{3,2,1,0:T(2,128)(2,1)}), bf16[32,4,2,1024]{3,2,1,0:T(2,128)(2,1)S(1)}, u32[]{:S(2)}, u32[]{:S(2)}) async-start(bf16[32,4,2,1024]{3,2,1,0:T(2,128)(2,1)} %bitcast.441), calls=%async_computation.11 | async-start | bytes 1048576 | tf_op jit(solution)/shard_map/all_to_all | solution.py:406
  1240.1 173.0 %all-to-all-start.9 = ((bf16[32,4,2,8192]{3,2,1,0:T(2,128)(2,1)}), bf16[32,4,2,8192]{3,2,1,0:T(2,128)(2,1)}, u32[]{:S(2)}, u32[]{:S(2)}) async-start(bf16[32,4,2,8192]{3,2,1,0:T(2,128)(2,1)} %bitcast.422), calls=%async_computation.9 | async-start | bytes 8388608 | tf_op jit(solution)/shard_map/all_to_all | solution.py:405
  (237 other events, 2463.1 us)
where the time goes:
time: 1460 us; the launch traced here: 1440 us
  local copies, waits for them, and re-layouts  331 us (23%)
  other arithmetic  308 us (21%)
  waiting for transfers between devices  279 us (19%)
  blocking collectives  176 us (12%)
  starting transfers between devices  141 us (10%)
  matrix products  131 us (9%)
  loops' own time  67 us (5%)
    ppermute x20, waiting for transfers between devices, passed_along(): lax.ppermute(value, axis, [(source, source + steps) for source in range(f...  186 us
    psum x1, blocking collectives, on_device(): lax.psum((weight_grads[0], jnp.stack([weight_grads[1], weight_grads[2]]),...  155 us
    another operation x103, other arithmetic  124 us
    dot_general x72, matrix products, contract(): return jnp.einsum(form, left, right, preferred_element_type=jnp.float32)  87.9 us
    ppermute x20, starting transfers between devices, passed_along(): lax.ppermute(value, axis, [(source, source + steps) for source in range(f...  61.1 us
    all_to_all x1, waiting for transfers between devices, on_device(): lax.all_to_all(place(loaded[0], mine), ('dp', 'ctx'), split_axis=0, conca...  44.6 us
    another operation x1, loops' own time, on_device(): lax.map(backward_batch, jnp.arange(batches, dtype=jnp.int32))  34.4 us
    another operation x1, loops' own time, on_device(): lax.map(summary, jnp.arange(batches, dtype=jnp.int32))  32.4 us
  transfers between devices with their start and end apart: 35, of which 22 were waited for; matrix products, arithmetic and copies ran while one was open for 10% of the time, Pallas kernels for 0%

commit v1 on v0

v1 whole, which is shorter than its diff:
```python
import functools

import jax
import jax.numpy as jnp
from jax import lax
from jax.experimental import pallas as pl
from jax.experimental.pallas import tpu as pltpu
from jax.sharding import PartitionSpec as P

HEADS = 128
HEAD_DIM = 64
GROUPS = 8
STATE = 128
KERNEL = 4
STRETCH = 256
BLK = 2
LANES = 128
OWNERS = 32
WAYS = 4
LBLOCKS = 64
DEPTH = 4
ROWS = 512
XCOLS = 2048
BCOLS = 256
COLS = XCOLS + 2 * BCOLS + LANES
PAIRS = 16
GROUP_PAIRS = 8
EXTRA = 16
NEG = -1e30

F32 = jnp.float32
BF16 = jnp.bfloat16
ROUTE = ("head", "dp", "ctx")


def dot(left, right):
    return lax.dot_general(left, right, (((1,), (0,)), ((), ())), preferred_element_type=F32)


def dot_nt(left, right):
    return lax.dot_general(left, right, (((1,), (1,)), ((), ())), preferred_element_type=F32)


def iota(shape, dim):
    return lax.broadcasted_iota(jnp.int32, shape, dim)


def one_hot(condition):
    return jnp.where(condition, 1.0, 0.0).astype(BF16)


def eye(size):
    return one_hot(iota((size, size), 0) == iota((size, size), 1))


def send_kernel(d_ref, x_ref, b_ref, c_ref, dt_ref, out_ref):
    way = pl.program_id(0)
    rows = x_ref.shape[0]
    spread = one_hot(iota((OWNERS * DEPTH * BLK, rows), 0) == d_ref[...])
    out_ref[0, :, :XCOLS] = dot(spread, x_ref[...]).astype(BF16)
    out_ref[0, :, XCOLS : XCOLS + BCOLS] = dot(spread, b_ref[...]).astype(BF16)
    out_ref[0, :, XCOLS + BCOLS : XCOLS + 2 * BCOLS] = dot(spread, c_ref[...]).astype(BF16)
    width = HEADS // WAYS
    lane = iota((LANES, LANES), 1)
    pick = one_hot((iota((LANES, LANES), 0) == way * width + lane) & (lane < width))
    dt_part = dot(dt_ref[...], pick).astype(BF16)
    out_ref[0, :, XCOLS + 2 * BCOLS :] = dot(spread, dt_part).astype(BF16)


def send_rows(d_row, x_rows, b_rows, c_rows, dt_rows):
    rows = x_rows.shape[0]
    slots = OWNERS * DEPTH * BLK
    return pl.pallas_call(
        send_kernel,
        grid=(WAYS,),
        in_specs=[
            pl.BlockSpec((1, rows), lambda h: (0, 0)),
            pl.BlockSpec((rows, XCOLS), lambda h: (0, h)),
            pl.BlockSpec((rows, BCOLS), lambda h: (0, h)),
            pl.BlockSpec((rows, BCOLS), lambda h: (0, h)),
            pl.BlockSpec((rows, HEADS), lambda h: (0, 0)),
        ],
        out_specs=pl.BlockSpec((1, slots, COLS), lambda h: (h, 0, 0)),
        out_shape=jax.ShapeDtypeStruct((WAYS, slots, COLS), BF16),
        name="send_rows",
    )(d_row, x_rows, b_rows, c_rows, dt_rows)


def pack_kernel(q_ref, in_ref, out_ref):
    rows = out_ref.shape[0]
    slots = in_ref.shape[1]
    pick = one_hot(iota((rows, slots), 1) == q_ref[0])
    out_ref[...] = dot(pick, in_ref[0]).astype(BF16)


def pack_rows(q_col, landed):
    slots = landed.shape[1]
    rows = ROWS // WAYS
    return pl.pallas_call(
        pack_kernel,
        grid=(WAYS,),
        in_specs=[
            pl.BlockSpec((1, rows, 1), lambda j: (j, 0, 0)),
            pl.BlockSpec((1, slots, COLS), lambda j: (j, 0, 0)),
        ],
        out_specs=pl.BlockSpec((rows, COLS), lambda j: (j, 0)),
        out_shape=jax.ShapeDtypeStruct((ROWS, COLS), BF16),
        name="pack_rows",
    )(q_col, landed)


def unpack_kernel(q_ref, x_ref, b_ref, c_ref, dt_ref, tx_ref, tb_ref, tc_ref, back_ref, out_ref):
    j = pl.program_id(0)
    rows = x_ref.shape[0]
    slots = out_ref.shape[1]
    spread = one_hot(iota((slots, rows), 0) == q_ref[0])
    last = j == WAYS - 1

    def one(ref, tail_ref, low, high):
        whole = ref[...].astype(F32)
        tail = tail_ref[...] + back_ref[:, low:high]
        fixed = jnp.concatenate([whole[: rows - 8], jnp.where(last, tail, whole[rows - 8 :])])
        out_ref[0, :, low:high] = dot(spread, fixed.astype(BF16)).astype(BF16)

    one(x_ref, tx_ref, 0, XCOLS)
    one(b_ref, tb_ref, XCOLS, XCOLS + BCOLS)
    one(c_ref, tc_ref, XCOLS + BCOLS, XCOLS + 2 * BCOLS)
    out_ref[0, :, XCOLS + 2 * BCOLS :] = dot(spread, dt_ref[...]).astype(BF16)


def unpack_rows(q_row, dx, db, dc, ddt, tx, tb, tc, back):
    slots = OWNERS * DEPTH * BLK
    rows = ROWS // WAYS
    full = lambda j: (0, 0)
    return pl.pallas_call(
        unpack_kernel,
        grid=(WAYS,),
        in_specs=[
            pl.BlockSpec((1, 1, rows), lambda j: (j, 0, 0)),
            pl.BlockSpec((rows, XCOLS), lambda j: (j, 0)),
            pl.BlockSpec((rows, BCOLS), lambda j: (j, 0)),
            pl.BlockSpec((rows, BCOLS), lambda j: (j, 0)),
            pl.BlockSpec((rows, LANES), lambda j: (j, 0)),
            pl.BlockSpec((8, XCOLS), full),
            pl.BlockSpec((8, BCOLS), full),
            pl.BlockSpec((8, BCOLS), full),
            pl.BlockSpec((8, XCOLS + 2 * BCOLS), full),
        ],
        out_specs=pl.BlockSpec((1, slots, COLS), lambda j: (j, 0, 0)),
        out_shape=jax.ShapeDtypeStruct((WAYS, slots, COLS), BF16),
        name="unpack_rows",
    )(q_row, dx, db, dc, ddt, tx, tb, tc, back)


def home_kernel(d_ref, in_ref, x_ref, b_ref, c_ref, dt_ref, acc_ref):
    way = pl.program_id(0)
    rows = x_ref.shape[0]
    slots = in_ref.shape[1]
    pick = one_hot(iota((rows, slots), 1) == d_ref[...])
    x_ref[...] = dot(pick, in_ref[0, :, :XCOLS]).astype(BF16)
    b_ref[...] = dot(pick, in_ref[0, :, XCOLS : XCOLS + BCOLS]).astype(BF16)
    c_ref[...] = dot(pick, in_ref[0, :, XCOLS + BCOLS : XCOLS + 2 * BCOLS]).astype(BF16)
    width = HEADS // WAYS
    lane = iota((LANES, LANES), 0)
    put = one_hot((iota((LANES, LANES), 1) == way * width + lane) & (lane < width))
    dt_part = dot(pick, in_ref[0, :, XCOLS + 2 * BCOLS :]).astype(BF16)

    @pl.when(way == 0)
    def _():
        acc_ref[...] = jnp.zeros_like(acc_ref)

    acc_ref[...] += dot(dt_part, put)
    dt_ref[...] = acc_ref[...].astype(BF16)


def home_rows(d_col, landed):
    slots = landed.shape[1]
    rows = d_col.shape[0]
    return pl.pallas_call(
        home_kernel,
        grid=(WAYS,),
        in_specs=[
            pl.BlockSpec((rows, 1), lambda h: (0, 0)),
            pl.BlockSpec((1, slots, COLS), lambda h: (h, 0, 0)),
        ],
        out_specs=[
            pl.BlockSpec((rows, XCOLS), lambda h: (0, h)),
            pl.BlockSpec((rows, BCOLS), lambda h: (0, h)),
            pl.BlockSpec((rows, BCOLS), lambda h: (0, h)),
            pl.BlockSpec((rows, HEADS), lambda h: (0, 0)),
        ],
        out_shape=[
            jax.ShapeDtypeStruct((rows, WAYS * XCOLS), BF16),
            jax.ShapeDtypeStruct((rows, WAYS * BCOLS), BF16),
            jax.ShapeDtypeStruct((rows, WAYS * BCOLS), BF16),
            jax.ShapeDtypeStruct((rows, HEADS), BF16),
        ],
        scratch_shapes=[pltpu.VMEM((rows, HEADS), F32)],
        name="home_rows",
    )(d_col, landed)


def fill_pad(pad_ref, rows_ref, halo_ref):
    pad_ref[0:8, :] = halo_ref[...].astype(F32)
    pad_ref[8 : 8 + ROWS, :] = rows_ref[...].astype(F32)


def conv_sum(pad_ref, taps, bias, keep_ref):
    total = bias + taps[0:1] * pad_ref[5 : 5 + ROWS, :] * keep_ref[0]
    total = total + taps[1:2] * pad_ref[6 : 6 + ROWS, :] * keep_ref[1]
    total = total + taps[2:3] * pad_ref[7 : 7 + ROWS, :] * keep_ref[2]
    return total + taps[3:4] * pad_ref[8 : 8 + ROWS, :]


def conv_value(pad_ref, rows_ref, halo_ref, taps, bias, keep_ref):
    fill_pad(pad_ref, rows_ref, halo_ref)
    total = conv_sum(pad_ref, taps, bias, keep_ref)
    return (total * jax.nn.sigmoid(total)).astype(BF16)


def conv_back(pad_ref, dpad_ref, rows_ref, halo_ref, taps, bias, keep_ref, keeps_ref, grad):
    fill_pad(pad_ref, rows_ref, halo_ref)
    total = conv_sum(pad_ref, taps, bias, keep_ref)
    sig = jax.nn.sigmoid(total)
    dpre = grad * (sig * (1.0 + total * (1.0 - sig)))
    dpad_ref[8 : 8 + ROWS, :] = dpre
    sums = []
    for k in range(KERNEL):
        value = dpre * pad_ref[5 + k : 5 + k + ROWS, :]
        if k < KERNEL - 1:
            value = value * keep_ref[k]
        sums.append(jnp.sum(value, axis=0, keepdims=True))
    sums.append(jnp.sum(dpre, axis=0, keepdims=True))
    sums.append(jnp.zeros((3, LANES), F32))
    span = ROWS + 8
    moved = taps[3:4] * dpad_ref[0:span, :]
    for k in range(KERNEL - 1):
        moved = moved + taps[k : k + 1] * (keeps_ref[k] * dpad_ref[3 - k : 3 - k + span, :])
    return moved, jnp.concatenate(sums)


def pair_rows(first, second, count=HEAD_DIM):
    width = first.shape[1]
    return jnp.concatenate(
        [jnp.broadcast_to(first, (count, width)), jnp.broadcast_to(second, (count, width))]
    )


def pair_scale(first, second, shape):
    return jnp.where(iota(shape, 0) < HEAD_DIM, first, second)


def first_kernel(
    gs_ref,
    rows_ref,
    x_ref,
    b_ref,
    c_ref,
    hx_ref,
    hb_ref,
    hc_ref,
    xt_ref,
    xb_ref,
    bt_ref,
    bb_ref,
    ct_ref,
    cb_ref,
    keep_ref,
    og_ref,
    ep_ref,
    xT_ref,
    gT_ref,
    bn_ref,
    cn_ref,
    e0_ref,
    t1_ref,
    pad_ref,
):
    i = pl.program_id(0)

    @pl.when(i % GROUP_PAIRS == 0)
    def _():
        bn_ref[...] = conv_value(pad_ref, b_ref, hb_ref, bt_ref[0], bb_ref[0], keep_ref)
        cn_ref[...] = conv_value(pad_ref, c_ref, hc_ref, ct_ref[0], cb_ref[0], keep_ref)

    unit = eye(LANES)
    xc = conv_value(pad_ref, x_ref, hx_ref, xt_ref[...], xb_ref[...], keep_ref)
    x_all = dot_nt(unit, xc)
    g_all = dot_nt(unit, og_ref[...])
    xT_ref[...] = x_all.astype(BF16)
    gT_ref[...] = g_all.astype(BF16)
    rows = rows_ref[0]
    states = []
    touched = []
    for k in range(2):
        span = slice(k * STRETCH, (k + 1) * STRETCH)
        coef = pair_rows(rows[0:1, span] * rows[4:5, span], rows[1:2, span] * rows[5:6, span])
        gain = pair_rows(rows[6:7, span], rows[7:8, span])
        states.append(dot((coef * x_all[:, span]).astype(BF16), bn_ref[span, :]))
        touched.append(dot((gain * g_all[:, span]).astype(BF16), cn_ref[span, :]))
    shape = (LANES, STATE)
    ga0, ga1 = gs_ref[4 * i], gs_ref[4 * i + 1]
    gb0, gb1 = gs_ref[4 * i + 2], gs_ref[4 * i + 3]
    ep_ref[0, 0:LANES, :] = (pair_scale(ga1, gb1, shape) * states[0] + states[1]).astype(BF16)
    ep_ref[0, LANES : 2 * LANES, :] = (
        touched[0] + pair_scale(ga0, gb0, shape) * touched[1]
    ).astype(BF16)
    lane = iota((EXTRA, LANES), 1)
    whole = jnp.where(lane < HEAD_DIM, ga0 * ga1, gb0 * gb1)
    high = whole.astype(BF16).astype(F32)
    low = whole - high
    ep_ref[0, 2 * LANES :, :] = jnp.where(iota((EXTRA, LANES), 0) < 8, high, low).astype(BF16)
    e0_ref[...] = states[0]
    t1_ref[...] = touched[1]


def conv_specs():
    group = lambda i: i // GROUP_PAIRS
    base_b = XCOLS // LANES
    base_c = base_b + BCOLS // LANES
    return [
        pl.BlockSpec((ROWS, LANES), lambda i: (0, i)),
        pl.BlockSpec((ROWS, LANES), lambda i: (0, base_b + group(i))),
        pl.BlockSpec((ROWS, LANES), lambda i: (0, base_c + group(i))),
        pl.BlockSpec((8, LANES), lambda i: (0, i)),
        pl.BlockSpec((8, LANES), lambda i: (0, base_b + group(i))),
        pl.BlockSpec((8, LANES), lambda i: (0, base_c + group(i))),
        pl.BlockSpec((KERNEL, LANES), lambda i: (0, i)),
        pl.BlockSpec((1, LANES), lambda i: (0, i)),
        pl.BlockSpec((1, KERNEL, LANES), lambda i: (0, 0, group(i))),
        pl.BlockSpec((1, 1, LANES), lambda i: (0, 0, group(i))),
        pl.BlockSpec((1, KERNEL, LANES), lambda i: (1, 0, group(i))),
        pl.BlockSpec((1, 1, LANES), lambda i: (1, 0, group(i))),
        pl.BlockSpec((KERNEL - 1, ROWS, LANES), lambda i: (0, 0, 0)),
    ]


def first_pass(gs, rows, conv_args, out_grad):
    wide = lambda i: (i, 0)
    group = lambda i: (0, i // GROUP_PAIRS)
    return pl.pallas_call(
        first_kernel,
        grid=(PAIRS,),
        in_specs=[
            pl.BlockSpec(memory_space=pltpu.SMEM),
            pl.BlockSpec((1, 8, ROWS), lambda i: (i, 0, 0)),
        ]
        + conv_specs()
        + [pl.BlockSpec((ROWS, LANES), lambda i: (0, i))],
        out_specs=[
            pl.BlockSpec((1, 2 * LANES + EXTRA, STATE), lambda i: (i, 0, 0)),
            pl.BlockSpec((LANES, ROWS), wide),
            pl.BlockSpec((LANES, ROWS), wide),
            pl.BlockSpec((ROWS, LANES), group),
            pl.BlockSpec((ROWS, LANES), group),
            pl.BlockSpec((LANES, STATE), wide),
            pl.BlockSpec((LANES, STATE), wide),
        ],
        out_shape=[
            jax.ShapeDtypeStruct((PAIRS, 2 * LANES + EXTRA, STATE), BF16),
            jax.ShapeDtypeStruct((XCOLS, ROWS), BF16),
            jax.ShapeDtypeStruct((XCOLS, ROWS), BF16),
            jax.ShapeDtypeStruct((ROWS, BCOLS), BF16),
            jax.ShapeDtypeStruct((ROWS, BCOLS), BF16),
            jax.ShapeDtypeStruct((XCOLS, STATE), F32),
            jax.ShapeDtypeStruct((XCOLS, STATE), F32),
        ],
        scratch_shapes=[pltpu.VMEM((ROWS + 16, LANES), F32)],
        name="first_pass",
    )(gs, rows, *conv_args, out_grad)


def scan_kernel(in_ref, out_ref):
    count = in_ref.shape[0]
    shape = (LANES, STATE)
    gains = []
    for at in range(count):
        extra = in_ref[at, 0, 2 * LANES :, :].astype(F32)
        gain = extra[0:1] + extra[8:9]
        gains.append(pair_scale(gain[:, 0:1], gain[:, HEAD_DIM : HEAD_DIM + 1], shape))
    state = jnp.zeros(shape, F32)
    for at in range(count):
        out_ref[at, 0, 0:LANES, :] = state.astype(BF16)
        state = gains[at] * state + in_ref[at, 0, 0:LANES, :].astype(F32)
    state = jnp.zeros(shape, F32)
    for at in reversed(range(count)):
        out_ref[at, 0, LANES : 2 * LANES, :] = state.astype(BF16)
        state = in_ref[at, 0, LANES : 2 * LANES, :].astype(F32) + gains[at] * state


def scan_states(landed):
    count, pairs = landed.shape[:2]
    return pl.pallas_call(
        scan_kernel,
        grid=(pairs,),
        in_specs=[pl.BlockSpec((count, 1, 2 * LANES + EXTRA, STATE), lambda i: (0, i, 0, 0))],
        out_specs=pl.BlockSpec((count, 1, 2 * LANES, STATE), lambda i: (0, i, 0, 0)),
        out_shape=jax.ShapeDtypeStruct((count, pairs, 2 * LANES, STATE), BF16),
        name="scan_states",
    )(landed)


def main_kernel(
    gs_ref,
    skip_ref,
    rows_ref,
    x_ref,
    b_ref,
    c_ref,
    hx_ref,
    hb_ref,
    hc_ref,
    xt_ref,
    xb_ref,
    bt_ref,
    bb_ref,
    ct_ref,
    cb_ref,
    keep_ref,
    keeps_ref,
    og_ref,
    xT_ref,
    gT_ref,
    bn_ref,
    cn_ref,
    ent_ref,
    e0_ref,
    t1_ref,
    labr_ref,
    labc_ref,
    y_ref,
    dx_ref,
    db_ref,
    dc_ref,
    tx_ref,
    tb_ref,
    tc_ref,
    px_ref,
    pb_ref,
    pc_ref,
    rout_ref,
    sx_ref,
    sb_ref,
    sc_ref,
    mask_ref,
    score_ref,
    dscore_ref,
    bT_ref,
    cT_ref,
    dbT_ref,
    dcT_ref,
    pad_ref,
    dpad_ref,
    dxn_ref,
):
    i = pl.program_id(0)
    unit = eye(LANES)
    wide_unit = eye(STRETCH)
    spans = [slice(k * STRETCH, (k + 1) * STRETCH) for k in range(2)]

    @pl.when(i == 0)
    def _():
        dpad_ref[...] = jnp.zeros_like(dpad_ref)
        for k in range(2):
            for t in range(2):
                shape = (STRETCH, LANES)
                left = k * STRETCH + t * LANES
                same = labc_ref[spans[k], :] == labr_ref[0:1, left : left + LANES]
                lower = iota(shape, 0) >= iota(shape, 1) + t * LANES
                mask_ref[k, :, t * LANES : (t + 1) * LANES] = jnp.where(same & lower, 0.0, NEG)

    @pl.when(i % GROUP_PAIRS == 0)
    def _():
        bT_ref[...] = dot_nt(unit, bn_ref[...]).astype(BF16)
        cT_ref[...] = dot_nt(unit, cn_ref[...]).astype(BF16)
        dbT_ref[...] = jnp.zeros_like(dbT_ref)
        dcT_ref[...] = jnp.zeros_like(dcT_ref)
        dscore_ref[...] = jnp.zeros_like(dscore_ref)
        for k in range(2):
            score_ref[k] = dot_nt(cn_ref[spans[k], :], bn_ref[spans[k], :])

    rows = rows_ref[0]
    columns = jnp.transpose(rows)
    shape = (LANES, STATE)
    gains = [
        (gs_ref[4 * i + k], gs_ref[4 * i + 2 + k]) for k in range(2)
    ]
    skip = pair_scale(skip_ref[2 * i], skip_ref[2 * i + 1], (LANES, STRETCH))
    enter0 = ent_ref[0, 0:LANES, :].astype(F32)
    leave1 = ent_ref[0, LANES : 2 * LANES, :].astype(F32)
    enter1 = pair_scale(*gains[0], shape) * enter0 + e0_ref[...]
    leave0 = t1_ref[...] + pair_scale(*gains[1], shape) * leave1
    enters = (enter0, enter1)
    leaves = (leave0, leave1)
    for k in range(2):
        span = spans[k]
        x = xT_ref[:, span].astype(F32)
        g_low = gT_ref[:, span]
        g = g_low.astype(F32)
        og = og_ref[span, :]
        step = pair_rows(rows[0:1, span], rows[1:2, span])
        ends = (rows[4:5, span], rows[5:6, span])
        coefs = (rows[0:1, span] * ends[0], rows[1:2, span] * ends[1])
        coef = pair_rows(*coefs)
        gain = pair_rows(rows[6:7, span], rows[7:8, span])
        xs = (step * x).astype(BF16)
        weighted = (coef * x).astype(BF16)
        nothing = jnp.zeros((HEAD_DIM, STRETCH), BF16)
        inner = []
        dxs = []
        for h in range(2):
            part = slice(h * HEAD_DIM, (h + 1) * HEAD_DIM)
            gap = columns[span, 2 + h : 3 + h] - rows[2 + h : 3 + h, span]
            decay = jnp.exp(gap + mask_ref[k])
            mix = (score_ref[k] * decay).astype(BF16)
            own = (xs[part], nothing) if h == 0 else (nothing, xs[part])
            dmix = dot(og, jnp.concatenate(own))
            dscore_ref[k] += dmix * decay
            inner.append(dot_nt(xs[part], mix))
            dxs.append(dot(g_low[part], mix))
        inner = jnp.concatenate(inner)
        dxs = jnp.concatenate(dxs)
        enter = enters[k].astype(BF16)
        leave = leaves[k].astype(BF16)
        carried = gain * dot_nt(enter, cn_ref[span, :])
        y = inner + carried + skip * x
        y_ref[span, :] = dot_nt(wide_unit, y.astype(BF16)).astype(BF16)
        enter_t = dot_nt(unit, enter).astype(BF16)
        leave_t = dot_nt(unit, leave).astype(BF16)
        dcT_ref[:, span] += dot(enter_t, (gain * g).astype(BF16))
        dbT_ref[:, span] += dot(leave_t, weighted)
        dweighted = dot_nt(leave, bn_ref[span, :])
        dx = step * dxs + coef * dweighted + skip * g
        dxn_ref[span, :] = dot_nt(wide_unit, dx.astype(BF16))
        moved = dweighted * x
        direct = dxs * x
        cums = g * (inner + carried) - xs.astype(F32) * dxs
        skipped = g * x
        turned = leaves[k] * enters[k]
        last = iota((1, STRETCH), 1) == STRETCH - 1
        for h in range(2):
            part = slice(h * HEAD_DIM, (h + 1) * HEAD_DIM)
            pulled = jnp.sum(moved[part], axis=0, keepdims=True)
            ended = coefs[h] * pulled
            total = jnp.sum(ended, axis=1, keepdims=True)
            bend = jnp.sum(
                jnp.sum(turned[part], axis=0, keepdims=True), axis=1, keepdims=True
            )
            dcum = jnp.sum(cums[part], axis=0, keepdims=True) - ended
            dcum = dcum + jnp.where(last, total + gains[k][h] * bend, 0.0)
            rout_ref[0, h : h + 1, span] = (
                jnp.sum(direct[part], axis=0, keepdims=True) + ends[h] * pulled
            )
            rout_ref[0, 2 + h : 3 + h, span] = dcum
            rout_ref[0, 4 + h : 5 + h, span] = jnp.sum(skipped[part], axis=0, keepdims=True)
    rout_ref[0, 6:8, :] = jnp.zeros((2, ROWS), F32)

    moved, sums = conv_back(
        pad_ref, dpad_ref, x_ref, hx_ref, xt_ref[...], xb_ref[...], keep_ref, keeps_ref, dxn_ref[...]
    )
    sx_ref[...] = moved[0:8]
    tx_ref[...] = moved[ROWS:]
    dx_ref[...] = moved[8:].astype(BF16)
    px_ref[0] = sums

    @pl.when(i % GROUP_PAIRS == GROUP_PAIRS - 1)
    def _():
        for k in range(2):
            span = spans[k]
            dscore = dscore_ref[k].astype(BF16)
            dcT = dcT_ref[:, span] + dot_nt(bT_ref[:, span], dscore)
            dbT = dbT_ref[:, span] + dot(cT_ref[:, span], dscore)
            dcT_ref[:, span] = dcT
            dbT_ref[:, span] = dbT
        sides = (
            (dbT_ref, b_ref, hb_ref, bt_ref, bb_ref, db_ref, sb_ref, tb_ref, pb_ref),
            (dcT_ref, c_ref, hc_ref, ct_ref, cb_ref, dc_ref, sc_ref, tc_ref, pc_ref),
        )
        for grad_ref, in_ref, halo_ref, tap_ref, bias_ref, out_ref, s_ref, t_ref, p_ref in sides:
            for span in spans:
                dxn_ref[span, :] = dot_nt(wide_unit, grad_ref[:, span].astype(BF16))
            moved, sums = conv_back(
                pad_ref,
                dpad_ref,
                in_ref,
                halo_ref,
                tap_ref[0],
                bias_ref[0],
                keep_ref,
                keeps_ref,
                dxn_ref[...],
            )
            s_ref[...] = moved[0:8]
            t_ref[...] = moved[ROWS:]
            out_ref[...] = moved[8:].astype(BF16)
            p_ref[0] = sums


def main_pass(gs, skip, rows, conv_args, keeps, out_grad, xT, gT, bn, cn, ent, e0, t1, labr, labc):
    wide = lambda i: (i, 0)
    col = lambda i: (0, i)
    group = lambda i: (0, i // GROUP_PAIRS)
    triple = lambda i: (i, 0, 0)
    square = (2, STRETCH, STRETCH)
    return pl.pallas_call(
        main_kernel,
        grid=(PAIRS,),
        in_specs=[
            pl.BlockSpec(memory_space=pltpu.SMEM),
            pl.BlockSpec(memory_space=pltpu.SMEM),
            pl.BlockSpec((1, 8, ROWS), triple),
        ]
        + conv_specs()
        + [
            pl.BlockSpec((KERNEL - 1, ROWS + 8, LANES), lambda i: (0, 0, 0)),
            pl.BlockSpec((ROWS, LANES), col),
            pl.BlockSpec((LANES, ROWS), wide),
            pl.BlockSpec((LANES, ROWS), wide),
            pl.BlockSpec((ROWS, LANES), group),
            pl.BlockSpec((ROWS, LANES), group),
            pl.BlockSpec((1, 2 * LANES, STATE), triple),
            pl.BlockSpec((LANES, STATE), wide),
            pl.BlockSpec((LANES, STATE), wide),
            pl.BlockSpec((8, ROWS), lambda i: (0, 0)),
            pl.BlockSpec((ROWS, LANES), lambda i: (0, 0)),
        ],
        out_specs=[
            pl.BlockSpec((ROWS, LANES), col),
            pl.BlockSpec((ROWS, LANES), col),
            pl.BlockSpec((ROWS, LANES), group),
            pl.BlockSpec((ROWS, LANES), group),
            pl.BlockSpec((8, LANES), col),
            pl.BlockSpec((8, LANES), group),
            pl.BlockSpec((8, LANES), group),
            pl.BlockSpec((1, 8, LANES), triple),
            pl.BlockSpec((1, 8, LANES), lambda i: (i // GROUP_PAIRS, 0, 0)),
            pl.BlockSpec((1, 8, LANES), lambda i: (i // GROUP_PAIRS, 0, 0)),
            pl.BlockSpec((1, 8, ROWS), triple),
            pl.BlockSpec((8, LANES), col),
            pl.BlockSpec((8, LANES), group),
            pl.BlockSpec((8, LANES), group),
        ],
        out_shape=[
            jax.ShapeDtypeStruct((ROWS, XCOLS), BF16),
            jax.ShapeDtypeStruct((ROWS, XCOLS), BF16),
            jax.ShapeDtypeStruct((ROWS, BCOLS), BF16),
            jax.ShapeDtypeStruct((ROWS, BCOLS), BF16),
            jax.ShapeDtypeStruct((8, XCOLS), F32),
            jax.ShapeDtypeStruct((8, BCOLS), F32),
            jax.ShapeDtypeStruct((8, BCOLS), F32),
            jax.ShapeDtypeStruct((PAIRS, 8, LANES), F32),
            jax.ShapeDtypeStruct((2, 8, LANES), F32),
            jax.ShapeDtypeStruct((2, 8, LANES), F32),
            jax.ShapeDtypeStruct((PAIRS, 8, ROWS), F32),
            jax.ShapeDtypeStruct((8, XCOLS), F32),
            jax.ShapeDtypeStruct((8, BCOLS), F32),
            jax.ShapeDtypeStruct((8, BCOLS), F32),
        ],
        scratch_shapes=[
            pltpu.VMEM(square, F32),
            pltpu.VMEM(square, F32),
            pltpu.VMEM(square, F32),
            pltpu.VMEM((LANES, ROWS), BF16),
            pltpu.VMEM((LANES, ROWS), BF16),
            pltpu.VMEM((LANES, ROWS), F32),
            pltpu.VMEM((LANES, ROWS), F32),
            pltpu.VMEM((ROWS + 16, LANES), F32),
            pltpu.VMEM((ROWS + 16, LANES), F32),
            pltpu.VMEM((ROWS, LANES), F32),
        ],
        name="main_pass",
    )(gs, skip, rows, *conv_args, keeps, out_grad, xT, gT, bn, cn, ent, e0, t1, labr, labc)


def segment_of(ends, positions):
    return jnp.sum((positions[:, None] >= ends[None, :]).astype(jnp.int32), axis=1)


def exact(form, left, right):
    return jnp.einsum(form, left, right, precision=lax.Precision.HIGHEST)


def passed_along(value, axis, steps):
    count = lax.axis_size(axis)
    first, last = (max(0, -steps), min(count, count - steps))
    return lax.ppermute(value, axis, [(source, source + steps) for source in range(first, last)])


def on_device(
    x_rows,
    b_rows,
    c_rows,
    dt_rows,
    length_plan,
    trace_lengths,
    x_taps,
    bc_taps,
    x_bias,
    bc_bias,
    dt_bias,
    decay_rate,
    skip_gain,
    out_grad,
):
    contexts = lax.axis_size("ctx")
    owner = lax.axis_index("dp") * contexts + lax.axis_index("ctx")
    head_at = lax.axis_index("head")
    owned = LBLOCKS * WAYS
    plan = length_plan.reshape(OWNERS, WAYS, LBLOCKS)
    column = lax.dynamic_index_in_dim(plan, head_at, 1, keepdims=False)
    base = (owner * WAYS + head_at) * LBLOCKS
    blocks = jnp.arange(LBLOCKS, dtype=jnp.int32)
    hits = column.reshape(-1)[:, None] == base + blocks[None, :]
    seats = (jnp.arange(OWNERS * LBLOCKS, dtype=jnp.int32) // LBLOCKS)[:, None]
    target = jnp.sum(jnp.where(hits, seats, 0), axis=0)
    earlier = blocks[None, :] < blocks[:, None]
    rank = jnp.sum(((target[None, :] == target[:, None]) & earlier).astype(jnp.int32), axis=1)
    pairs = jnp.arange(BLK, dtype=jnp.int32)
    goes = (((target * DEPTH + rank) * BLK)[:, None] + pairs[None, :]).reshape(-1)
    mine = lax.dynamic_slice_in_dim(length_plan, owner * owned, owned).reshape(WAYS, LBLOCKS)
    source = mine // owned
    same = source[:, :, None] == source[:, None, :]
    lower = mine[:, None, :] < mine[:, :, None]
    place = jnp.sum((same & lower).astype(jnp.int32), axis=2)
    comes = ((source * DEPTH + place) * BLK)[:, :, None] + pairs
    comes = comes.reshape(WAYS, LBLOCKS * BLK)

    spread = send_rows(goes[None, :], x_rows, b_rows, c_rows, dt_rows)
    slots = spread.shape[1]
    devices = WAYS * OWNERS

    def exchange(value):
        value = value.reshape(devices, DEPTH * BLK, COLS)
        value = lax.all_to_all(value, ROUTE, split_axis=0, concat_axis=0, tiled=True)
        return value.reshape(WAYS, slots, COLS)

    packed = pack_rows(comes[:, :, None], exchange(spread))
    halo = passed_along(packed[-8:], "ctx", 1)

    start = lax.axis_index("ctx") * ROWS
    ends = jnp.cumsum(trace_lengths[0])
    positions = start - 8 + jnp.arange(ROWS + 16, dtype=jnp.int32)
    wide_labels = jnp.where(positions >= 0, segment_of(ends, positions), -1)
    labels = wide_labels[8 : 8 + ROWS]
    keep = jnp.stack([wide_labels[5 + k : 5 + k + ROWS] == labels for k in range(KERNEL - 1)])
    keep = jnp.broadcast_to(keep.astype(F32)[:, :, None], (KERNEL - 1, ROWS, LANES))
    front = wide_labels[: ROWS + 8]
    keeps = jnp.stack(
        [
            (wide_labels[3 - k : 3 - k + ROWS + 8] == front) & (front >= 0)
            for k in range(KERNEL - 1)
        ]
    )
    keeps = jnp.broadcast_to(keeps.astype(F32)[:, :, None], (KERNEL - 1, ROWS + 8, LANES))
    grid = labels.reshape(2, STRETCH)
    before = jnp.stack([wide_labels[7], labels[STRETCH - 1]])
    last_keep = (grid == grid[:, -1:]).astype(F32)
    first_keep = (grid == before[:, None]).astype(F32)
    carry_keep = (grid[:, -1] == before).astype(F32)
    labr = jnp.broadcast_to(labels[None, :], (8, ROWS))
    labc = jnp.broadcast_to(labels[:, None], (ROWS, LANES))

    heads_dev = dt_bias.shape[0]
    dt_in = packed[:, XCOLS + 2 * BCOLS : XCOLS + 2 * BCOLS + heads_dev].astype(F32).T
    logits = dt_in + dt_bias[:, None]
    step = jax.nn.softplus(logits)
    tri = jnp.tril(jnp.ones((STRETCH, STRETCH), F32))
    folded = step.reshape(heads_dev, 2, STRETCH)
    cum = exact("hks,rs->hkr", -decay_rate[:, None, None] * folded, tri)
    to_end = jnp.exp(cum[:, :, -1:] - cum) * last_keep[None]
    gain = jnp.exp(cum) * first_keep[None]
    gs = (jnp.exp(cum[:, :, -1]) * carry_keep[None]).reshape(-1)
    rows = jnp.stack([folded, cum, to_end, gain]).reshape(4, PAIRS, 2, ROWS)
    rows = jnp.swapaxes(rows, 0, 1).reshape(PAIRS, 8, ROWS)

    bias_bc = bc_bias[:, None, :]
    conv_args = (
        packed,
        packed,
        packed,
        halo,
        halo,
        halo,
        x_taps,
        x_bias[None, :],
        bc_taps,
        bias_bc,
        bc_taps,
        bias_bc,
        keep,
    )
    ep, xT, gT, bn, cn, e0, t1 = first_pass(gs, rows, conv_args, out_grad)

    per = PAIRS // contexts
    tall = 2 * LANES + EXTRA
    ep = lax.all_to_all(
        ep.reshape(contexts, per * tall, STATE), "ctx", split_axis=0, concat_axis=0, tiled=True
    )
    scanned = scan_states(ep.reshape(contexts, per, tall, STATE))
    scanned = lax.all_to_all(
        scanned.reshape(contexts, per * 2 * LANES, STATE),
        "ctx",
        split_axis=0,
        concat_axis=0,
        tiled=True,
    )
    ent = scanned.reshape(PAIRS, 2 * LANES, STATE)

    y, dx, db, dc, tx, tb, tc, px, pb, pc, rout, sx, sb, sc = main_pass(
        gs, skip_gain, rows, conv_args, keeps, out_grad, xT, gT, bn, cn, ent, e0, t1, labr, labc
    )
    back = passed_along(jnp.concatenate([sx, sb, sc], axis=1), "ctx", -1)

    parts = rout.reshape(PAIRS, 4, 2, 2, STRETCH)
    parts = jnp.swapaxes(parts, 0, 1).reshape(4, heads_dev, 2, STRETCH)
    after = exact("hks,sr->hkr", parts[1], tri)
    dstep = parts[0] - decay_rate[:, None, None] * after
    dlogit = dstep.reshape(heads_dev, ROWS) * jax.nn.sigmoid(logits)
    ddt = jnp.pad(dlogit.T.astype(BF16), ((0, 0), (0, LANES - heads_dev)))
    scalars = jnp.concatenate(
        [
            jnp.sum(dlogit, axis=1),
            -jnp.sum(after * folded, axis=(1, 2)),
            jnp.sum(parts[2], axis=(1, 2)),
            jnp.zeros((LANES - 3 * heads_dev,), F32),
        ]
    )

    stacked = jnp.concatenate(
        [
            px[:, :5].reshape(-1, LANES),
            pb[:, :5].reshape(-1, LANES),
            pc[:, :5].reshape(-1, LANES),
            scalars[None, :],
        ]
    )
    count = stacked.shape[0]
    chunk = 4
    stacked = jnp.pad(stacked, ((0, OWNERS * chunk - count), (0, 0)))

    returned = exchange(
        unpack_rows(comes[:, None, :], dx, db, dc, ddt, tx, tb, tc, back)
    )
    x_grad, b_grad, c_grad, dt_grad = home_rows(goes[:, None], returned)

    swap = functools.partial(
        lax.all_to_all, axis_name=("dp", "ctx"), split_axis=0, concat_axis=0, tiled=True
    )
    partial_sum = jnp.sum(swap(stacked.reshape(OWNERS, chunk, LANES)), axis=0)
    whole = swap(jnp.broadcast_to(partial_sum[None], (OWNERS, chunk, LANES)))
    whole = whole.reshape(OWNERS * chunk, LANES)
    at = PAIRS * 5
    sum_x = jnp.swapaxes(whole[:at].reshape(PAIRS, 5, LANES), 0, 1).reshape(5, XCOLS)
    sum_b = jnp.swapaxes(whole[at : at + 10].reshape(2, 5, LANES), 0, 1).reshape(5, BCOLS)
    sum_c = jnp.swapaxes(whole[at + 10 : at + 20].reshape(2, 5, LANES), 0, 1).reshape(5, BCOLS)
    tail = whole[at + 20]
    return (
        y,
        x_grad,
        b_grad,
        c_grad,
        dt_grad,
        sum_x[:4],
        jnp.stack([sum_b[:4], sum_c[:4]]),
        sum_x[4],
        jnp.stack([sum_b[4], sum_c[4]]),
        tail[:heads_dev],
        tail[heads_dev : 2 * heads_dev],
        tail[2 * heads_dev : 3 * heads_dev],
    )


def solution(mesh):
    rows = P(("dp", "ctx", "head"), None)
    return jax.shard_map(
        on_device,
        mesh=mesh,
        in_specs=(
            rows,
            rows,
            rows,
            rows,
            P(),
            P("dp", None),
            P(None, "head"),
            P(None, None, "head"),
            P("head"),
            P(None, "head"),
            P("head"),
            P("head"),
            P("head"),
            P(("dp", "ctx"), "head"),
        ),
        out_specs=(
            P(("dp", "ctx"), "head"),
            rows,
            rows,
            rows,
            rows,
            P(None, "head"),
            P(None, None, "head"),
            P("head"),
            P(None, "head"),
            P("head"),
            P("head"),
            P("head"),
        ),
        check_vma=False,
    )
```

time: 1460 us -> 312 us (0.21); the launches traced: 1440 us -> 310 us
  local copies, waits for them, and re-layouts: 331 us -> 20 us
  other arithmetic: 308 us -> 9.05 us
  blocking collectives: 176 us -> 19.7 us
  waiting for transfers between devices: 279 us -> 143 us
  matrix products: 131 us -> 0.76 us
  starting transfers between devices: 141 us -> 38.1 us
  Pallas kernels: 0 us -> 78.3 us
  loops' own time: 67 us -> 0 us
    ppermute x20 -> x2, waiting for transfers between devices: 186 us -> 0.01 us  [passed_along(): lax.ppermute(value, axis, [(source, source + steps) for source in range(f...]
    psum x1 -> x0, blocking collectives: 155 us -> none  [on_device(): lax.psum((weight_grads[0], jnp.stack([weight_grads[1], weight_grads[2]]),...]
    another operation x107 -> x3, other arithmetic: 124 us -> 1.37 us  [the longest x1 0.6 us: on_device(): jnp.stack([sum_b[:4], sum_c[:4]])]
    dot_general x96 -> x2, matrix products: 121 us -> 0.76 us  [exact(): return jnp.einsum(form, left, right, precision=lax.Precision.HIGHEST)]
    pallas_call x0 -> x7, Pallas kernels: none -> 78.3 us  [the longest x1 37.9 us: main_pass(): pl.pallas_call(main_kernel, grid=(PAIRS,), in_specs=[pl.BlockSpec(memory_...]
    gather x23 -> x0, local copies, waits for them, and re-layouts: 70.8 us -> none  [the longest x8 29.7 us: unplace(): return padded[source]]
    another operation x4 -> x0, loops' own time: 67 us -> none  [the longest x1 34.4 us: on_device(): lax.map(backward_batch, jnp.arange(batches, dtype=jnp.int32))]
    reduce_sum x61 -> x6, other arithmetic: 57.9 us -> 1.85 us  [the longest x1 1.02 us: on_device(): jnp.sum(dlogit, axis=1)]
  transfers between devices with their start and end apart: 35 -> 7, of which waited for: 22 -> 4; matrix products, arithmetic and copies ran while one was open for 10% -> 5% of each run, Pallas kernels for 0% -> 2%
where the time goes in v1:
time: 312 us; the launch traced here: 310 us
  waiting for transfers between devices  143 us (46%)
  Pallas kernels  78.3 us (25%)
  starting transfers between devices  38.1 us (12%)
  local copies, waits for them, and re-layouts  20 us (6%)
  blocking collectives  19.7 us (6%)
  other arithmetic  9.05 us (3%)
    all_to_all x2, waiting for transfers between devices, exchange(): lax.all_to_all(value, ROUTE, split_axis=0, concat_axis=0, tiled=True)  123 us
    pallas_call x1, Pallas kernels, main_pass(): pl.pallas_call(main_kernel, grid=(PAIRS,), in_specs=[pl.BlockSpec(memory_...  37.9 us
    all_to_all x2, starting transfers between devices, exchange(): lax.all_to_all(value, ROUTE, split_axis=0, concat_axis=0, tiled=True)  20.3 us
    all_to_all x1, blocking collectives, on_device(): lax.all_to_all(ep.reshape(contexts, per * tall, STATE), 'ctx', split_axis...  19.7 us
    pallas_call x1, Pallas kernels, first_pass(): pl.pallas_call(first_kernel, grid=(PAIRS,), in_specs=[pl.BlockSpec(memory...  15.8 us
    all_to_all x1, waiting for transfers between devices, on_device(): lax.all_to_all(scanned.reshape(contexts, per * 2 * LANES, STATE), 'ctx',...  14.8 us
  transfers between devices with their start and end apart: 7, of which 4 were waited for; matrix products, arithmetic and copies ran while one was open for 5% of the time, Pallas kernels for 2%

profile of v1, /device:TPU:1, one launch (start us, length us, event | category | flops | bytes accessed | tf_op | source)
XLA Modules:
  0.0 310.1 jit_solution(6962510345000710662)
XLA Ops:
  0.7 0.8 reshape.486
  2.8 5.8 %send_rows.1 = bf16[4,256,2688]{2,1,0:T(8,128)(2,1)} custom-call(s32[1,128]{1,0:T(1,128)} %add.181.d_ref, bf16[128,8192]{1,0:T(8,128)(2,1)} %x_ref.1, bf16[128,1024]{1,0:T(8,128)(2,1)} %b_ref.1, bf16[128,1024]{1,0:T(8,128)(2,1)} %c_ref.1, bf16[128,128]{1,0:T(8,128)(2,1)} %dt_ref.1), custom_call_target="tpu_custom_call" | custom-call | tf_op jit(solution)/shard_map/send_rows/pallas_call | solution.py:73
  8.6 11.9 %all-to-all-start = ((bf16[128,8,2688]{2,1,0:T(8,128)(2,1)}), bf16[128,8,2688]{2,1,0:T(8,128)(2,1)}, u32[]{:S(2)}, u32[]{:S(2)}) async-start(bf16[128,8,2688]{2,1,0:T(8,128)(2,1)} %bitcast.94), calls=%async_computation | async-start | bytes 11010048 | tf_op jit(solution)/shard_map/all_to_all | solution.py:734
  23.2 1.4 compare_convert_fusion.2
  25.3 1.0 copy.87
  26.4 0.8 broadcast_add_fusion.q_ref
  27.2 60.2 %all-to-all-done = bf16[128,8,2688]{2,1,0:T(8,128)(2,1)} async-done(((bf16[128,8,2688]{2,1,0:T(8,128)(2,1)}), bf16[128,8,2688]{2,1,0:T(8,128)(2,1)}, u32[]{:S(2)}, u32[]{:S(2)}) %all-to-all-start) | async-done | bytes 5505056 | tf_op jit(solution)/shard_map/all_to_all | solution.py:734
  87.4 5.4 %pack_rows.1.x_ref.b_ref.c_ref = bf16[512,2688]{1,0:T(8,128)(2,1)} custom-call(s32[4,128,1]{2,1,0:T(8,128)} %broadcast_add_fusion.q_ref, bf16[4,256,2688]{2,1,0:T(8,128)(2,1)} %bitcast.2.in_ref), custom_call_target="tpu_custom_call" | custom-call | tf_op jit(solution)/shard_map/pack_rows/pallas_call | solution.py:99
  92.8 0.8 slice.169
  93.6 1.1 compare_select_fusion
  95.4 2.9 collective-permute-start
  99.3 0.9 reshape.493.rows_ref
  100.7 1.1 broadcast_in_dim.47.keep_ref
  101.8 15.8 %first_pass.1 = (bf16[16,272,128]{2,1,0:T(8,128)(2,1)}, bf16[2048,512]{1,0:T(8,128)(2,1)}, bf16[2048,512]{1,0:T(8,128)(2,1)}, bf16[512,256]{1,0:T(8,128)(2,1)}, ...) custom-call(f32[64]{0:T(128)} %mul.121.gs_ref, f32[16,8,512]{2,1,0:T(8,128)} %reshape.493.rows_ref, ...), custom_call_target="tpu_custom_call" | custom-call | tf_op jit(solution)/shard_map/first_pass/pallas_call | solution.py:341
  117.7 19.7 %all_to_all.30 = bf16[8,544,128]{2,1,0:T(8,128)(2,1)} all-to-all(bf16[8,544,128]{2,1,0:T(8,128)(2,1)} %bitcast.100), channel_id=1, replica_groups=mesh['dp'=4,'ctx'=8,'head'=4] {'ctx'}, dimensions={0} | all-to-all | bytes 2228224 | tf_op jit(solution)/shard_map/all_to_all | solution.py:796
  137.3 2.3 scan_states.1
  139.6 4.2 %all-to-all-start.2 = ((bf16[8,512,128]{2,1,0:T(8,128)(2,1)}), bf16[8,512,128]{2,1,0:T(8,128)(2,1)S(1)}, u32[]{:S(2)}, u32[]{:S(2)}) async-start(bf16[8,512,128]{2,1,0:T(8,128)(2,1)} %bitcast.97), calls=%async_computation.2 | async-start | bytes 2097152 | tf_op jit(solution)/shard_map/all_to_all | solution.py:800
  144.0 14.8 %all-to-all-done.2 = bf16[8,512,128]{2,1,0:T(8,128)(2,1)S(1)} async-done(((bf16[8,512,128]{2,1,0:T(8,128)(2,1)}), bf16[8,512,128]{2,1,0:T(8,128)(2,1)S(1)}, u32[]{:S(2)}, u32[]{:S(2)}) %all-to-all-start.2) | async-done | bytes 1048608 | tf_op jit(solution)/shard_map/all_to_all | solution.py:800
  159.5 0.8 broadcast_in_dim.50.labc_ref
  160.3 1.2 broadcast_in_dim.48.keeps_ref
  161.5 37.9 %main_pass.1 = (bf16[512,2048]{1,0:T(8,128)(2,1)}, bf16[512,2048]{1,0:T(8,128)(2,1)}, bf16[512,256]{1,0:T(8,128)(2,1)}, bf16[512,256]{1,0:T(8,128)(2,1)}, f32[8,...) custom-call(f32[64]{0:T(128)} %mul.121.gs_ref, ...), custom_call_target="tpu_custom_call" | custom-call | tf_op jit(solution)/shard_map/main_pass/pallas_call | solution.py:605
  200.8 0.8 reshape.502
  201.6 1.1 reshape.498
  203.5 1.0 fusion.33
  205.2 4.5 %all-to-all-start.4 = ((f32[32,4,128]{2,1,0:T(4,128)}), f32[32,4,128]{2,1,0:T(4,128)S(1)}, u32[]{:S(2)}, u32[]{:S(2)}) async-start(f32[32,4,128]{2,1,0:T(4,128)} %bitcast.25), calls=%async_computation.4 | async-start | bytes 131072 | tf_op jit(solution)/shard_map/all_to_all | solution.py:849
  209.8 2.2 collective-permute-start.1
  212.0 5.2 %all-to-all-done.4 = f32[32,4,128]{2,1,0:T(4,128)S(1)} async-done(((f32[32,4,128]{2,1,0:T(4,128)}), f32[32,4,128]{2,1,0:T(4,128)S(1)}, u32[]{:S(2)}, u32[]{:S(2)}) %all-to-all-start.4) | async-done | bytes 65568 | tf_op jit(solution)/shard_map/all_to_all | solution.py:849
  217.9 3.9 %all-to-all-start.5 = ((f32[32,4,128]{2,1,0:T(4,128)}), f32[32,4,128]{2,1,0:T(4,128)S(1)}, u32[]{:S(2)}, u32[]{:S(2)}) async-start(f32[32,4,128]{2,1,0:T(4,128)} %broadcast_in_dim.53), calls=%async_computation.5 | async-start | bytes 131072 | tf_op jit(solution)/shard_map/all_to_all | solution.py:850
  223.8 5.8 %unpack_rows.1 = bf16[4,256,2688]{2,1,0:T(8,128)(2,1)} custom-call(s32[4,1,128]{2,1,0:T(1,128)} %add.191.q_ref, bf16[512,2048]{1,0:T(8,128)(2,1)} %get-tuple-element.45.x_ref, bf16[512,256]{1,0:T(8,128)(2,1)} %get-tuple-element.46.b_ref, bf16[512,256]{1,0:T(8,128)(2,1)} %get-tuple-element.47.c_ref, bf16[512,128]{1,0:T(8,128)(2,1)} %pad.8.dt_ref, ...), custom_call_target="tpu_custom_call" | custom-call | tf_op jit(solution)/shard_map/unpack_rows/pallas_call | solution.py:135
  229.6 8.4 %all-to-all-start.3 = ((bf16[128,8,2688]{2,1,0:T(8,128)(2,1)}), bf16[128,8,2688]{2,1,0:T(8,128)(2,1)}, u32[]{:S(2)}, u32[]{:S(2)}) async-start(bf16[128,8,2688]{2,1,0:T(8,128)(2,1)} %bitcast.95), calls=%async_computation.3 | async-start | bytes 11010048 | tf_op jit(solution)/shard_map/all_to_all | solution.py:734
  241.8 63.0 %all-to-all-done.3 = bf16[128,8,2688]{2,1,0:T(8,128)(2,1)} async-done(((bf16[128,8,2688]{2,1,0:T(8,128)(2,1)}), bf16[128,8,2688]{2,1,0:T(8,128)(2,1)}, u32[]{:S(2)}, u32[]{:S(2)}) %all-to-all-start.3) | async-done | bytes 5505056 | tf_op jit(solution)/shard_map/all_to_all | solution.py:734
  304.8 5.3 %home_rows.1 = (bf16[128,8192]{1,0:T(8,128)(2,1)}, bf16[128,1024]{1,0:T(8,128)(2,1)}, bf16[128,1024]{1,0:T(8,128)(2,1)}, bf16[128,128]{1,0:T(8,128)(2,1)}) custom-call(s32[128,1]{1,0:T(8,128)} %add.193.d_ref, bf16[4,256,2688]{2,1,0:T(8,128)(2,1)} %bitcast.23.in_ref), custom_call_target="tpu_custom_call" | custom-call | tf_op jit(solution)/shard_map/home_rows/pallas_call | solution.py:179
  (115 shorter events, 17.0 us)
Async XLA Ops:
  8.6 11.9 %copy-start.8 = (s32[1,6]{1,0:T(1,128)S(1)}, s32[1,6]{1,0:T(1,128)}, u32[]{:S(2)}) copy-start(s32[1,6]{1,0:T(1,128)} %param.19) | copy-start | bytes 76
  8.6 12.9 %copy-start.9 = (f32[32]{0:T(128)S(1)}, f32[32]{0:T(128)}, u32[]{:S(2)}) copy-start(f32[32]{0:T(128)} %param.25) | copy-start | bytes 388
  8.6 12.9 %copy-start.6 = (f32[2,256]{1,0:T(2,128)S(1)}, f32[2,256]{1,0:T(2,128)}, u32[]{:S(2)}) copy-start(f32[2,256]{1,0:T(2,128)} %param.23) | copy-start | bytes 6148
  8.6 78.7 %all-to-all-start = ((bf16[128,8,2688]{2,1,0:T(8,128)(2,1)}), bf16[128,8,2688]{2,1,0:T(8,128)(2,1)}, u32[]{:S(2)}, u32[]{:S(2)}) async-start(bf16[128,8,2688]{2,1,0:T(8,128)(2,1)} %bitcast.94), calls=%async_computation | async-start | bytes 11010048 | tf_op jit(solution)/shard_map/all_to_all | solution.py:734
  87.4 6.2 %copy-start.7 = (f32[32]{0:T(128)S(1)}, f32[32]{0:T(128)}, u32[]{:S(2)}) copy-start(f32[32]{0:T(128)} %param.24) | copy-start | bytes 388
  95.4 5.3 %collective-permute-start = (bf16[8,2688]{1,0:T(8,128)(2,1)S(1)}, bf16[8,2688]{1,0:T(8,128)(2,1)S(1)}, u32[]{:S(2)}, u32[]{:S(2)}) collective-permute-start(bf16[8,2688]{1,0:T(8,128)(2,1)S(1)} %slice.169), channel_id=1, source_target_pairs={{0,4},{4,8},{8,12},{12,16},{16,20},{20,24},{24,28},{1,5},{5,9},{9,... | collective-permute-start | bytes 129032 | tf_op jit(solution)/shard_map/ppermute | solution.py:686
  100.7 1.1 copy-start.1
  139.6 19.2 %all-to-all-start.2 = ((bf16[8,512,128]{2,1,0:T(8,128)(2,1)}), bf16[8,512,128]{2,1,0:T(8,128)(2,1)S(1)}, u32[]{:S(2)}, u32[]{:S(2)}) async-start(bf16[8,512,128]{2,1,0:T(8,128)(2,1)} %bitcast.97), calls=%async_computation.2 | async-start | bytes 2097152 | tf_op jit(solution)/shard_map/all_to_all | solution.py:800
  158.8 2.6 copy-start
  199.3 10.4 %copy-start.3 = (f32[8,2048]{1,0:T(8,128)S(1)}, f32[8,2048]{1,0:T(8,128)}, u32[]{:S(2)}) copy-start(f32[8,2048]{1,0:T(8,128)} %get-tuple-element.52) | copy-start | bytes 196612
  199.3 10.4 %copy-start.4 = (f32[8,256]{1,0:T(8,128)S(1)}, f32[8,256]{1,0:T(8,128)}, u32[]{:S(2)}) copy-start(f32[8,256]{1,0:T(8,128)} %get-tuple-element.53) | copy-start | bytes 24580
  199.3 10.4 %copy-start.5 = (f32[8,256]{1,0:T(8,128)S(1)}, f32[8,256]{1,0:T(8,128)}, u32[]{:S(2)}) copy-start(f32[8,256]{1,0:T(8,128)} %get-tuple-element.54) | copy-start | bytes 24580
  205.2 12.0 %all-to-all-start.4 = ((f32[32,4,128]{2,1,0:T(4,128)}), f32[32,4,128]{2,1,0:T(4,128)S(1)}, u32[]{:S(2)}, u32[]{:S(2)}) async-start(f32[32,4,128]{2,1,0:T(4,128)} %bitcast.25), calls=%async_computation.4 | async-start | bytes 131072 | tf_op jit(solution)/shard_map/all_to_all | solution.py:849
  209.8 13.3 %collective-permute-start.1 = (f32[8,2560]{1,0:T(8,128)S(1)}, f32[8,2560]{1,0:T(8,128)S(1)}, u32[]{:S(2)}, u32[]{:S(2)}) collective-permute-start(f32[8,2560]{1,0:T(8,128)S(1)} %pad_maximum_fusion), channel_id=1, source_target_pairs={{4,0},{8,4},{12,8},{16,12},{20,16},{24,20},{28,24},{5,1},{9,5},{13... | collective-permute-start | bytes 245768 | tf_op jit(solution)/shard_map/ppermute | solution.py:686
  217.9 11.7 %all-to-all-start.5 = ((f32[32,4,128]{2,1,0:T(4,128)}), f32[32,4,128]{2,1,0:T(4,128)S(1)}, u32[]{:S(2)}, u32[]{:S(2)}) async-start(f32[32,4,128]{2,1,0:T(4,128)} %broadcast_in_dim.53), calls=%async_computation.5 | async-start | bytes 131072 | tf_op jit(solution)/shard_map/all_to_all | solution.py:850
  223.1 0.6 copy-start.2
  229.6 75.2 %all-to-all-start.3 = ((bf16[128,8,2688]{2,1,0:T(8,128)(2,1)}), bf16[128,8,2688]{2,1,0:T(8,128)(2,1)}, u32[]{:S(2)}, u32[]{:S(2)}) async-start(bf16[128,8,2688]{2,1,0:T(8,128)(2,1)} %bitcast.95), calls=%async_computation.3 | async-start | bytes 11010048 | tf_op jit(solution)/shard_map/all_to_all | solution.py:734

commit v2 on v1

--- a/solution.py
+++ b/solution.py
@@ -26,6 +26,8 @@
 PAIRS = 16
 GROUP_PAIRS = 8
 EXTRA = 16
+CMAIN = XCOLS + 2 * BCOLS
+OWN_HEADS = HEADS // WAYS
 NEG = -1e30
 
 F32 = jnp.float32
@@ -109,26 +111,26 @@
     )(q_col, landed)
 
 
-def unpack_kernel(q_ref, x_ref, b_ref, c_ref, dt_ref, tx_ref, tb_ref, tc_ref, back_ref, out_ref):
+def unpack_kernel(q_ref, x_ref, b_ref, c_ref, dt_ref, tail_ref, back_ref, out_ref):
     j = pl.program_id(0)
     rows = x_ref.shape[0]
     slots = out_ref.shape[1]
     spread = one_hot(iota((slots, rows), 0) == q_ref[0])
     last = j == WAYS - 1
 
-    def one(ref, tail_ref, low, high):
+    def one(ref, low, high):
         whole = ref[...].astype(F32)
-        tail = tail_ref[...] + back_ref[:, low:high]
+        tail = tail_ref[:, low:high] + back_ref[:, low:high]
         fixed = jnp.concatenate([whole[: rows - 8], jnp.where(last, tail, whole[rows - 8 :])])
         out_ref[0, :, low:high] = dot(spread, fixed.astype(BF16)).astype(BF16)
 
-    one(x_ref, tx_ref, 0, XCOLS)
-    one(b_ref, tb_ref, XCOLS, XCOLS + BCOLS)
-    one(c_ref, tc_ref, XCOLS + BCOLS, XCOLS + 2 * BCOLS)
+    one(x_ref, 0, XCOLS)
+    one(b_ref, XCOLS, XCOLS + BCOLS)
+    one(c_ref, XCOLS + BCOLS, XCOLS + 2 * BCOLS)
     out_ref[0, :, XCOLS + 2 * BCOLS :] = dot(spread, dt_ref[...]).astype(BF16)
 
 
-def unpack_rows(q_row, dx, db, dc, ddt, tx, tb, tc, back):
+def unpack_rows(q_row, dx, db, dc, ddt, tails, back):
     slots = OWNERS * DEPTH * BLK
     rows = ROWS // WAYS
     full = lambda j: (0, 0)
@@ -141,15 +143,13 @@
             pl.BlockSpec((rows, BCOLS), lambda j: (j, 0)),
             pl.BlockSpec((rows, BCOLS), lambda j: (j, 0)),
             pl.BlockSpec((rows, LANES), lambda j: (j, 0)),
-            pl.BlockSpec((8, XCOLS), full),
-            pl.BlockSpec((8, BCOLS), full),
-            pl.BlockSpec((8, BCOLS), full),
-            pl.BlockSpec((8, XCOLS + 2 * BCOLS), full),
+            pl.BlockSpec((8, CMAIN), full),
+            pl.BlockSpec((8, CMAIN), full),
         ],
         out_specs=pl.BlockSpec((1, slots, COLS), lambda j: (j, 0, 0)),
         out_shape=jax.ShapeDtypeStruct((WAYS, slots, COLS), BF16),
         name="unpack_rows",
-    )(q_row, dx, db, dc, ddt, tx, tb, tc, back)
+    )(q_row, dx, db, dc, ddt, tails, back)
 
 
 def home_kernel(d_ref, in_ref, x_ref, b_ref, c_ref, dt_ref, acc_ref):
@@ -370,34 +370,84 @@
     )(gs, rows, *conv_args, out_grad)
 
 
-def scan_kernel(in_ref, out_ref):
-    count = in_ref.shape[0]
+def state_kernel(count, in_ref, out_ref, land_ref, part_ref, send, recv, send2, recv2, own, own2):
+    me = lax.axis_index("ctx")
+    dp, head = lax.axis_index("dp"), lax.axis_index("head")
+    barrier = pltpu.get_barrier_semaphore()
+    for d in range(1, count):
+        pl.semaphore_signal(
+            barrier,
+            inc=1,
+            device_id=(dp, lax.rem(me + d, count), head),
+            device_id_type=pl.DeviceIdType.MESH,
+        )
+    pl.semaphore_wait(barrier, count - 1)
+
+    def moved(source, target, sends, recvs, d):
+        peer = lax.rem(me + d, count)
+        return pltpu.make_async_remote_copy(
+            src_ref=source.at[peer],
+            dst_ref=target.at[me],
+            send_sem=sends.at[d],
+            recv_sem=recvs.at[d],
+            device_id=(dp, peer, head),
+            device_id_type=pl.DeviceIdType.MESH,
+        )
+
+    first = [moved(in_ref, land_ref, send, recv, d) for d in range(1, count)]
+    for copy in first:
+        copy.start()
+    kept = pltpu.make_async_copy(in_ref.at[me], land_ref.at[me], own)
+    kept.start()
+    kept.wait()
+    for copy in first:
+        copy.wait()
+    pairs = land_ref.shape[1]
     shape = (LANES, STATE)
-    gains = []
-    for at in range(count):
-        extra = in_ref[at, 0, 2 * LANES :, :].astype(F32)
-        gain = extra[0:1] + extra[8:9]
-        gains.append(pair_scale(gain[:, 0:1], gain[:, HEAD_DIM : HEAD_DIM + 1], shape))
-    state = jnp.zeros(shape, F32)
-    for at in range(count):
-        out_ref[at, 0, 0:LANES, :] = state.astype(BF16)
-        state = gains[at] * state + in_ref[at, 0, 0:LANES, :].astype(F32)
-    state = jnp.zeros(shape, F32)
-    for at in reversed(range(count)):
-        out_ref[at, 0, LANES : 2 * LANES, :] = state.astype(BF16)
-        state = in_ref[at, 0, LANES : 2 * LANES, :].astype(F32) + gains[at] * state
-
-
-def scan_states(landed):
-    count, pairs = landed.shape[:2]
+    for pair in range(pairs):
+        gains = []
+        for at in range(count):
+            extra = land_ref[at, pair, 2 * LANES :, :].astype(F32)
+            gain = extra[0:1] + extra[8:9]
+            gains.append(pair_scale(gain[:, 0:1], gain[:, HEAD_DIM : HEAD_DIM + 1], shape))
+        state = jnp.zeros(shape, F32)
+        for at in range(count):
+            part_ref[at, pair, 0:LANES, :] = state.astype(BF16)
+            state = gains[at] * state + land_ref[at, pair, 0:LANES, :].astype(F32)
+        state = jnp.zeros(shape, F32)
+        for at in reversed(range(count)):
+            part_ref[at, pair, LANES : 2 * LANES, :] = state.astype(BF16)
+            state = land_ref[at, pair, LANES : 2 * LANES, :].astype(F32) + gains[at] * state
+    second = [moved(part_ref, out_ref, send2, recv2, d) for d in range(1, count)]
+    for copy in second:
+        copy.start()
+    kept = pltpu.make_async_copy(part_ref.at[me], out_ref.at[me], own2)
+    kept.start()
+    kept.wait()
+    for copy in second:
+        copy.wait()
+
+
+def exchange_states(parts):
+    count, pairs = parts.shape[:2]
     return pl.pallas_call(
-        scan_kernel,
-        grid=(pairs,),
-        in_specs=[pl.BlockSpec((count, 1, 2 * LANES + EXTRA, STATE), lambda i: (0, i, 0, 0))],
-        out_specs=pl.BlockSpec((count, 1, 2 * LANES, STATE), lambda i: (0, i, 0, 0)),
+        functools.partial(state_kernel, count),
+        in_specs=[pl.BlockSpec(memory_space=pltpu.VMEM)],
+        out_specs=pl.BlockSpec(memory_space=pltpu.VMEM),
         out_shape=jax.ShapeDtypeStruct((count, pairs, 2 * LANES, STATE), BF16),
-        name="scan_states",
-    )(landed)
+        scratch_shapes=[
+            pltpu.VMEM(parts.shape, BF16),
+            pltpu.VMEM((count, pairs, 2 * LANES, STATE), BF16),
+            pltpu.SemaphoreType.DMA((count,)),
+            pltpu.SemaphoreType.DMA((count,)),
+            pltpu.SemaphoreType.DMA((count,)),
+            pltpu.SemaphoreType.DMA((count,)),
+            pltpu.SemaphoreType.DMA,
+            pltpu.SemaphoreType.DMA,
+        ],
+        compiler_params=pltpu.CompilerParams(collective_id=0, has_side_effects=True),
+        name="exchange_states",
+    )(parts)
 
 
 def main_kernel(
@@ -428,20 +478,20 @@
     t1_ref,
     labr_ref,
     labc_ref,
+    step_ref,
+    sig_ref,
+    rate_ref,
     y_ref,
     dx_ref,
     db_ref,
     dc_ref,
-    tx_ref,
-    tb_ref,
-    tc_ref,
-    px_ref,
-    pb_ref,
-    pc_ref,
-    rout_ref,
-    sx_ref,
-    sb_ref,
-    sc_ref,
+    ddt_ref,
+    tail_ref,
+    front_ref,
+    sums_ref,
+    dcum_ref,
+    dstep_ref,
+    dskip_ref,
     mask_ref,
     score_ref,
     dscore_ref,
@@ -461,6 +511,9 @@
     @pl.when(i == 0)
     def _():
         dpad_ref[...] = jnp.zeros_like(dpad_ref)
+        dcum_ref[...] = jnp.zeros_like(dcum_ref)
+        dstep_ref[...] = jnp.zeros_like(dstep_ref)
+        dskip_ref[...] = jnp.zeros_like(dskip_ref)
         for k in range(2):
             for t in range(2):
                 shape = (STRETCH, LANES)
@@ -492,6 +545,7 @@
     leave0 = t1_ref[...] + pair_scale(*gains[1], shape) * leave1
     enters = (enter0, enter1)
     leaves = (leave0, leave1)
+    seat = iota((OWN_HEADS, STRETCH), 0)
     for k in range(2):
         span = spans[k]
         x = xT_ref[:, span].astype(F32)
@@ -548,20 +602,21 @@
             )
             dcum = jnp.sum(cums[part], axis=0, keepdims=True) - ended
             dcum = dcum + jnp.where(last, total + gains[k][h] * bend, 0.0)
-            rout_ref[0, h : h + 1, span] = (
-                jnp.sum(direct[part], axis=0, keepdims=True) + ends[h] * pulled
-            )
-            rout_ref[0, 2 + h : 3 + h, span] = dcum
-            rout_ref[0, 4 + h : 5 + h, span] = jnp.sum(skipped[part], axis=0, keepdims=True)
-    rout_ref[0, 6:8, :] = jnp.zeros((2, ROWS), F32)
+            dstep = jnp.sum(direct[part], axis=0, keepdims=True) + ends[h] * pulled
+            dskip = jnp.sum(skipped[part], axis=0, keepdims=True)
+            here = seat == 2 * i + h
+            dcum_ref[:, span] += jnp.where(here, dcum, 0.0)
+            dstep_ref[:, span] += jnp.where(here, dstep, 0.0)
+            dskip_ref[:, span] += jnp.where(here, dskip, 0.0)
 
     moved, sums = conv_back(
         pad_ref, dpad_ref, x_ref, hx_ref, xt_ref[...], xb_ref[...], keep_ref, keeps_ref, dxn_ref[...]
     )
-    sx_ref[...] = moved[0:8]
-    tx_ref[...] = moved[ROWS:]
+    lanes = pl.ds(pl.multiple_of(i * LANES, LANES), LANES)
+    front_ref[:, lanes] = moved[0:8]
+    tail_ref[:, lanes] = moved[ROWS:]
     dx_ref[...] = moved[8:].astype(BF16)
-    px_ref[0] = sums
+    sums_ref[:, lanes] = sums
 
     @pl.when(i % GROUP_PAIRS == GROUP_PAIRS - 1)
     def _():
@@ -573,10 +628,10 @@
             dcT_ref[:, span] = dcT
             dbT_ref[:, span] = dbT
         sides = (
-            (dbT_ref, b_ref, hb_ref, bt_ref, bb_ref, db_ref, sb_ref, tb_ref, pb_ref),
-            (dcT_ref, c_ref, hc_ref, ct_ref, cb_ref, dc_ref, sc_ref, tc_ref, pc_ref),
+            (dbT_ref, b_ref, hb_ref, bt_ref, bb_ref, db_ref, XCOLS),
+            (dcT_ref, c_ref, hc_ref, ct_ref, cb_ref, dc_ref, XCOLS + BCOLS),
         )
-        for grad_ref, in_ref, halo_ref, tap_ref, bias_ref, out_ref, s_ref, t_ref, p_ref in sides:
+        for grad_ref, in_ref, halo_ref, tap_ref, bias_ref, out_ref, left in sides:
             for span in spans:
                 dxn_ref[span, :] = dot_nt(wide_unit, grad_ref[:, span].astype(BF16))
             moved, sums = conv_back(
@@ -590,17 +645,48 @@
                 keeps_ref,
                 dxn_ref[...],
             )
-            s_ref[...] = moved[0:8]
-            t_ref[...] = moved[ROWS:]
+            at = pl.multiple_of(left + (i // GROUP_PAIRS) * LANES, LANES)
+            front_ref[:, pl.ds(at, LANES)] = moved[0:8]
+            tail_ref[:, pl.ds(at, LANES)] = moved[ROWS:]
             out_ref[...] = moved[8:].astype(BF16)
-            p_ref[0] = sums
-
-
-def main_pass(gs, skip, rows, conv_args, keeps, out_grad, xT, gT, bn, cn, ent, e0, t1, labr, labc):
+            sums_ref[:, pl.ds(at, LANES)] = sums
+
+    @pl.when(i == PAIRS - 1)
+    def _():
+        shape = (STRETCH, STRETCH)
+        tri = jnp.where(iota(shape, 0) >= iota(shape, 1), 1.0, 0.0)
+        bias_sum = jnp.zeros((OWN_HEADS, 1), F32)
+        rate_sum = jnp.zeros((OWN_HEADS, 1), F32)
+        for span in spans:
+            after = lax.dot_general(
+                dcum_ref[:, span],
+                tri,
+                (((1,), (0,)), ((), ())),
+                precision=lax.Precision.HIGHEST,
+                preferred_element_type=F32,
+            )
+            dlogit = (dstep_ref[:, span] - rate_ref[...] * after) * sig_ref[:, span]
+            bias_sum += jnp.sum(dlogit, axis=1, keepdims=True)
+            rate_sum -= jnp.sum(after * step_ref[:, span], axis=1, keepdims=True)
+            tall = jnp.concatenate([dlogit, jnp.zeros((LANES - OWN_HEADS, STRETCH), F32)])
+            ddt_ref[span, :] = dot_nt(wide_unit, tall.astype(BF16)).astype(BF16)
+        skip_sum = jnp.sum(dskip_ref[...], axis=1, keepdims=True)
+        diagonal = iota((OWN_HEADS, LANES), 0) == iota((OWN_HEADS, LANES), 1)
+        lines = [
+            jnp.sum(jnp.where(diagonal, value, 0.0), axis=0, keepdims=True)
+            for value in (bias_sum, rate_sum, skip_sum)
+        ]
+        sums_ref[:, CMAIN:] = jnp.concatenate(lines + [jnp.zeros((5, LANES), F32)])
+
+
+def main_pass(
+    gs, skip, rows, conv_args, keeps, out_grad, xT, gT, bn, cn, ent, e0, t1, labr, labc, heads
+):
     wide = lambda i: (i, 0)
     col = lambda i: (0, i)
     group = lambda i: (0, i // GROUP_PAIRS)
     triple = lambda i: (i, 0, 0)
+    fixed = lambda i: (0, 0)
     square = (2, STRETCH, STRETCH)
     return pl.pallas_call(
         main_kernel,
@@ -621,42 +707,36 @@
             pl.BlockSpec((1, 2 * LANES, STATE), triple),
             pl.BlockSpec((LANES, STATE), wide),
             pl.BlockSpec((LANES, STATE), wide),
-            pl.BlockSpec((8, ROWS), lambda i: (0, 0)),
-            pl.BlockSpec((ROWS, LANES), lambda i: (0, 0)),
+            pl.BlockSpec((8, ROWS), fixed),
+            pl.BlockSpec((ROWS, LANES), fixed),
+            pl.BlockSpec((OWN_HEADS, ROWS), fixed),
+            pl.BlockSpec((OWN_HEADS, ROWS), fixed),
+            pl.BlockSpec((OWN_HEADS, 1), fixed),
         ],
         out_specs=[
             pl.BlockSpec((ROWS, LANES), col),
             pl.BlockSpec((ROWS, LANES), col),
             pl.BlockSpec((ROWS, LANES), group),
             pl.BlockSpec((ROWS, LANES), group),
-            pl.BlockSpec((8, LANES), col),
-            pl.BlockSpec((8, LANES), group),
-            pl.BlockSpec((8, LANES), group),
-            pl.BlockSpec((1, 8, LANES), triple),
-            pl.BlockSpec((1, 8, LANES), lambda i: (i // GROUP_PAIRS, 0, 0)),
-            pl.BlockSpec((1, 8, LANES), lambda i: (i // GROUP_PAIRS, 0, 0)),
-            pl.BlockSpec((1, 8, ROWS), triple),
-            pl.BlockSpec((8, LANES), col),
-            pl.BlockSpec((8, LANES), group),
-            pl.BlockSpec((8, LANES), group),
+            pl.BlockSpec((ROWS, LANES), fixed),
+            pl.BlockSpec((8, CMAIN), fixed),
+            pl.BlockSpec((8, CMAIN), fixed),
+            pl.BlockSpec((8, COLS), fixed),
         ],
         out_shape=[
             jax.ShapeDtypeStruct((ROWS, XCOLS), BF16),
             jax.ShapeDtypeStruct((ROWS, XCOLS), BF16),
             jax.ShapeDtypeStruct((ROWS, BCOLS), BF16),
             jax.ShapeDtypeStruct((ROWS, BCOLS), BF16),
-            jax.ShapeDtypeStruct((8, XCOLS), F32),
-            jax.ShapeDtypeStruct((8, BCOLS), F32),
-            jax.ShapeDtypeStruct((8, BCOLS), F32),
-            jax.ShapeDtypeStruct((PAIRS, 8, LANES), F32),
-            jax.ShapeDtypeStruct((2, 8, LANES), F32),
-            jax.ShapeDtypeStruct((2, 8, LANES), F32),
-            jax.ShapeDtypeStruct((PAIRS, 8, ROWS), F32),
-            jax.ShapeDtypeStruct((8, XCOLS), F32),
-            jax.ShapeDtypeStruct((8, BCOLS), F32),
-            jax.ShapeDtypeStruct((8, BCOLS), F32),
+            jax.ShapeDtypeStruct((ROWS, LANES), BF16),
+            jax.ShapeDtypeStruct((8, CMAIN), F32),
+            jax.ShapeDtypeStruct((8, CMAIN), F32),
+            jax.ShapeDtypeStruct((8, COLS), F32),
         ],
         scratch_shapes=[
+            pltpu.VMEM((OWN_HEADS, ROWS), F32),
+            pltpu.VMEM((OWN_HEADS, ROWS), F32),
+            pltpu.VMEM((OWN_HEADS, ROWS), F32),
             pltpu.VMEM(square, F32),
             pltpu.VMEM(square, F32),
             pltpu.VMEM(square, F32),
@@ -669,7 +749,7 @@
             pltpu.VMEM((ROWS, LANES), F32),
         ],
         name="main_pass",
-    )(gs, skip, rows, *conv_args, keeps, out_grad, xT, gT, bn, cn, ent, e0, t1, labr, labc)
+    )(gs, skip, rows, *conv_args, keeps, out_grad, xT, gT, bn, cn, ent, e0, t1, labr, labc, *heads)
 
 
 def segment_of(ends, positions):
@@ -764,6 +844,7 @@
     dt_in = packed[:, XCOLS + 2 * BCOLS : XCOLS + 2 * BCOLS + heads_dev].astype(F32).T
     logits = dt_in + dt_bias[:, None]
     step = jax.nn.softplus(logits)
+    sig = jax.nn.sigmoid(logits)
     tri = jnp.tril(jnp.ones((STRETCH, STRETCH), F32))
     folded = step.reshape(heads_dev, 2, STRETCH)
     cum = exact("hks,rs->hkr", -decay_rate[:, None, None] * folded, tri)
@@ -793,67 +874,43 @@
 
     per = PAIRS // contexts
     tall = 2 * LANES + EXTRA
-    ep = lax.all_to_all(
-        ep.reshape(contexts, per * tall, STATE), "ctx", split_axis=0, concat_axis=0, tiled=True
+    ent = exchange_states(ep.reshape(contexts, per, tall, STATE))
+    ent = ent.reshape(PAIRS, 2 * LANES, STATE)
+
+    heads = (step, sig, decay_rate[:, None])
+    y, dx, db, dc, ddt, tails, fronts, sums = main_pass(
+        gs,
+        skip_gain,
+        rows,
+        conv_args,
+        keeps,
+        out_grad,
+        xT,
+        gT,
+        bn,
+        cn,
+        ent,
+        e0,
+        t1,
+        labr,
+        labc,
+        heads,
     )
-    scanned = scan_states(ep.reshape(contexts, per, tall, STATE))
-    scanned = lax.all_to_all(
-        scanned.reshape(contexts, per * 2 * LANES, STATE),
-        "ctx",
-        split_axis=0,
-        concat_axis=0,
-        tiled=True,
-    )
-    ent = scanned.reshape(PAIRS, 2 * LANES, STATE)
-
-    y, dx, db, dc, tx, tb, tc, px, pb, pc, rout, sx, sb, sc = main_pass(
-        gs, skip_gain, rows, conv_args, keeps, out_grad, xT, gT, bn, cn, ent, e0, t1, labr, labc
-    )
-    back = passed_along(jnp.concatenate([sx, sb, sc], axis=1), "ctx", -1)
-
-    parts = rout.reshape(PAIRS, 4, 2, 2, STRETCH)
-    parts = jnp.swapaxes(parts, 0, 1).reshape(4, heads_dev, 2, STRETCH)
-    after = exact("hks,sr->hkr", parts[1], tri)
-    dstep = parts[0] - decay_rate[:, None, None] * after
-    dlogit = dstep.reshape(heads_dev, ROWS) * jax.nn.sigmoid(logits)
-    ddt = jnp.pad(dlogit.T.astype(BF16), ((0, 0), (0, LANES - heads_dev)))
-    scalars = jnp.concatenate(
-        [
-            jnp.sum(dlogit, axis=1),
-            -jnp.sum(after * folded, axis=(1, 2)),
-            jnp.sum(parts[2], axis=(1, 2)),
-            jnp.zeros((LANES - 3 * heads_dev,), F32),
-        ]
-    )
-
-    stacked = jnp.concatenate(
-        [
-            px[:, :5].reshape(-1, LANES),
-            pb[:, :5].reshape(-1, LANES),
-            pc[:, :5].reshape(-1, LANES),
-            scalars[None, :],
-        ]
-    )
-    count = stacked.shape[0]
-    chunk = 4
-    stacked = jnp.pad(stacked, ((0, OWNERS * chunk - count), (0, 0)))
-
-    returned = exchange(
-        unpack_rows(comes[:, None, :], dx, db, dc, ddt, tx, tb, tc, back)
-    )
+    back = passed_along(fronts, "ctx", -1)
+    returned = exchange(unpack_rows(comes[:, None, :], dx, db, dc, ddt, tails, back))
     x_grad, b_grad, c_grad, dt_grad = home_rows(goes[:, None], returned)
 
     swap = functools.partial(
         lax.all_to_all, axis_name=("dp", "ctx"), split_axis=0, concat_axis=0, tiled=True
     )
-    partial_sum = jnp.sum(swap(stacked.reshape(OWNERS, chunk, LANES)), axis=0)
-    whole = swap(jnp.broadcast_to(partial_sum[None], (OWNERS, chunk, LANES)))
-    whole = whole.reshape(OWNERS * chunk, LANES)
-    at = PAIRS * 5
-    sum_x = jnp.swapaxes(whole[:at].reshape(PAIRS, 5, LANES), 0, 1).reshape(5, XCOLS)
-    sum_b = jnp.swapaxes(whole[at : at + 10].reshape(2, 5, LANES), 0, 1).reshape(5, BCOLS)
-    sum_c = jnp.swapaxes(whole[at + 10 : at + 20].reshape(2, 5, LANES), 0, 1).reshape(5, BCOLS)
-    tail = whole[at + 20]
+    share = COLS // OWNERS
+    partial_sum = jnp.sum(swap(jnp.swapaxes(sums.reshape(8, OWNERS, share), 0, 1)), axis=0)
+    whole = swap(jnp.broadcast_to(partial_sum[None], (OWNERS, 8, share)))
+    whole = jnp.swapaxes(whole, 0, 1).reshape(8, COLS)
+    sum_x = whole[:, :XCOLS]
+    sum_b = whole[:, XCOLS : XCOLS + BCOLS]
+    sum_c = whole[:, XCOLS + BCOLS : CMAIN]
+    tail = whole[:, CMAIN : CMAIN + heads_dev]
     return (
         y,
         x_grad,
@@ -864,9 +921,9 @@
         jnp.stack([sum_b[:4], sum_c[:4]]),
         sum_x[4],
         jnp.stack([sum_b[4], sum_c[4]]),
-        tail[:heads_dev],
-        tail[heads_dev : 2 * heads_dev],
-        tail[2 * heads_dev : 3 * heads_dev],
+        tail[0],
+        tail[1],
+        tail[2],
     )
 
 

time: 312 us -> 303 us (0.971)
  Pallas kernels: 78.3 us -> 109 us
  waiting for transfers between devices: 143 us -> 126 us
  starting transfers between devices: 38.1 us -> 28.1 us
  blocking collectives: 19.7 us -> 11.9 us
    pallas_call x1, Pallas kernels: 2.29 us -> 31.7 us  [exchange_states(): pl.pallas_call(functools.partial(state_kernel, count), in_specs=[pl.Block...]
    all_to_all x3 -> x1, waiting for transfers between devices: 20 us -> 0.01 us  [on_device(): whole = swap(jnp.broadcast_to(partial_sum[None], (OWNERS, 8, share)))]
    all_to_all x3 -> x1, starting transfers between devices: 12.6 us -> 3.91 us  [on_device(): whole = swap(jnp.broadcast_to(partial_sum[None], (OWNERS, 8, share)))]
    all_to_all x1, blocking collectives: 19.7 us -> 11.9 us  [on_device(): swap(jnp.swapaxes(sums.reshape(8, OWNERS, share), 0, 1))]
    ppermute x2, waiting for transfers between devices: 0.01 us -> 3.8 us  [passed_along(): lax.ppermute(value, axis, [(source, source + steps) for source in range(f...]
  transfers between devices with their start and end apart: 7 -> 5, of which waited for: 4 -> 3; matrix products, arithmetic and copies ran while one was open for 5% -> 5% of each run, Pallas kernels for 2% -> 2%
where the time goes in v2:
time: 303 us; the launch traced here: 302 us
  waiting for transfers between devices  126 us (42%)
  Pallas kernels  109 us (36%)
  starting transfers between devices  28.1 us (9%)
  local copies, waits for them, and re-layouts  18.5 us (6%)
  blocking collectives  11.9 us (4%)
  other arithmetic  6.84 us (2%)
    all_to_all x2, waiting for transfers between devices, exchange(): lax.all_to_all(value, ROUTE, split_axis=0, concat_axis=0, tiled=True)  122 us
    pallas_call x1, Pallas kernels, main_pass(): pl.pallas_call(main_kernel, grid=(PAIRS,), in_specs=[pl.BlockSpec(memory_...  38.9 us
    pallas_call x1, Pallas kernels, exchange_states(): pl.pallas_call(functools.partial(state_kernel, count), in_specs=[pl.Block...  31.7 us
    all_to_all x2, starting transfers between devices, exchange(): lax.all_to_all(value, ROUTE, split_axis=0, concat_axis=0, tiled=True)  19.1 us
    pallas_call x1, Pallas kernels, first_pass(): pl.pallas_call(first_kernel, grid=(PAIRS,), in_specs=[pl.BlockSpec(memory...  15.8 us
    all_to_all x1, blocking collectives, on_device(): swap(jnp.swapaxes(sums.reshape(8, OWNERS, share), 0, 1))  11.9 us
  transfers between devices with their start and end apart: 5, of which 3 were waited for; matrix products, arithmetic and copies ran while one was open for 5% of the time, Pallas kernels for 2%

profile of v2, /device:TPU:1, one launch (start us, length us, event | category | flops | bytes accessed | tf_op | source)
XLA Modules:
  0.0 301.6 jit_solution(4276407656888797915)
XLA Ops:
  0.7 0.8 reshape.430
  2.8 5.8 %send_rows.1 = bf16[4,256,2688]{2,1,0:T(8,128)(2,1)} custom-call(s32[1,128]{1,0:T(1,128)} %add.177.d_ref, bf16[128,8192]{1,0:T(8,128)(2,1)} %x_ref.1, bf16[128,1024]{1,0:T(8,128)(2,1)} %b_ref.1, bf16[128,1024]{1,0:T(8,128)(2,1)} %c_ref.1, bf16[128,128]{1,0:T(8,128)(2,1)} %dt_ref.1), custom_call_target="tpu_custom_call" | custom-call | tf_op jit(solution)/shard_map/send_rows/pallas_call | solution.py:75
  8.6 11.9 %all-to-all-start = ((bf16[128,8,2688]{2,1,0:T(8,128)(2,1)}), bf16[128,8,2688]{2,1,0:T(8,128)(2,1)}, u32[]{:S(2)}, u32[]{:S(2)}) async-start(bf16[128,8,2688]{2,1,0:T(8,128)(2,1)} %bitcast.63), calls=%async_computation | async-start | bytes 11010048 | tf_op jit(solution)/shard_map/all_to_all | solution.py:814
  20.7 0.8 dynamic_slice.7
  23.4 1.4 compare_convert_fusion.2
  24.9 0.7 copy.113.rate_ref
  26.2 1.0 copy.103
  27.3 0.8 broadcast_add_fusion.q_ref
  28.1 59.3 %all-to-all-done = bf16[128,8,2688]{2,1,0:T(8,128)(2,1)} async-done(((bf16[128,8,2688]{2,1,0:T(8,128)(2,1)}), bf16[128,8,2688]{2,1,0:T(8,128)(2,1)}, u32[]{:S(2)}, u32[]{:S(2)}) %all-to-all-start) | async-done | bytes 5505056 | tf_op jit(solution)/shard_map/all_to_all | solution.py:814
  87.4 5.4 %pack_rows.1.x_ref.b_ref.c_ref = bf16[512,2688]{1,0:T(8,128)(2,1)} custom-call(s32[4,128,1]{2,1,0:T(8,128)} %broadcast_add_fusion.q_ref, bf16[4,256,2688]{2,1,0:T(8,128)(2,1)} %bitcast.2.in_ref), custom_call_target="tpu_custom_call" | custom-call | tf_op jit(solution)/shard_map/pack_rows/pallas_call | solution.py:101
  92.8 0.8 slice.111
  93.6 0.9 slice.108
  94.6 0.7 fusion.8
  95.9 2.9 collective-permute-start
  99.7 0.9 reshape.437.rows_ref
  101.2 1.1 broadcast_in_dim.45.keep_ref
  102.3 15.8 %first_pass.1 = (bf16[16,272,128]{2,1,0:T(8,128)(2,1)}, bf16[2048,512]{1,0:T(8,128)(2,1)}, bf16[2048,512]{1,0:T(8,128)(2,1)}, bf16[512,256]{1,0:T(8,128)(2,1)}, ...) custom-call(f32[64]{0:T(128)} %mul.107.gs_ref, f32[16,8,512]{2,1,0:T(8,128)} %reshape.437.rows_ref, ...), custom_call_target="tpu_custom_call" | custom-call | tf_op jit(solution)/shard_map/first_pass/pallas_call | solution.py:341
  118.1 31.7 %exchange_states.1 = bf16[8,2,256,128]{3,2,1,0:T(8,128)(2,1)} custom-call(bf16[8,2,272,128]{3,2,1,0:T(8,128)(2,1)} %bitcast.66), custom_call_target="tpu_custom_call" | custom-call | tf_op jit(solution)/shard_map/exchange_states/pallas_call | solution.py:433
  150.4 0.8 broadcast_in_dim.48.labc_ref
  151.3 1.2 broadcast_in_dim.46.keeps_ref
  152.5 38.9 %main_pass.1 = (bf16[512,2048]{1,0:T(8,128)(2,1)}, bf16[512,2048]{1,0:T(8,128)(2,1)}, bf16[512,256]{1,0:T(8,128)(2,1)}, bf16[512,256]{1,0:T(8,128)(2,1)}, bf16[5...) custom-call(f32[64]{0:T(128)} %mul.107.gs_ref, f32[32]{0:T(128)} %skip_ref.1, ...), custom_call_target="tpu_custom_call" | custom-call | tf_op jit(solution)/shard_map/main_pass/pallas_call | solution.py:691
  191.4 1.1 reshape.442
  192.6 11.9 %all_to_all.20 = f32[32,8,84]{2,1,0:T(8,128)S(1)} all-to-all(f32[32,8,84]{2,1,0:T(8,128)S(1)} %bitcast.71), channel_id=1, replica_groups=mesh['dp'=4,'ctx'=8,'head'=4] {'dp','ctx'}, dimensions={0} | all-to-all | bytes 172032 | tf_op jit(solution)/shard_map/all_to_all | solution.py:907
  204.5 0.7 broadcast_in_dim.50
  205.2 3.9 %all-to-all-start.3 = ((f32[32,8,84]{2,1,0:T(8,128)}), f32[32,8,84]{2,1,0:T(8,128)S(1)}, u32[]{:S(2)}, u32[]{:S(2)}) async-start(f32[32,8,84]{2,1,0:T(8,128)} %broadcast_in_dim.50), calls=%async_computation.3 | async-start | bytes 262144 | tf_op jit(solution)/shard_map/all_to_all | solution.py:908
  209.1 2.3 collective-permute-start.1
  212.1 3.8 %collective-permute-done.1.back_ref = f32[8,2560]{1,0:T(8,128)S(1)} collective-permute-done((f32[8,2560]{1,0:T(8,128)}, f32[8,2560]{1,0:T(8,128)S(1)}, u32[]{:S(2)}, u32[]{:S(2)}) %collective-permute-start.1) | collective-permute-done | bytes 81952 | tf_op jit(solution)/shard_map/ppermute | solution.py:766
  216.5 5.7 %unpack_rows.1 = bf16[4,256,2688]{2,1,0:T(8,128)(2,1)} custom-call(s32[4,1,128]{2,1,0:T(1,128)} %add.188.q_ref, bf16[512,2048]{1,0:T(8,128)(2,1)} %get-tuple-element.39.x_ref, bf16[512,256]{1,0:T(8,128)(2,1)} %get-tuple-element.40.b_ref, bf16[512,256]{1,0:T(8,128)(2,1)} %get-tuple-element.41.c_ref, bf16[512,128]{1,0:T(8,128)(2,1)} %get-tuple-element.42.dt_ref, ...), custom_call_target="tpu_custom_call" | custom-call | tf_op jit(solution)/shard_map/unpack_rows/pallas_call | solution.py:137
  222.2 7.2 %all-to-all-start.1 = ((bf16[128,8,2688]{2,1,0:T(8,128)(2,1)}), bf16[128,8,2688]{2,1,0:T(8,128)(2,1)}, u32[]{:S(2)}, u32[]{:S(2)}) async-start(bf16[128,8,2688]{2,1,0:T(8,128)(2,1)} %bitcast.64), calls=%async_computation.1 | async-start | bytes 11010048 | tf_op jit(solution)/shard_map/all_to_all | solution.py:814
  229.4 0.7 add.189.d_ref
  233.2 63.0 %all-to-all-done.1 = bf16[128,8,2688]{2,1,0:T(8,128)(2,1)} async-done(((bf16[128,8,2688]{2,1,0:T(8,128)(2,1)}), bf16[128,8,2688]{2,1,0:T(8,128)(2,1)}, u32[]{:S(2)}, u32[]{:S(2)}) %all-to-all-start.1) | async-done | bytes 5505056 | tf_op jit(solution)/shard_map/all_to_all | solution.py:814
  296.2 5.3 %home_rows.1 = (bf16[128,8192]{1,0:T(8,128)(2,1)}, bf16[128,1024]{1,0:T(8,128)(2,1)}, bf16[128,1024]{1,0:T(8,128)(2,1)}, bf16[128,128]{1,0:T(8,128)(2,1)}) custom-call(s32[128,1]{1,0:T(8,128)} %add.189.d_ref, bf16[4,256,2688]{2,1,0:T(8,128)(2,1)} %bitcast.16.in_ref), custom_call_target="tpu_custom_call" | custom-call | tf_op jit(solution)/shard_map/home_rows/pallas_call | solution.py:179
  (90 shorter events, 11.3 us)
Async XLA Ops:
  8.6 11.9 %copy-start.6 = (s32[1,6]{1,0:T(1,128)S(1)}, s32[1,6]{1,0:T(1,128)}, u32[]{:S(2)}) copy-start(s32[1,6]{1,0:T(1,128)} %param.19) | copy-start | bytes 76
  8.6 12.9 %copy-start.5 = (f32[32]{0:T(128)S(1)}, f32[32]{0:T(128)}, u32[]{:S(2)}) copy-start(f32[32]{0:T(128)} %param.25) | copy-start | bytes 388
  8.6 12.9 %copy-start.3 = (f32[2,256]{1,0:T(2,128)S(1)}, f32[2,256]{1,0:T(2,128)}, u32[]{:S(2)}) copy-start(f32[2,256]{1,0:T(2,128)} %param.23) | copy-start | bytes 6148
  8.6 78.7 %all-to-all-start = ((bf16[128,8,2688]{2,1,0:T(8,128)(2,1)}), bf16[128,8,2688]{2,1,0:T(8,128)(2,1)}, u32[]{:S(2)}, u32[]{:S(2)}) async-start(bf16[128,8,2688]{2,1,0:T(8,128)(2,1)} %bitcast.63), calls=%async_computation | async-start | bytes 11010048 | tf_op jit(solution)/shard_map/all_to_all | solution.py:814
  87.4 7.2 %copy-start.4 = (f32[32]{0:T(128)S(1)}, f32[32]{0:T(128)}, u32[]{:S(2)}) copy-start(f32[32]{0:T(128)} %param.24) | copy-start | bytes 388
  95.3 22.8 %copy-start.1 = (f32[32,512]{1,0:T(8,128)}, f32[32,512]{1,0:T(8,128)S(1)}, u32[]{:S(2)}) copy-start(f32[32,512]{1,0:T(8,128)S(1)} %get-tuple-element.64.step_ref) | copy-start | bytes 196612
  95.9 5.3 %collective-permute-start = (bf16[8,2688]{1,0:T(8,128)(2,1)S(1)}, bf16[8,2688]{1,0:T(8,128)(2,1)S(1)}, u32[]{:S(2)}, u32[]{:S(2)}) collective-permute-start(bf16[8,2688]{1,0:T(8,128)(2,1)S(1)} %slice.111), channel_id=1, source_target_pairs={{0,4},{4,8},{8,12},{12,16},{16,20},{20,24},{24,28},{1,5},{5,9},{9,... | collective-permute-start | bytes 129032 | tf_op jit(solution)/shard_map/ppermute | solution.py:766
  101.2 1.1 copy-start
  205.2 17.0 %all-to-all-start.3 = ((f32[32,8,84]{2,1,0:T(8,128)}), f32[32,8,84]{2,1,0:T(8,128)S(1)}, u32[]{:S(2)}, u32[]{:S(2)}) async-start(f32[32,8,84]{2,1,0:T(8,128)} %broadcast_in_dim.50), calls=%async_computation.3 | async-start | bytes 262144 | tf_op jit(solution)/shard_map/all_to_all | solution.py:908
  209.1 6.7 %collective-permute-start.1 = (f32[8,2560]{1,0:T(8,128)}, f32[8,2560]{1,0:T(8,128)S(1)}, u32[]{:S(2)}, u32[]{:S(2)}) collective-permute-start(f32[8,2560]{1,0:T(8,128)} %get-tuple-element.44), channel_id=1, source_target_pairs={{4,0},{8,4},{12,8},{16,12},{20,16},{24,20},{28,24},{5,1},{9,5},{13... | collective-permute-start | bytes 245768 | tf_op jit(solution)/shard_map/ppermute | solution.py:766
  215.9 0.6 copy-start.2
  222.2 74.0 %all-to-all-start.1 = ((bf16[128,8,2688]{2,1,0:T(8,128)(2,1)}), bf16[128,8,2688]{2,1,0:T(8,128)(2,1)}, u32[]{:S(2)}, u32[]{:S(2)}) async-start(bf16[128,8,2688]{2,1,0:T(8,128)(2,1)} %bitcast.64), calls=%async_computation.1 | async-start | bytes 11010048 | tf_op jit(solution)/shard_map/all_to_all | solution.py:814

commit v3 on v2

--- a/solution.py
+++ b/solution.py
@@ -29,10 +29,10 @@
 CMAIN = XCOLS + 2 * BCOLS
 OWN_HEADS = HEADS // WAYS
 NEG = -1e30
+STRIDE = 37
 
 F32 = jnp.float32
 BF16 = jnp.bfloat16
-ROUTE = ("head", "dp", "ctx")
 
 
 def dot(left, right):
@@ -55,149 +55,272 @@
     return one_hot(iota((size, size), 0) == iota((size, size), 1))
 
 
-def send_kernel(d_ref, x_ref, b_ref, c_ref, dt_ref, out_ref):
-    way = pl.program_id(0)
+def device_of(slot, head):
+    contexts = lax.axis_size("ctx")
+    return (slot // contexts, lax.rem(slot, contexts), head)
+
+
+def greet_all(barrier, owner, head):
+    for s in range(WAYS):
+        way = lax.rem(head + s, WAYS)
+
+        def greet(t, carry, way=way):
+            pl.semaphore_signal(
+                barrier,
+                inc=1,
+                device_id=device_of(lax.rem(owner + t, OWNERS), way),
+                device_id_type=pl.DeviceIdType.MESH,
+            )
+            return carry
+
+        lax.fori_loop(0 if s else 1, OWNERS, greet, 0)
+
+
+def slot_rows(at):
+    return pl.ds(pl.multiple_of(at * DEPTH * BLK, DEPTH * BLK), DEPTH * BLK)
+
+
+def block_copy(stage_ref, land_ref, send, recv, owner, head, s, t):
+    way = lax.rem(head + s, WAYS)
+    slot = lax.rem(owner + t, OWNERS)
+    return pltpu.make_async_remote_copy(
+        src_ref=stage_ref.at[way, slot_rows(slot), :],
+        dst_ref=land_ref.at[head, slot_rows(owner), :],
+        send_sem=send.at[s, t],
+        recv_sem=recv.at[s, t],
+        device_id=device_of(slot, way),
+        device_id_type=pl.DeviceIdType.MESH,
+    )
+
+
+def over_slots(act):
+    def body(t, carry):
+        act(t)
+        return carry
+
+    lax.fori_loop(1, OWNERS, body, 0)
+
+
+def over_blocks(act):
+    count = WAYS * OWNERS
+
+    def body(m, carry):
+        at = lax.rem(m * STRIDE, count)
+        act(lax.rem(at, WAYS), at // WAYS)
+        return carry
+
+    lax.fori_loop(1, count, body, 0)
+
+
+def route_in_kernel(
+    d_ref, q_ref, x_ref, b_ref, c_ref, dt_ref, out_ref, stage_ref, land_ref, send, recv, own
+):
+    head = lax.axis_index("head")
+    owner = lax.axis_index("dp") * lax.axis_size("ctx") + lax.axis_index("ctx")
+    barrier = pltpu.get_barrier_semaphore()
+    greet_all(barrier, owner, head)
     rows = x_ref.shape[0]
-    spread = one_hot(iota((OWNERS * DEPTH * BLK, rows), 0) == d_ref[...])
-    out_ref[0, :, :XCOLS] = dot(spread, x_ref[...]).astype(BF16)
-    out_ref[0, :, XCOLS : XCOLS + BCOLS] = dot(spread, b_ref[...]).astype(BF16)
-    out_ref[0, :, XCOLS + BCOLS : XCOLS + 2 * BCOLS] = dot(spread, c_ref[...]).astype(BF16)
-    width = HEADS // WAYS
-    lane = iota((LANES, LANES), 1)
-    pick = one_hot((iota((LANES, LANES), 0) == way * width + lane) & (lane < width))
-    dt_part = dot(dt_ref[...], pick).astype(BF16)
-    out_ref[0, :, XCOLS + 2 * BCOLS :] = dot(spread, dt_part).astype(BF16)
-
-
-def send_rows(d_row, x_rows, b_rows, c_rows, dt_rows):
-    rows = x_rows.shape[0]
+    slots = OWNERS * DEPTH * BLK
+    spread = one_hot(iota((slots, rows), 0) == d_ref[...])
+    copies = functools.partial(block_copy, stage_ref, land_ref, send, recv, owner, head)
+    for s in range(WAYS):
+        way = lax.rem(head + s, WAYS)
+
+        def columns(size):
+            return pl.ds(pl.multiple_of(way * size, size), size)
+
+        stage_ref[way, :, :XCOLS] = dot(spread, x_ref[:, columns(XCOLS)]).astype(BF16)
+        stage_ref[way, :, XCOLS : XCOLS + BCOLS] = dot(spread, b_ref[:, columns(BCOLS)]).astype(
+            BF16
+        )
+        stage_ref[way, :, XCOLS + BCOLS : CMAIN] = dot(spread, c_ref[:, columns(BCOLS)]).astype(
+            BF16
+        )
+        lane = iota((LANES, LANES), 1)
+        pick = one_hot(
+            (iota((LANES, LANES), 0) == way * OWN_HEADS + lane) & (lane < OWN_HEADS)
+        )
+        dt_part = dot(dt_ref[...], pick).astype(BF16)
+        stage_ref[way, :, CMAIN:] = dot(spread, dt_part).astype(BF16)
+    pl.semaphore_wait(barrier, WAYS * OWNERS - 1)
+    over_blocks(lambda s, t: copies(s, t).start())
+    kept = pltpu.make_async_copy(
+        stage_ref.at[head, slot_rows(owner), :], land_ref.at[head, slot_rows(owner), :], own
+    )
+    kept.start()
+    kept.wait()
+    part = ROWS // WAYS
+    over_blocks(lambda s, t: copies(s, t).wait_recv())
+    for s in range(WAYS):
+        way = lax.rem(head + WAYS - s, WAYS)
+        pick = one_hot(iota((part, slots), 1) == q_ref[way])
+        out_ref[pl.ds(pl.multiple_of(way * part, part), part), :] = dot(
+            pick, land_ref[way]
+        ).astype(BF16)
+    over_blocks(lambda s, t: copies(s, t).wait_send())
+
+
+def route_in(d_row, q_col, x_rows, b_rows, c_rows, dt_rows):
     slots = OWNERS * DEPTH * BLK
     return pl.pallas_call(
-        send_kernel,
-        grid=(WAYS,),
-        in_specs=[
-            pl.BlockSpec((1, rows), lambda h: (0, 0)),
-            pl.BlockSpec((rows, XCOLS), lambda h: (0, h)),
-            pl.BlockSpec((rows, BCOLS), lambda h: (0, h)),
-            pl.BlockSpec((rows, BCOLS), lambda h: (0, h)),
-            pl.BlockSpec((rows, HEADS), lambda h: (0, 0)),
+        route_in_kernel,
+        in_specs=[pl.BlockSpec(memory_space=pltpu.VMEM)] * 6,
+        out_specs=pl.BlockSpec(memory_space=pltpu.VMEM),
+        out_shape=jax.ShapeDtypeStruct((ROWS, COLS), BF16),
+        scratch_shapes=[
+            pltpu.VMEM((WAYS, slots, COLS), BF16),
+            pltpu.VMEM((WAYS, slots, COLS), BF16),
+            pltpu.SemaphoreType.DMA((WAYS, OWNERS)),
+            pltpu.SemaphoreType.DMA((WAYS, OWNERS)),
+            pltpu.SemaphoreType.DMA,
         ],
-        out_specs=pl.BlockSpec((1, slots, COLS), lambda h: (h, 0, 0)),
-        out_shape=jax.ShapeDtypeStruct((WAYS, slots, COLS), BF16),
-        name="send_rows",
-    )(d_row, x_rows, b_rows, c_rows, dt_rows)
-
-
-def pack_kernel(q_ref, in_ref, out_ref):
-    rows = out_ref.shape[0]
-    slots = in_ref.shape[1]
-    pick = one_hot(iota((rows, slots), 1) == q_ref[0])
-    out_ref[...] = dot(pick, in_ref[0]).astype(BF16)
-
-
-def pack_rows(q_col, landed):
-    slots = landed.shape[1]
+        compiler_params=pltpu.CompilerParams(collective_id=1, has_side_effects=True),
+        name="route_in",
+    )(d_row, q_col, x_rows, b_rows, c_rows, dt_rows)
+
+
+def route_out_kernel(
+    q_ref,
+    d_ref,
+    dx_ref,
+    db_ref,
+    dc_ref,
+    ddt_ref,
+    tail_ref,
+    back_ref,
+    sums_ref,
+    x_ref,
+    b_ref,
+    c_ref,
+    dt_ref,
+    total_ref,
+    stage_ref,
+    land_ref,
+    held_ref,
+    part_ref,
+    send,
+    recv,
+    send1,
+    recv1,
+    send2,
+    recv2,
+    own,
+):
+    head = lax.axis_index("head")
+    owner = lax.axis_index("dp") * lax.axis_size("ctx") + lax.axis_index("ctx")
+    barrier = pltpu.get_barrier_semaphore()
+    greet_all(barrier, owner, head)
     rows = ROWS // WAYS
+    slots = OWNERS * DEPTH * BLK
+    copies = functools.partial(block_copy, stage_ref, land_ref, send, recv, owner, head)
+
+    def sum_copy(t):
+        slot = lax.rem(owner + t, OWNERS)
+        return pltpu.make_async_remote_copy(
+            src_ref=sums_ref.at[slot],
+            dst_ref=held_ref.at[owner],
+            send_sem=send1.at[t],
+            recv_sem=recv1.at[t],
+            device_id=device_of(slot, head),
+            device_id_type=pl.DeviceIdType.MESH,
+        )
+
+    def total_copy(t):
+        return pltpu.make_async_remote_copy(
+            src_ref=part_ref,
+            dst_ref=total_ref.at[owner],
+            send_sem=send2.at[t],
+            recv_sem=recv2.at[t],
+            device_id=device_of(lax.rem(owner + t, OWNERS), head),
+            device_id_type=pl.DeviceIdType.MESH,
+        )
+
+    for s in range(WAYS):
+        way = lax.rem(head + s, WAYS)
+        here = pl.ds(pl.multiple_of(way * rows, rows), rows)
+        spread = one_hot(iota((slots, rows), 0) == q_ref[way])
+
+        def one(ref, low, high):
+            whole = ref[here, :].astype(F32)
+            tail = tail_ref[:, low:high] + back_ref[:, low:high]
+            tail = jnp.where(way == WAYS - 1, tail, whole[rows - 8 :])
+            fixed = jnp.concatenate([whole[: rows - 8], tail])
+            stage_ref[way, :, low:high] = dot(spread, fixed.astype(BF16)).astype(BF16)
+
+        one(dx_ref, 0, XCOLS)
+        one(db_ref, XCOLS, XCOLS + BCOLS)
+        one(dc_ref, XCOLS + BCOLS, CMAIN)
+        stage_ref[way, :, CMAIN:] = dot(spread, ddt_ref[here, :]).astype(BF16)
+    pl.semaphore_wait(barrier, WAYS * OWNERS - 1)
+    over_slots(lambda t: sum_copy(t).start())
+    over_blocks(lambda s, t: copies(s, t).start())
+    kept = pltpu.make_async_copy(
+        stage_ref.at[head, slot_rows(owner), :], land_ref.at[head, slot_rows(owner), :], own
+    )
+    kept.start()
+    kept.wait()
+    held_ref[owner] = sums_ref[owner]
+    over_slots(lambda t: sum_copy(t).wait_recv())
+    total = jnp.sum(held_ref[...], axis=0)
+    part_ref[...] = total
+    total_ref[owner] = total
+    over_slots(lambda t: total_copy(t).start())
+    rows = d_ref.shape[0]
+    pick = one_hot(iota((rows, slots), 1) == d_ref[...])
+    times = jnp.zeros((rows, HEADS), F32)
+    over_blocks(lambda s, t: copies(s, t).wait_recv())
+    for s in range(WAYS):
+        way = lax.rem(head + WAYS - s, WAYS)
+
+        def columns(size):
+            return pl.ds(pl.multiple_of(way * size, size), size)
+
+        x_ref[:, columns(XCOLS)] = dot(pick, land_ref[way, :, :XCOLS]).astype(BF16)
+        b_ref[:, columns(BCOLS)] = dot(pick, land_ref[way, :, XCOLS : XCOLS + BCOLS]).astype(BF16)
+        c_ref[:, columns(BCOLS)] = dot(pick, land_ref[way, :, XCOLS + BCOLS : CMAIN]).astype(BF16)
+        lane = iota((LANES, LANES), 0)
+        put = one_hot(
+            (iota((LANES, LANES), 1) == way * OWN_HEADS + lane) & (lane < OWN_HEADS)
+        )
+        times += dot(dot(pick, land_ref[way, :, CMAIN:]).astype(BF16), put)
+    dt_ref[...] = times.astype(BF16)
+    over_slots(lambda t: total_copy(t).wait_recv())
+    over_slots(lambda t: sum_copy(t).wait_send())
+    over_slots(lambda t: total_copy(t).wait_send())
+    over_blocks(lambda s, t: copies(s, t).wait_send())
+
+
+def route_out(q_row, d_col, dx, db, dc, ddt, tails, back, sums):
+    slots = OWNERS * DEPTH * BLK
+    rows = d_col.shape[0]
+    space = pl.BlockSpec(memory_space=pltpu.VMEM)
     return pl.pallas_call(
-        pack_kernel,
-        grid=(WAYS,),
-        in_specs=[
-            pl.BlockSpec((1, rows, 1), lambda j: (j, 0, 0)),
-            pl.BlockSpec((1, slots, COLS), lambda j: (j, 0, 0)),
-        ],
-        out_specs=pl.BlockSpec((rows, COLS), lambda j: (j, 0)),
-        out_shape=jax.ShapeDtypeStruct((ROWS, COLS), BF16),
-        name="pack_rows",
-    )(q_col, landed)
-
-
-def unpack_kernel(q_ref, x_ref, b_ref, c_ref, dt_ref, tail_ref, back_ref, out_ref):
-    j = pl.program_id(0)
-    rows = x_ref.shape[0]
-    slots = out_ref.shape[1]
-    spread = one_hot(iota((slots, rows), 0) == q_ref[0])
-    last = j == WAYS - 1
-
-    def one(ref, low, high):
-        whole = ref[...].astype(F32)
-        tail = tail_ref[:, low:high] + back_ref[:, low:high]
-        fixed = jnp.concatenate([whole[: rows - 8], jnp.where(last, tail, whole[rows - 8 :])])
-        out_ref[0, :, low:high] = dot(spread, fixed.astype(BF16)).astype(BF16)
-
-    one(x_ref, 0, XCOLS)
-    one(b_ref, XCOLS, XCOLS + BCOLS)
-    one(c_ref, XCOLS + BCOLS, XCOLS + 2 * BCOLS)
-    out_ref[0, :, XCOLS + 2 * BCOLS :] = dot(spread, dt_ref[...]).astype(BF16)
-
-
-def unpack_rows(q_row, dx, db, dc, ddt, tails, back):
-    slots = OWNERS * DEPTH * BLK
-    rows = ROWS // WAYS
-    full = lambda j: (0, 0)
-    return pl.pallas_call(
-        unpack_kernel,
-        grid=(WAYS,),
-        in_specs=[
-            pl.BlockSpec((1, 1, rows), lambda j: (j, 0, 0)),
-            pl.BlockSpec((rows, XCOLS), lambda j: (j, 0)),
-            pl.BlockSpec((rows, BCOLS), lambda j: (j, 0)),
-            pl.BlockSpec((rows, BCOLS), lambda j: (j, 0)),
-            pl.BlockSpec((rows, LANES), lambda j: (j, 0)),
-            pl.BlockSpec((8, CMAIN), full),
-            pl.BlockSpec((8, CMAIN), full),
-        ],
-        out_specs=pl.BlockSpec((1, slots, COLS), lambda j: (j, 0, 0)),
-        out_shape=jax.ShapeDtypeStruct((WAYS, slots, COLS), BF16),
-        name="unpack_rows",
-    )(q_row, dx, db, dc, ddt, tails, back)
-
-
-def home_kernel(d_ref, in_ref, x_ref, b_ref, c_ref, dt_ref, acc_ref):
-    way = pl.program_id(0)
-    rows = x_ref.shape[0]
-    slots = in_ref.shape[1]
-    pick = one_hot(iota((rows, slots), 1) == d_ref[...])
-    x_ref[...] = dot(pick, in_ref[0, :, :XCOLS]).astype(BF16)
-    b_ref[...] = dot(pick, in_ref[0, :, XCOLS : XCOLS + BCOLS]).astype(BF16)
-    c_ref[...] = dot(pick, in_ref[0, :, XCOLS + BCOLS : XCOLS + 2 * BCOLS]).astype(BF16)
-    width = HEADS // WAYS
-    lane = iota((LANES, LANES), 0)
-    put = one_hot((iota((LANES, LANES), 1) == way * width + lane) & (lane < width))
-    dt_part = dot(pick, in_ref[0, :, XCOLS + 2 * BCOLS :]).astype(BF16)
-
-    @pl.when(way == 0)
-    def _():
-        acc_ref[...] = jnp.zeros_like(acc_ref)
-
-    acc_ref[...] += dot(dt_part, put)
-    dt_ref[...] = acc_ref[...].astype(BF16)
-
-
-def home_rows(d_col, landed):
-    slots = landed.shape[1]
-    rows = d_col.shape[0]
-    return pl.pallas_call(
-        home_kernel,
-        grid=(WAYS,),
-        in_specs=[
-            pl.BlockSpec((rows, 1), lambda h: (0, 0)),
-            pl.BlockSpec((1, slots, COLS), lambda h: (h, 0, 0)),
-        ],
-        out_specs=[
-            pl.BlockSpec((rows, XCOLS), lambda h: (0, h)),
-            pl.BlockSpec((rows, BCOLS), lambda h: (0, h)),
-            pl.BlockSpec((rows, BCOLS), lambda h: (0, h)),
-            pl.BlockSpec((rows, HEADS), lambda h: (0, 0)),
-        ],
+        route_out_kernel,
+        in_specs=[space] * 9,
+        out_specs=[space] * 5,
         out_shape=[
             jax.ShapeDtypeStruct((rows, WAYS * XCOLS), BF16),
             jax.ShapeDtypeStruct((rows, WAYS * BCOLS), BF16),
             jax.ShapeDtypeStruct((rows, WAYS * BCOLS), BF16),
             jax.ShapeDtypeStruct((rows, HEADS), BF16),
+            jax.ShapeDtypeStruct((OWNERS, 8, LANES), F32),
         ],
-        scratch_shapes=[pltpu.VMEM((rows, HEADS), F32)],
-        name="home_rows",
-    )(d_col, landed)
+        scratch_shapes=[
+            pltpu.VMEM((WAYS, slots, COLS), BF16),
+            pltpu.VMEM((WAYS, slots, COLS), BF16),
+            pltpu.VMEM((OWNERS, 8, LANES), F32),
+            pltpu.VMEM((8, LANES), F32),
+            pltpu.SemaphoreType.DMA((WAYS, OWNERS)),
+            pltpu.SemaphoreType.DMA((WAYS, OWNERS)),
+            pltpu.SemaphoreType.DMA((OWNERS,)),
+            pltpu.SemaphoreType.DMA((OWNERS,)),
+            pltpu.SemaphoreType.DMA((OWNERS,)),
+            pltpu.SemaphoreType.DMA((OWNERS,)),
+            pltpu.SemaphoreType.DMA,
+        ],
+        compiler_params=pltpu.CompilerParams(collective_id=2, has_side_effects=True),
+        name="route_out",
+    )(q_row, d_col, dx, db, dc, ddt, tails, back, sums)
 
 
 def fill_pad(pad_ref, rows_ref, halo_ref):
@@ -511,6 +634,7 @@
     @pl.when(i == 0)
     def _():
         dpad_ref[...] = jnp.zeros_like(dpad_ref)
+        sums_ref[...] = jnp.zeros_like(sums_ref)
         dcum_ref[...] = jnp.zeros_like(dcum_ref)
         dstep_ref[...] = jnp.zeros_like(dstep_ref)
         dskip_ref[...] = jnp.zeros_like(dskip_ref)
@@ -616,7 +740,7 @@
     front_ref[:, lanes] = moved[0:8]
     tail_ref[:, lanes] = moved[ROWS:]
     dx_ref[...] = moved[8:].astype(BF16)
-    sums_ref[:, lanes] = sums
+    sums_ref[i] = sums
 
     @pl.when(i % GROUP_PAIRS == GROUP_PAIRS - 1)
     def _():
@@ -649,7 +773,7 @@
             front_ref[:, pl.ds(at, LANES)] = moved[0:8]
             tail_ref[:, pl.ds(at, LANES)] = moved[ROWS:]
             out_ref[...] = moved[8:].astype(BF16)
-            sums_ref[:, pl.ds(at, LANES)] = sums
+            sums_ref[left // LANES + i // GROUP_PAIRS] = sums
 
     @pl.when(i == PAIRS - 1)
     def _():
@@ -676,7 +800,7 @@
             jnp.sum(jnp.where(diagonal, value, 0.0), axis=0, keepdims=True)
             for value in (bias_sum, rate_sum, skip_sum)
         ]
-        sums_ref[:, CMAIN:] = jnp.concatenate(lines + [jnp.zeros((5, LANES), F32)])
+        sums_ref[CMAIN // LANES] = jnp.concatenate(lines + [jnp.zeros((5, LANES), F32)])
 
 
 def main_pass(
@@ -721,7 +845,7 @@
             pl.BlockSpec((ROWS, LANES), fixed),
             pl.BlockSpec((8, CMAIN), fixed),
             pl.BlockSpec((8, CMAIN), fixed),
-            pl.BlockSpec((8, COLS), fixed),
+            pl.BlockSpec((OWNERS, 8, LANES), lambda i: (0, 0, 0)),
         ],
         out_shape=[
             jax.ShapeDtypeStruct((ROWS, XCOLS), BF16),
@@ -731,7 +855,7 @@
             jax.ShapeDtypeStruct((ROWS, LANES), BF16),
             jax.ShapeDtypeStruct((8, CMAIN), F32),
             jax.ShapeDtypeStruct((8, CMAIN), F32),
-            jax.ShapeDtypeStruct((8, COLS), F32),
+            jax.ShapeDtypeStruct((OWNERS, 8, LANES), F32),
         ],
         scratch_shapes=[
             pltpu.VMEM((OWN_HEADS, ROWS), F32),
@@ -805,16 +929,7 @@
     comes = ((source * DEPTH + place) * BLK)[:, :, None] + pairs
     comes = comes.reshape(WAYS, LBLOCKS * BLK)
 
-    spread = send_rows(goes[None, :], x_rows, b_rows, c_rows, dt_rows)
-    slots = spread.shape[1]
-    devices = WAYS * OWNERS
-
-    def exchange(value):
-        value = value.reshape(devices, DEPTH * BLK, COLS)
-        value = lax.all_to_all(value, ROUTE, split_axis=0, concat_axis=0, tiled=True)
-        return value.reshape(WAYS, slots, COLS)
-
-    packed = pack_rows(comes[:, :, None], exchange(spread))
+    packed = route_in(goes[None, :], comes[:, :, None], x_rows, b_rows, c_rows, dt_rows)
     halo = passed_along(packed[-8:], "ctx", 1)
 
     start = lax.axis_index("ctx") * ROWS
@@ -897,16 +1012,10 @@
         heads,
     )
     back = passed_along(fronts, "ctx", -1)
-    returned = exchange(unpack_rows(comes[:, None, :], dx, db, dc, ddt, tails, back))
-    x_grad, b_grad, c_grad, dt_grad = home_rows(goes[:, None], returned)
-
-    swap = functools.partial(
-        lax.all_to_all, axis_name=("dp", "ctx"), split_axis=0, concat_axis=0, tiled=True
+    x_grad, b_grad, c_grad, dt_grad, whole = route_out(
+        comes[:, None, :], goes[:, None], dx, db, dc, ddt, tails, back, sums
     )
-    share = COLS // OWNERS
-    partial_sum = jnp.sum(swap(jnp.swapaxes(sums.reshape(8, OWNERS, share), 0, 1)), axis=0)
-    whole = swap(jnp.broadcast_to(partial_sum[None], (OWNERS, 8, share)))
-    whole = jnp.swapaxes(whole, 0, 1).reshape(8, COLS)
+    whole = jnp.swapaxes(whole, 0, 1).reshape(8, OWNERS * LANES)
     sum_x = whole[:, :XCOLS]
     sum_b = whole[:, XCOLS : XCOLS + BCOLS]
     sum_c = whole[:, XCOLS + BCOLS : CMAIN]

time: 303 us -> 299 us (0.987)
  Pallas kernels: 109 us -> 256 us
  waiting for transfers between devices: 126 us -> 2.67 us
  starting transfers between devices: 28.1 us -> 4.66 us
  blocking collectives: 11.9 us -> 0 us
  local copies, waits for them, and re-layouts: 18.5 us -> 25.6 us
    pallas_call x4 -> x2, Pallas kernels: 22.3 us -> 170 us  [the longest x1 85.8 us: route_out(): pl.pallas_call(route_out_kernel, in_specs=[space] * 9, out_specs=[space]...]
    all_to_all x3 -> x0, waiting for transfers between devices: 122 us -> none  [the longest x2 122 us: exchange(): lax.all_to_all(value, ROUTE, split_axis=0, concat_axis=0, tiled=True)]
    all_to_all x3 -> x0, starting transfers between devices: 23 us -> none  [the longest x2 19.1 us: exchange(): lax.all_to_all(value, ROUTE, split_axis=0, concat_axis=0, tiled=True)]
    all_to_all x1 -> x0, blocking collectives: 11.9 us -> none  [on_device(): swap(jnp.swapaxes(sums.reshape(8, OWNERS, share), 0, 1))]
    unnamed x16 -> x26, local copies, waits for them, and re-layouts: 0.82 us -> 6.01 us
  transfers between devices with their start and end apart: 5 -> 2, of which waited for: 3 -> 1; matrix products, arithmetic and copies ran while one was open for 5% -> 3% of each run, Pallas kernels for 2% -> 0%
where the time goes in v3:
time: 299 us; the launch traced here: 298 us
  Pallas kernels  256 us (86%)
  local copies, waits for them, and re-layouts  25.6 us (9%)
  other arithmetic  6.81 us (2%)
  starting transfers between devices  4.66 us (2%)
    pallas_call x1, Pallas kernels, route_out(): pl.pallas_call(route_out_kernel, in_specs=[space] * 9, out_specs=[space]...  85.8 us
    pallas_call x1, Pallas kernels, route_in(): pl.pallas_call(route_in_kernel, in_specs=[pl.BlockSpec(memory_space=pltpu...  83.9 us
    pallas_call x1, Pallas kernels, main_pass(): pl.pallas_call(main_kernel, grid=(PAIRS,), in_specs=[pl.BlockSpec(memory_...  39.2 us
    pallas_call x1, Pallas kernels, exchange_states(): pl.pallas_call(functools.partial(state_kernel, count), in_specs=[pl.Block...  31.8 us
    pallas_call x1, Pallas kernels, first_pass(): pl.pallas_call(first_kernel, grid=(PAIRS,), in_specs=[pl.BlockSpec(memory...  15.8 us
    unnamed x26, local copies, waits for them, and re-layouts  6.01 us
  transfers between devices with their start and end apart: 2, of which 1 were waited for; matrix products, arithmetic and copies ran while one was open for 3% of the time, Pallas kernels for 0%

profile of v3, /device:TPU:1, one launch (start us, length us, event | category | flops | bytes accessed | tf_op | source)
XLA Modules:
  0.0 297.6 jit_solution(5301466726366078861)
XLA Ops:
  0.7 0.8 reshape.413
  1.5 0.8 dynamic_slice.8
  3.6 0.7 add.169.d_ref
  4.2 1.0 copy.74
  5.3 0.8 broadcast_add_fusion.q_ref
  6.1 83.9 %route_in.1.x_ref.b_ref.c_ref = bf16[512,2688]{1,0:T(8,128)(2,1)} custom-call(s32[1,128]{1,0:T(1,128)} %add.169.d_ref, s32[4,128,1]{2,1,0:T(8,128)} %broadcast_add_fusion.q_ref, bf16[128,8192]{1,0:T(8,128)(2,1)} %x_ref.1, bf16[128,1024]{1,0:T(8,128)(2,1)} %b_ref.1, bf16[128,1024]{1,0:T(8,128)(2,1)} %c_ref.1, bf16[128,128]{1,0:T(8,128)(2,1)} %dt_ref.1), custom_call_target="tpu_custom_call" | custom-call | tf_op jit(solution)/shard_map/route_in/pallas_call | solution.py:165
  90.0 0.8 slice.91
  90.8 2.7 collective-permute-start
  94.6 0.9 slice.85
  95.7 0.7 fusion.8
  97.2 1.4 compare_convert_fusion.2
  100.2 0.7 copy.84.rate_ref
  101.1 0.9 reshape.419.rows_ref
  102.5 1.2 broadcast_in_dim.42.keep_ref
  103.7 15.8 %first_pass.1 = (bf16[16,272,128]{2,1,0:T(8,128)(2,1)}, bf16[2048,512]{1,0:T(8,128)(2,1)}, bf16[2048,512]{1,0:T(8,128)(2,1)}, bf16[512,256]{1,0:T(8,128)(2,1)}, ...) custom-call(f32[64]{0:T(128)} %mul.107.gs_ref, f32[16,8,512]{2,1,0:T(8,128)} %reshape.419.rows_ref, ...), custom_call_target="tpu_custom_call" | custom-call | tf_op jit(solution)/shard_map/first_pass/pallas_call | solution.py:464
  119.5 31.8 %exchange_states.1 = bf16[8,2,256,128]{3,2,1,0:T(8,128)(2,1)} custom-call(bf16[8,2,272,128]{3,2,1,0:T(8,128)(2,1)} %bitcast.59), custom_call_target="tpu_custom_call" | custom-call | tf_op jit(solution)/shard_map/exchange_states/pallas_call | solution.py:556
  152.0 0.8 broadcast_in_dim.46.labc_ref
  152.8 1.2 broadcast_in_dim.43.keeps_ref
  154.0 39.2 %main_pass.1 = (bf16[512,2048]{1,0:T(8,128)(2,1)}, bf16[512,2048]{1,0:T(8,128)(2,1)}, bf16[512,256]{1,0:T(8,128)(2,1)}, bf16[512,256]{1,0:T(8,128)(2,1)}, bf16[5...) custom-call(f32[64]{0:T(128)} %mul.107.gs_ref, f32[32]{0:T(128)} %skip_ref.1, ...), custom_call_target="tpu_custom_call" | custom-call | tf_op jit(solution)/shard_map/main_pass/pallas_call | solution.py:815
  193.2 1.9 collective-permute-start.1
  195.1 0.7 add.189.d_ref
  196.5 2.7 collective-permute-done.1.back_ref
  199.1 0.6 copy-done.4
  199.8 85.8 %route_out.1 = (bf16[128,8192]{1,0:T(8,128)(2,1)}, bf16[128,1024]{1,0:T(8,128)(2,1)}, bf16[128,1024]{1,0:T(8,128)(2,1)}, bf16[128,128]{1,0:T(8,128)(2,1)}, f32[32,8,128]{2,1,0:T(8,128)}) custom-call(s32[4,1,128]{2,1,0:T(1,128)} %add.187.q_ref, s32[128,1]{1,0:T(8,128)} %add.189.d_ref, bf16[512,2048]{1,0:T(8,128)(2,1)} %get-tuple-element.40.dx_ref, ...), custom_call_target="tpu_custom_call" | custom-call | tf_op jit(solution)/shard_map/route_out/pallas_call | solution.py:297
  285.6 1.3 slice_bitcast_fusion.2
  286.9 0.7 fusion.25
  287.6 1.4 slice.113
  289.1 0.7 slice_bitcast_fusion.1
  289.8 1.5 slice.110
  292.4 3.2 %copy.99 = bf16[128,8192]{1,0:T(8,128)(2,1)} copy(bf16[128,8192]{1,0:T(8,128)(2,1)} %get-tuple-element.89) | data formatting | bytes 4194304
  295.6 0.7 copy.100
  296.3 0.7 copy.101
  (85 shorter events, 8.5 us)
Async XLA Ops:
  6.1 87.4 %copy-start.9 = (s32[1,6]{1,0:T(1,128)S(1)}, s32[1,6]{1,0:T(1,128)}, u32[]{:S(2)}) copy-start(s32[1,6]{1,0:T(1,128)} %param.19) | copy-start | bytes 76
  6.1 89.5 %copy-start.8 = (f32[32]{0:T(128)S(1)}, f32[32]{0:T(128)}, u32[]{:S(2)}) copy-start(f32[32]{0:T(128)} %param.25) | copy-start | bytes 388
  6.1 89.6 %copy-start.7 = (f32[32]{0:T(128)S(1)}, f32[32]{0:T(128)}, u32[]{:S(2)}) copy-start(f32[32]{0:T(128)} %param.24) | copy-start | bytes 388
  90.0 9.5 %copy-start.6 = (f32[2,256]{1,0:T(2,128)S(1)}, f32[2,256]{1,0:T(2,128)}, u32[]{:S(2)}) copy-start(f32[2,256]{1,0:T(2,128)} %param.23) | copy-start | bytes 6148
  90.8 11.7 %collective-permute-start = (bf16[8,2688]{1,0:T(8,128)(2,1)S(1)}, bf16[8,2688]{1,0:T(8,128)(2,1)S(1)}, u32[]{:S(2)}, u32[]{:S(2)}) collective-permute-start(bf16[8,2688]{1,0:T(8,128)(2,1)S(1)} %slice.91), channel_id=1, source_target_pairs={{0,4},{4,8},{8,12},{12,16},{16,20},{20,24},{24,28},{1,5},{5,9},{9,... | collective-permute-start | bytes 129032 | tf_op jit(solution)/shard_map/ppermute | solution.py:890
  96.4 23.1 %copy-start.1 = (f32[32,512]{1,0:T(8,128)}, f32[32,512]{1,0:T(8,128)S(1)}, u32[]{:S(2)}) copy-start(f32[32,512]{1,0:T(8,128)S(1)} %get-tuple-element.66.step_ref) | copy-start | bytes 196612
  102.5 1.2 copy-start
  193.2 6.0 %collective-permute-start.1 = (f32[8,2560]{1,0:T(8,128)}, f32[8,2560]{1,0:T(8,128)S(1)}, u32[]{:S(2)}, u32[]{:S(2)}) collective-permute-start(f32[8,2560]{1,0:T(8,128)} %get-tuple-element.45), channel_id=1, source_target_pairs={{4,0},{8,4},{12,8},{16,12},{20,16},{24,20},{28,24},{5,1},{9,5},{13... | collective-permute-start | bytes 245768 | tf_op jit(solution)/shard_map/ppermute | solution.py:890
  199.1 0.6 copy-start.4
  292.4 3.2 %copy-start.3 = (bf16[128,1024]{1,0:T(8,128)(2,1)S(1)}, bf16[128,1024]{1,0:T(8,128)(2,1)}, u32[]{:S(2)}) copy-start(bf16[128,1024]{1,0:T(8,128)(2,1)} %get-tuple-element.90) | copy-start | bytes 786436
  292.4 3.9 %copy-start.2 = (bf16[128,1024]{1,0:T(8,128)(2,1)S(1)}, bf16[128,1024]{1,0:T(8,128)(2,1)}, u32[]{:S(2)}) copy-start(bf16[128,1024]{1,0:T(8,128)(2,1)} %get-tuple-element.91) | copy-start | bytes 786436
  292.4 4.6 %copy-start.5 = (bf16[128,128]{1,0:T(8,128)(2,1)S(1)}, bf16[128,128]{1,0:T(8,128)(2,1)}, u32[]{:S(2)}) copy-start(bf16[128,128]{1,0:T(8,128)(2,1)} %get-tuple-element.92) | copy-start | bytes 98308

commit v4 on v3

--- a/solution.py
+++ b/solution.py
@@ -112,8 +112,37 @@
     lax.fori_loop(1, count, body, 0)
 
 
+def as_column(row):
+    size = row.shape[1]
+    diagonal = iota((size, size), 0) == iota((size, size), 1)
+    return jnp.sum(jnp.where(diagonal, row, 0.0), axis=1, keepdims=True)
+
+
 def route_in_kernel(
-    d_ref, q_ref, x_ref, b_ref, c_ref, dt_ref, out_ref, stage_ref, land_ref, send, recv, own
+    d_ref,
+    q_ref,
+    x_ref,
+    b_ref,
+    c_ref,
+    dt_ref,
+    bias_ref,
+    rate_ref,
+    lengths_ref,
+    out_ref,
+    halo_ref,
+    rows_ref,
+    step_ref,
+    sig_ref,
+    gain_ref,
+    label_ref,
+    labr_ref,
+    stage_ref,
+    land_ref,
+    send,
+    recv,
+    own,
+    send_halo,
+    recv_halo,
 ):
     head = lax.axis_index("head")
     owner = lax.axis_index("dp") * lax.axis_size("ctx") + lax.axis_index("ctx")
@@ -149,34 +178,126 @@
     )
     kept.start()
     kept.wait()
+    start = lax.axis_index("ctx") * ROWS
+    ends = []
+    for at in range(lengths_ref.shape[1]):
+        ends.append(lengths_ref[0, at] + (ends[-1] if ends else 0))
+
+    def label_of(places):
+        total = jnp.zeros(places.shape, jnp.int32)
+        for end in ends:
+            total = total + jnp.where(places >= end, 1, 0)
+        return jnp.where(places >= 0, total, -1)
+
+    label_ref[...] = label_of(iota(label_ref.shape, 0) + (start - 8))
+    labr_ref[...] = label_of(iota(labr_ref.shape, 1) + start)
+    labels = labr_ref[0:1, :]
+    lasts = [labels[:, STRETCH - 1 : STRETCH], labels[:, ROWS - 1 : ROWS]]
+    befores = [label_of(iota((1, LANES), 0) + (start - 1))[:, 0:1], lasts[0]]
+    bias, rate = as_column(bias_ref[...]), as_column(rate_ref[...])
     part = ROWS // WAYS
     over_blocks(lambda s, t: copies(s, t).wait_recv())
     for s in range(WAYS):
         way = lax.rem(head + WAYS - s, WAYS)
-        pick = one_hot(iota((part, slots), 1) == q_ref[way])
+        places = as_column(q_ref[way].astype(F32))
+        pick = one_hot(iota((part, slots), 1).astype(F32) == places)
         out_ref[pl.ds(pl.multiple_of(way * part, part), part), :] = dot(
             pick, land_ref[way]
         ).astype(BF16)
+    context = lax.axis_index("ctx")
+    contexts = lax.axis_size("ctx")
+    passed = pltpu.make_async_remote_copy(
+        src_ref=out_ref.at[pl.ds(ROWS - 8, 8), :],
+        dst_ref=halo_ref,
+        send_sem=send_halo,
+        recv_sem=recv_halo,
+        device_id=(lax.axis_index("dp"), lax.rem(context + 1, contexts), head),
+        device_id_type=pl.DeviceIdType.MESH,
+    )
+
+    @pl.when(context < contexts - 1)
+    def _():
+        passed.start()
+
+    @pl.when(context == 0)
+    def _():
+        halo_ref[...] = jnp.zeros_like(halo_ref)
+
+    logits = dot_nt(eye(LANES), out_ref[:, CMAIN:])[:OWN_HEADS] + bias
+    step = jnp.maximum(logits, 0.0) + jnp.log1p(jnp.exp(-jnp.abs(logits)))
+    step_ref[...] = step
+    sig_ref[...] = jax.nn.sigmoid(logits)
+    falls = -rate * step
+    shape = (STRETCH, STRETCH)
+    tri = jnp.where(iota(shape, 0) <= iota(shape, 1), 1.0, 0.0)
+    lane = iota((OWN_HEADS, LANES), 1)
+    gains = jnp.zeros((OWN_HEADS, LANES), F32)
+    for k in range(2):
+        span = slice(k * STRETCH, (k + 1) * STRETCH)
+        cum = lax.dot_general(
+            falls[:, span],
+            tri,
+            (((1,), (0,)), ((), ())),
+            precision=lax.Precision.HIGHEST,
+            preferred_element_type=F32,
+        )
+        end = cum[:, STRETCH - 1 :]
+        own_last = jnp.where(labels[:, span] == lasts[k], 1.0, 0.0)
+        own_first = jnp.where(labels[:, span] == befores[k], 1.0, 0.0)
+        carried = jnp.where(lasts[k] == befores[k], 1.0, 0.0)
+        values = (
+            step[:, span],
+            cum,
+            jnp.exp(end - cum) * own_last,
+            jnp.exp(cum) * own_first,
+        )
+        whole = jnp.exp(end) * carried
+        gains = gains + jnp.where(lane == k, whole, 0.0)
+        for i in range(PAIRS):
+            for at, value in enumerate(values):
+                rows_ref[i, 2 * at : 2 * at + 2, span] = value[2 * i : 2 * i + 2]
+    gain_ref[...] = gains
+
+    @pl.when(context > 0)
+    def _():
+        passed.wait_recv()
+
+    @pl.when(context < contexts - 1)
+    def _():
+        passed.wait_send()
+
     over_blocks(lambda s, t: copies(s, t).wait_send())
 
 
-def route_in(d_row, q_col, x_rows, b_rows, c_rows, dt_rows):
+def route_in(d_row, q_row, x_rows, b_rows, c_rows, dt_rows, bias, rate, lengths):
     slots = OWNERS * DEPTH * BLK
     return pl.pallas_call(
         route_in_kernel,
-        in_specs=[pl.BlockSpec(memory_space=pltpu.VMEM)] * 6,
-        out_specs=pl.BlockSpec(memory_space=pltpu.VMEM),
-        out_shape=jax.ShapeDtypeStruct((ROWS, COLS), BF16),
+        in_specs=[pl.BlockSpec(memory_space=pltpu.VMEM)] * 8
+        + [pl.BlockSpec(memory_space=pltpu.SMEM)],
+        out_specs=[pl.BlockSpec(memory_space=pltpu.VMEM)] * 8,
+        out_shape=[
+            jax.ShapeDtypeStruct((ROWS, COLS), BF16),
+            jax.ShapeDtypeStruct((8, COLS), BF16),
+            jax.ShapeDtypeStruct((PAIRS, 8, ROWS), F32),
+            jax.ShapeDtypeStruct((OWN_HEADS, ROWS), F32),
+            jax.ShapeDtypeStruct((OWN_HEADS, ROWS), F32),
+            jax.ShapeDtypeStruct((OWN_HEADS, LANES), F32),
+            jax.ShapeDtypeStruct((ROWS + 16, LANES), jnp.int32),
+            jax.ShapeDtypeStruct((8, ROWS), jnp.int32),
+        ],
         scratch_shapes=[
             pltpu.VMEM((WAYS, slots, COLS), BF16),
             pltpu.VMEM((WAYS, slots, COLS), BF16),
             pltpu.SemaphoreType.DMA((WAYS, OWNERS)),
             pltpu.SemaphoreType.DMA((WAYS, OWNERS)),
             pltpu.SemaphoreType.DMA,
+            pltpu.SemaphoreType.DMA,
+            pltpu.SemaphoreType.DMA,
         ],
         compiler_params=pltpu.CompilerParams(collective_id=1, has_side_effects=True),
         name="route_in",
-    )(d_row, q_col, x_rows, b_rows, c_rows, dt_rows)
+    )(d_row, q_row, x_rows, b_rows, c_rows, dt_rows, bias, rate, lengths)
 
 
 def route_out_kernel(
@@ -187,12 +308,17 @@
     dc_ref,
     ddt_ref,
     tail_ref,
-    back_ref,
+    front_ref,
     sums_ref,
     x_ref,
     b_ref,
     c_ref,
     dt_ref,
+    xt_ref,
+    bct_ref,
+    xb_ref,
+    bcb_ref,
+    heads_ref,
     total_ref,
     stage_ref,
     land_ref,
@@ -205,6 +331,9 @@
     send2,
     recv2,
     own,
+    back_ref,
+    send3,
+    recv3,
 ):
     head = lax.axis_index("head")
     owner = lax.axis_index("dp") * lax.axis_size("ctx") + lax.axis_index("ctx")
@@ -235,24 +364,49 @@
             device_id_type=pl.DeviceIdType.MESH,
         )
 
-    for s in range(WAYS):
-        way = lax.rem(head + s, WAYS)
-        here = pl.ds(pl.multiple_of(way * rows, rows), rows)
+    context = lax.axis_index("ctx")
+    contexts = lax.axis_size("ctx")
+    passed = pltpu.make_async_remote_copy(
+        src_ref=front_ref,
+        dst_ref=back_ref,
+        send_sem=send3,
+        recv_sem=recv3,
+        device_id=(lax.axis_index("dp"), lax.rem(context + contexts - 1, contexts), head),
+        device_id_type=pl.DeviceIdType.MESH,
+    )
+    for way in range(WAYS):
+        here = slice(way * rows, (way + 1) * rows)
         spread = one_hot(iota((slots, rows), 0) == q_ref[way])
+        if way == WAYS - 1:
+
+            @pl.when(context < contexts - 1)
+            def _():
+                passed.wait_recv()
+
+            @pl.when(context == contexts - 1)
+            def _():
+                back_ref[...] = jnp.zeros_like(back_ref)
 
         def one(ref, low, high):
-            whole = ref[here, :].astype(F32)
-            tail = tail_ref[:, low:high] + back_ref[:, low:high]
-            tail = jnp.where(way == WAYS - 1, tail, whole[rows - 8 :])
-            fixed = jnp.concatenate([whole[: rows - 8], tail])
-            stage_ref[way, :, low:high] = dot(spread, fixed.astype(BF16)).astype(BF16)
+            fixed = ref[here, :]
+            if way == WAYS - 1:
+                whole = fixed.astype(F32)
+                tail = tail_ref[:, low:high] + back_ref[:, low:high]
+                fixed = jnp.concatenate([whole[: rows - 8], tail]).astype(BF16)
+            stage_ref[way, :, low:high] = dot(spread, fixed).astype(BF16)
 
         one(dx_ref, 0, XCOLS)
         one(db_ref, XCOLS, XCOLS + BCOLS)
         one(dc_ref, XCOLS + BCOLS, CMAIN)
         stage_ref[way, :, CMAIN:] = dot(spread, ddt_ref[here, :]).astype(BF16)
-    pl.semaphore_wait(barrier, WAYS * OWNERS - 1)
-    over_slots(lambda t: sum_copy(t).start())
+        if way == 0:
+            pl.semaphore_wait(barrier, WAYS * OWNERS - 1)
+
+            @pl.when(context > 0)
+            def _():
+                passed.start()
+
+            over_slots(lambda t: sum_copy(t).start())
     over_blocks(lambda s, t: copies(s, t).start())
     kept = pltpu.make_async_copy(
         stage_ref.at[head, slot_rows(owner), :], land_ref.at[head, slot_rows(owner), :], own
@@ -285,27 +439,48 @@
         times += dot(dot(pick, land_ref[way, :, CMAIN:]).astype(BF16), put)
     dt_ref[...] = times.astype(BF16)
     over_slots(lambda t: total_copy(t).wait_recv())
+    for i in range(PAIRS):
+        lanes = slice(i * LANES, (i + 1) * LANES)
+        xt_ref[:, lanes] = total_ref[i, 0:KERNEL, :]
+        xb_ref[:, lanes] = total_ref[i, KERNEL : KERNEL + 1, :]
+    for side in range(2):
+        for g in range(BCOLS // LANES):
+            lanes = slice(g * LANES, (g + 1) * LANES)
+            at = (XCOLS + side * BCOLS) // LANES + g
+            bct_ref[side, :, lanes] = total_ref[at, 0:KERNEL, :]
+            bcb_ref[side : side + 1, lanes] = total_ref[at, KERNEL : KERNEL + 1, :]
+    heads_ref[...] = total_ref[CMAIN // LANES, 0:3, 0:OWN_HEADS]
     over_slots(lambda t: sum_copy(t).wait_send())
     over_slots(lambda t: total_copy(t).wait_send())
+
+    @pl.when(context > 0)
+    def _():
+        passed.wait_send()
+
     over_blocks(lambda s, t: copies(s, t).wait_send())
 
 
-def route_out(q_row, d_col, dx, db, dc, ddt, tails, back, sums):
+def route_out(q_row, d_col, dx, db, dc, ddt, tails, fronts, sums):
     slots = OWNERS * DEPTH * BLK
     rows = d_col.shape[0]
     space = pl.BlockSpec(memory_space=pltpu.VMEM)
     return pl.pallas_call(
         route_out_kernel,
         in_specs=[space] * 9,
-        out_specs=[space] * 5,
+        out_specs=[space] * 9,
         out_shape=[
             jax.ShapeDtypeStruct((rows, WAYS * XCOLS), BF16),
             jax.ShapeDtypeStruct((rows, WAYS * BCOLS), BF16),
             jax.ShapeDtypeStruct((rows, WAYS * BCOLS), BF16),
             jax.ShapeDtypeStruct((rows, HEADS), BF16),
-            jax.ShapeDtypeStruct((OWNERS, 8, LANES), F32),
+            jax.ShapeDtypeStruct((KERNEL, XCOLS), F32),
+            jax.ShapeDtypeStruct((2, KERNEL, BCOLS), F32),
+            jax.ShapeDtypeStruct((1, XCOLS), F32),
+            jax.ShapeDtypeStruct((2, BCOLS), F32),
+            jax.ShapeDtypeStruct((3, OWN_HEADS), F32),
         ],
         scratch_shapes=[
+            pltpu.VMEM((OWNERS, 8, LANES), F32),
             pltpu.VMEM((WAYS, slots, COLS), BF16),
             pltpu.VMEM((WAYS, slots, COLS), BF16),
             pltpu.VMEM((OWNERS, 8, LANES), F32),
@@ -317,15 +492,33 @@
             pltpu.SemaphoreType.DMA((OWNERS,)),
             pltpu.SemaphoreType.DMA((OWNERS,)),
             pltpu.SemaphoreType.DMA,
+            pltpu.VMEM((8, CMAIN), F32),
+            pltpu.SemaphoreType.DMA,
+            pltpu.SemaphoreType.DMA,
         ],
         compiler_params=pltpu.CompilerParams(collective_id=2, has_side_effects=True),
         name="route_out",
-    )(q_row, d_col, dx, db, dc, ddt, tails, back, sums)
+    )(q_row, d_col, dx, db, dc, ddt, tails, fronts, sums)
 
 
 def fill_pad(pad_ref, rows_ref, halo_ref):
     pad_ref[0:8, :] = halo_ref[...].astype(F32)
     pad_ref[8 : 8 + ROWS, :] = rows_ref[...].astype(F32)
+
+
+def fill_keep(keep_ref, label_ref):
+    labels = label_ref[8 : 8 + ROWS, :]
+    for k in range(KERNEL - 1):
+        same = label_ref[5 + k : 5 + k + ROWS, :] == labels
+        keep_ref[k] = jnp.where(same, 1.0, 0.0)
+
+
+def fill_keeps(keeps_ref, label_ref):
+    span = ROWS + 8
+    front = label_ref[0:span, :]
+    for k in range(KERNEL - 1):
+        same = label_ref[3 - k : 3 - k + span, :] == front
+        keeps_ref[k] = jnp.where(same & (front >= 0), 1.0, 0.0)
 
 
 def conv_sum(pad_ref, taps, bias, keep_ref):
@@ -388,7 +581,7 @@
     bb_ref,
     ct_ref,
     cb_ref,
-    keep_ref,
+    label_ref,
     og_ref,
     ep_ref,
     xT_ref,
@@ -398,13 +591,18 @@
     e0_ref,
     t1_ref,
     pad_ref,
+    keep_ref,
 ):
     i = pl.program_id(0)
 
+    @pl.when(i == 0)
+    def _():
+        fill_keep(keep_ref, label_ref)
+
     @pl.when(i % GROUP_PAIRS == 0)
     def _():
-        bn_ref[...] = conv_value(pad_ref, b_ref, hb_ref, bt_ref[0], bb_ref[0], keep_ref)
-        cn_ref[...] = conv_value(pad_ref, c_ref, hc_ref, ct_ref[0], cb_ref[0], keep_ref)
+        bn_ref[...] = conv_value(pad_ref, b_ref, hb_ref, bt_ref[0], bb_ref[0:1], keep_ref)
+        cn_ref[...] = conv_value(pad_ref, c_ref, hc_ref, ct_ref[0], cb_ref[1:2], keep_ref)
 
     unit = eye(LANES)
     xc = conv_value(pad_ref, x_ref, hx_ref, xt_ref[...], xb_ref[...], keep_ref)
@@ -422,8 +620,8 @@
         states.append(dot((coef * x_all[:, span]).astype(BF16), bn_ref[span, :]))
         touched.append(dot((gain * g_all[:, span]).astype(BF16), cn_ref[span, :]))
     shape = (LANES, STATE)
-    ga0, ga1 = gs_ref[4 * i], gs_ref[4 * i + 1]
-    gb0, gb1 = gs_ref[4 * i + 2], gs_ref[4 * i + 3]
+    ga0, ga1 = gs_ref[2 * i, 0], gs_ref[2 * i, 1]
+    gb0, gb1 = gs_ref[2 * i + 1, 0], gs_ref[2 * i + 1, 1]
     ep_ref[0, 0:LANES, :] = (pair_scale(ga1, gb1, shape) * states[0] + states[1]).astype(BF16)
     ep_ref[0, LANES : 2 * LANES, :] = (
         touched[0] + pair_scale(ga0, gb0, shape) * touched[1]
@@ -451,10 +649,10 @@
         pl.BlockSpec((KERNEL, LANES), lambda i: (0, i)),
         pl.BlockSpec((1, LANES), lambda i: (0, i)),
         pl.BlockSpec((1, KERNEL, LANES), lambda i: (0, 0, group(i))),
-        pl.BlockSpec((1, 1, LANES), lambda i: (0, 0, group(i))),
+        pl.BlockSpec((2, LANES), lambda i: (0, group(i))),
         pl.BlockSpec((1, KERNEL, LANES), lambda i: (1, 0, group(i))),
-        pl.BlockSpec((1, 1, LANES), lambda i: (1, 0, group(i))),
-        pl.BlockSpec((KERNEL - 1, ROWS, LANES), lambda i: (0, 0, 0)),
+        pl.BlockSpec((2, LANES), lambda i: (0, group(i))),
+        pl.BlockSpec((ROWS + 16, LANES), lambda i: (0, 0)),
     ]
 
 
@@ -488,85 +686,158 @@
             jax.ShapeDtypeStruct((XCOLS, STATE), F32),
             jax.ShapeDtypeStruct((XCOLS, STATE), F32),
         ],
-        scratch_shapes=[pltpu.VMEM((ROWS + 16, LANES), F32)],
+        scratch_shapes=[
+            pltpu.VMEM((ROWS + 16, LANES), F32),
+            pltpu.VMEM((KERNEL - 1, ROWS, LANES), F32),
+        ],
         name="first_pass",
     )(gs, rows, *conv_args, out_grad)
 
 
-def state_kernel(count, in_ref, out_ref, land_ref, part_ref, send, recv, send2, recv2, own, own2):
+def gain_row(ref, at, pair):
+    extra = ref[at, pair, 2 * LANES :, :].astype(F32)
+    return extra[0:1] + extra[8:9]
+
+
+def gain_scale(row):
+    return pair_scale(row[:, 0:1], row[:, HEAD_DIM : HEAD_DIM + 1], (LANES, STATE))
+
+
+ENTER = slice(0, LANES)
+LEAVE = slice(LANES, 2 * LANES)
+
+
+def state_kernel(
+    chips, in_ref, out_ref, near_ref, join_ref, land_ref, part_ref, got_ref, give_ref, send, recv
+):
     me = lax.axis_index("ctx")
     dp, head = lax.axis_index("dp"), lax.axis_index("head")
+    chip, side = me // 2, lax.rem(me, 2)
+    partner = me + 1 - 2 * side
+    pairs = in_ref.shape[1]
+
+    def place(context):
+        return dict(
+            device_id=(dp, context, head), device_id_type=pl.DeviceIdType.MESH
+        )
+
+    def chip_at(d):
+        return lax.rem(chip + d, chips)
+
     barrier = pltpu.get_barrier_semaphore()
-    for d in range(1, count):
-        pl.semaphore_signal(
-            barrier,
-            inc=1,
-            device_id=(dp, lax.rem(me + d, count), head),
-            device_id_type=pl.DeviceIdType.MESH,
+    pl.semaphore_signal(barrier, inc=1, **place(partner))
+    for d in range(1, chips):
+        pl.semaphore_signal(barrier, inc=1, **place(2 * chip_at(d) + side))
+    pl.semaphore_wait(barrier, chips)
+
+    def copy(source, target, stage, d, context):
+        return pltpu.make_async_remote_copy(
+            src_ref=source,
+            dst_ref=target,
+            send_sem=send.at[stage, d],
+            recv_sem=recv.at[stage, d],
+            **place(context),
         )
-    pl.semaphore_wait(barrier, count - 1)
-
-    def moved(source, target, sends, recvs, d):
-        peer = lax.rem(me + d, count)
-        return pltpu.make_async_remote_copy(
-            src_ref=source.at[peer],
-            dst_ref=target.at[me],
-            send_sem=sends.at[d],
-            recv_sem=recvs.at[d],
-            device_id=(dp, peer, head),
-            device_id_type=pl.DeviceIdType.MESH,
-        )
-
-    first = [moved(in_ref, land_ref, send, recv, d) for d in range(1, count)]
-    for copy in first:
-        copy.start()
-    kept = pltpu.make_async_copy(in_ref.at[me], land_ref.at[me], own)
-    kept.start()
-    kept.wait()
-    for copy in first:
-        copy.wait()
-    pairs = land_ref.shape[1]
-    shape = (LANES, STATE)
+
+    def shared(y):
+        return copy(in_ref.at[2 * y + 1 - side], near_ref.at[y], 0, y, partner)
+
+    for y in range(chips):
+        shared(y).start()
+    for y in range(chips):
+        shared(y).wait()
+
+    def both(y, pair, rows):
+        own = in_ref[2 * y + side, pair, rows, :].astype(F32)
+        other = near_ref[y, pair, rows, :].astype(F32)
+        return jnp.where(side == 0, own, other), jnp.where(side == 0, other, own)
+
+    def gain_rows(y, pair):
+        own, other = gain_row(in_ref, 2 * y + side, pair), gain_row(near_ref, y, pair)
+        return jnp.where(side == 0, own, other), jnp.where(side == 0, other, own)
+
+    def joined(d):
+        y = chip_at(d)
+        return copy(join_ref.at[y], land_ref.at[chip], 1, d, 2 * y + side)
+
+    for d in list(range(1, chips)) + [0]:
+        y = chip_at(d)
+        target = join_ref if d else land_ref
+        for pair in range(pairs):
+            first, second = gain_rows(y, pair)
+            e_first, e_second = both(y, pair, ENTER)
+            p_first, p_second = both(y, pair, LEAVE)
+            target[y, pair, ENTER, :] = (gain_scale(second) * e_first + e_second).astype(BF16)
+            target[y, pair, LEAVE, :] = (p_first + gain_scale(first) * p_second).astype(BF16)
+            whole = first * second
+            high = whole.astype(BF16).astype(F32)
+            upper = iota((EXTRA, LANES), 0) < 8
+            target[y, pair, 2 * LANES :, :] = jnp.where(upper, high, whole - high).astype(BF16)
+        if d:
+            joined(d).start()
+    for d in range(1, chips):
+        joined(d).wait()
+
     for pair in range(pairs):
-        gains = []
-        for at in range(count):
-            extra = land_ref[at, pair, 2 * LANES :, :].astype(F32)
-            gain = extra[0:1] + extra[8:9]
-            gains.append(pair_scale(gain[:, 0:1], gain[:, HEAD_DIM : HEAD_DIM + 1], shape))
-        state = jnp.zeros(shape, F32)
-        for at in range(count):
-            part_ref[at, pair, 0:LANES, :] = state.astype(BF16)
-            state = gains[at] * state + land_ref[at, pair, 0:LANES, :].astype(F32)
-        state = jnp.zeros(shape, F32)
-        for at in reversed(range(count)):
-            part_ref[at, pair, LANES : 2 * LANES, :] = state.astype(BF16)
-            state = land_ref[at, pair, LANES : 2 * LANES, :].astype(F32) + gains[at] * state
-    second = [moved(part_ref, out_ref, send2, recv2, d) for d in range(1, count)]
-    for copy in second:
-        copy.start()
-    kept = pltpu.make_async_copy(part_ref.at[me], out_ref.at[me], own2)
-    kept.start()
-    kept.wait()
-    for copy in second:
-        copy.wait()
+        gains = [gain_scale(gain_row(land_ref, at, pair)) for at in range(chips)]
+        state = jnp.zeros((LANES, STATE), F32)
+        for at in range(chips):
+            part_ref[at, pair, ENTER, :] = state.astype(BF16)
+            state = gains[at] * state + land_ref[at, pair, ENTER, :].astype(F32)
+        state = jnp.zeros((LANES, STATE), F32)
+        for at in reversed(range(chips)):
+            part_ref[at, pair, LEAVE, :] = state.astype(BF16)
+            state = land_ref[at, pair, LEAVE, :].astype(F32) + gains[at] * state
+
+    def scanned(d):
+        y = chip_at(d)
+        return copy(part_ref.at[y], got_ref.at[chip], 2, d, 2 * y + side)
+
+    for d in range(1, chips):
+        scanned(d).start()
+    got_ref[chip] = part_ref[chip]
+    for d in range(1, chips):
+        scanned(d).wait()
+
+    def given(y):
+        return copy(give_ref.at[y], out_ref.at[2 * y + side], 3, y, partner)
+
+    for y in range(chips):
+        for pair in range(pairs):
+            first, second = gain_rows(y, pair)
+            e_first, _ = both(y, pair, ENTER)
+            _, p_second = both(y, pair, LEAVE)
+            enter = got_ref[y, pair, ENTER, :].astype(F32)
+            leave = got_ref[y, pair, LEAVE, :].astype(F32)
+            enter_second = gain_scale(first) * enter + e_first
+            leave_first = p_second + gain_scale(second) * leave
+            for rows, one, two in ((ENTER, enter, enter_second), (LEAVE, leave_first, leave)):
+                out_ref[2 * y + side, pair, rows, :] = jnp.where(side == 0, one, two).astype(BF16)
+                give_ref[y, pair, rows, :] = jnp.where(side == 0, two, one).astype(BF16)
+        given(y).start()
+    for y in range(chips):
+        given(y).wait()
 
 
 def exchange_states(parts):
-    count, pairs = parts.shape[:2]
+    count, pairs, tall = parts.shape[:3]
+    chips = count // 2
+    wide = pltpu.VMEM((chips, pairs, tall, STATE), BF16)
+    slim = pltpu.VMEM((chips, pairs, 2 * LANES, STATE), BF16)
     return pl.pallas_call(
-        functools.partial(state_kernel, count),
+        functools.partial(state_kernel, chips),
         in_specs=[pl.BlockSpec(memory_space=pltpu.VMEM)],
         out_specs=pl.BlockSpec(memory_space=pltpu.VMEM),
         out_shape=jax.ShapeDtypeStruct((count, pairs, 2 * LANES, STATE), BF16),
         scratch_shapes=[
-            pltpu.VMEM(parts.shape, BF16),
-            pltpu.VMEM((count, pairs, 2 * LANES, STATE), BF16),
-            pltpu.SemaphoreType.DMA((count,)),
-            pltpu.SemaphoreType.DMA((count,)),
-            pltpu.SemaphoreType.DMA((count,)),
-            pltpu.SemaphoreType.DMA((count,)),
-            pltpu.SemaphoreType.DMA,
-            pltpu.SemaphoreType.DMA,
+            wide,
+            wide,
+            wide,
+            slim,
+            slim,
+            slim,
+            pltpu.SemaphoreType.DMA((4, chips)),
+            pltpu.SemaphoreType.DMA((4, chips)),
         ],
         compiler_params=pltpu.CompilerParams(collective_id=0, has_side_effects=True),
         name="exchange_states",
@@ -589,8 +860,7 @@
     bb_ref,
     ct_ref,
     cb_ref,
-    keep_ref,
-    keeps_ref,
+    label_ref,
     og_ref,
     xT_ref,
     gT_ref,
@@ -600,7 +870,6 @@
     e0_ref,
     t1_ref,
     labr_ref,
-    labc_ref,
     step_ref,
     sig_ref,
     rate_ref,
@@ -625,6 +894,8 @@
     pad_ref,
     dpad_ref,
     dxn_ref,
+    keep_ref,
+    keeps_ref,
 ):
     i = pl.program_id(0)
     unit = eye(LANES)
@@ -633,6 +904,8 @@
 
     @pl.when(i == 0)
     def _():
+        fill_keep(keep_ref, label_ref)
+        fill_keeps(keeps_ref, label_ref)
         dpad_ref[...] = jnp.zeros_like(dpad_ref)
         sums_ref[...] = jnp.zeros_like(sums_ref)
         dcum_ref[...] = jnp.zeros_like(dcum_ref)
@@ -642,7 +915,8 @@
             for t in range(2):
                 shape = (STRETCH, LANES)
                 left = k * STRETCH + t * LANES
-                same = labc_ref[spans[k], :] == labr_ref[0:1, left : left + LANES]
+                low = 8 + k * STRETCH
+                same = label_ref[low : low + STRETCH, :] == labr_ref[0:1, left : left + LANES]
                 lower = iota(shape, 0) >= iota(shape, 1) + t * LANES
                 mask_ref[k, :, t * LANES : (t + 1) * LANES] = jnp.where(same & lower, 0.0, NEG)
 
@@ -660,7 +934,7 @@
     columns = jnp.transpose(rows)
     shape = (LANES, STATE)
     gains = [
-        (gs_ref[4 * i + k], gs_ref[4 * i + 2 + k]) for k in range(2)
+        (gs_ref[2 * i, k], gs_ref[2 * i + 1, k]) for k in range(2)
     ]
     skip = pair_scale(skip_ref[2 * i], skip_ref[2 * i + 1], (LANES, STRETCH))
     enter0 = ent_ref[0, 0:LANES, :].astype(F32)
@@ -752,10 +1026,10 @@
             dcT_ref[:, span] = dcT
             dbT_ref[:, span] = dbT
         sides = (
-            (dbT_ref, b_ref, hb_ref, bt_ref, bb_ref, db_ref, XCOLS),
-            (dcT_ref, c_ref, hc_ref, ct_ref, cb_ref, dc_ref, XCOLS + BCOLS),
+            (dbT_ref, b_ref, hb_ref, bt_ref, bb_ref[0:1], db_ref, XCOLS),
+            (dcT_ref, c_ref, hc_ref, ct_ref, cb_ref[1:2], dc_ref, XCOLS + BCOLS),
         )
-        for grad_ref, in_ref, halo_ref, tap_ref, bias_ref, out_ref, left in sides:
+        for grad_ref, in_ref, halo_ref, tap_ref, bias, out_ref, left in sides:
             for span in spans:
                 dxn_ref[span, :] = dot_nt(wide_unit, grad_ref[:, span].astype(BF16))
             moved, sums = conv_back(
@@ -764,7 +1038,7 @@
                 in_ref,
                 halo_ref,
                 tap_ref[0],
-                bias_ref[0],
+                bias,
                 keep_ref,
                 keeps_ref,
                 dxn_ref[...],
@@ -779,6 +1053,7 @@
     def _():
         shape = (STRETCH, STRETCH)
         tri = jnp.where(iota(shape, 0) >= iota(shape, 1), 1.0, 0.0)
+        rate = as_column(rate_ref[...])
         bias_sum = jnp.zeros((OWN_HEADS, 1), F32)
         rate_sum = jnp.zeros((OWN_HEADS, 1), F32)
         for span in spans:
@@ -789,7 +1064,7 @@
                 precision=lax.Precision.HIGHEST,
                 preferred_element_type=F32,
             )
-            dlogit = (dstep_ref[:, span] - rate_ref[...] * after) * sig_ref[:, span]
+            dlogit = (dstep_ref[:, span] - rate * after) * sig_ref[:, span]
             bias_sum += jnp.sum(dlogit, axis=1, keepdims=True)
             rate_sum -= jnp.sum(after * step_ref[:, span], axis=1, keepdims=True)
             tall = jnp.concatenate([dlogit, jnp.zeros((LANES - OWN_HEADS, STRETCH), F32)])
@@ -804,7 +1079,7 @@
 
 
 def main_pass(
-    gs, skip, rows, conv_args, keeps, out_grad, xT, gT, bn, cn, ent, e0, t1, labr, labc, heads
+    gs, skip, rows, conv_args, out_grad, xT, gT, bn, cn, ent, e0, t1, labr, heads
 ):
     wide = lambda i: (i, 0)
     col = lambda i: (0, i)
@@ -822,7 +1097,6 @@
         ]
         + conv_specs()
         + [
-            pl.BlockSpec((KERNEL - 1, ROWS + 8, LANES), lambda i: (0, 0, 0)),
             pl.BlockSpec((ROWS, LANES), col),
             pl.BlockSpec((LANES, ROWS), wide),
             pl.BlockSpec((LANES, ROWS), wide),
@@ -832,10 +1106,9 @@
             pl.BlockSpec((LANES, STATE), wide),
             pl.BlockSpec((LANES, STATE), wide),
             pl.BlockSpec((8, ROWS), fixed),
-            pl.BlockSpec((ROWS, LANES), fixed),
             pl.BlockSpec((OWN_HEADS, ROWS), fixed),
             pl.BlockSpec((OWN_HEADS, ROWS), fixed),
-            pl.BlockSpec((OWN_HEADS, 1), fixed),
+            pl.BlockSpec((1, OWN_HEADS), fixed),
         ],
         out_specs=[
             pl.BlockSpec((ROWS, LANES), col),
@@ -871,23 +1144,11 @@
             pltpu.VMEM((ROWS + 16, LANES), F32),
             pltpu.VMEM((ROWS + 16, LANES), F32),
             pltpu.VMEM((ROWS, LANES), F32),
+            pltpu.VMEM((KERNEL - 1, ROWS, LANES), F32),
+            pltpu.VMEM((KERNEL - 1, ROWS + 8, LANES), F32),
         ],
         name="main_pass",
-    )(gs, skip, rows, *conv_args, keeps, out_grad, xT, gT, bn, cn, ent, e0, t1, labr, labc, *heads)
-
-
-def segment_of(ends, positions):
-    return jnp.sum((positions[:, None] >= ends[None, :]).astype(jnp.int32), axis=1)
-
-
-def exact(form, left, right):
-    return jnp.einsum(form, left, right, precision=lax.Precision.HIGHEST)
-
-
-def passed_along(value, axis, steps):
-    count = lax.axis_size(axis)
-    first, last = (max(0, -steps), min(count, count - steps))
-    return lax.ppermute(value, axis, [(source, source + steps) for source in range(first, last)])
+    )(gs, skip, rows, *conv_args, out_grad, xT, gT, bn, cn, ent, e0, t1, labr, *heads)
 
 
 def on_device(
@@ -929,47 +1190,19 @@
     comes = ((source * DEPTH + place) * BLK)[:, :, None] + pairs
     comes = comes.reshape(WAYS, LBLOCKS * BLK)
 
-    packed = route_in(goes[None, :], comes[:, :, None], x_rows, b_rows, c_rows, dt_rows)
-    halo = passed_along(packed[-8:], "ctx", 1)
-
-    start = lax.axis_index("ctx") * ROWS
-    ends = jnp.cumsum(trace_lengths[0])
-    positions = start - 8 + jnp.arange(ROWS + 16, dtype=jnp.int32)
-    wide_labels = jnp.where(positions >= 0, segment_of(ends, positions), -1)
-    labels = wide_labels[8 : 8 + ROWS]
-    keep = jnp.stack([wide_labels[5 + k : 5 + k + ROWS] == labels for k in range(KERNEL - 1)])
-    keep = jnp.broadcast_to(keep.astype(F32)[:, :, None], (KERNEL - 1, ROWS, LANES))
-    front = wide_labels[: ROWS + 8]
-    keeps = jnp.stack(
-        [
-            (wide_labels[3 - k : 3 - k + ROWS + 8] == front) & (front >= 0)
-            for k in range(KERNEL - 1)
-        ]
+    heads_dev = dt_bias.shape[0]
+    packed, halo, rows, step, sig, gs, label, labr = route_in(
+        goes[None, :],
+        comes[:, None, :],
+        x_rows,
+        b_rows,
+        c_rows,
+        dt_rows,
+        dt_bias[None, :],
+        decay_rate[None, :],
+        trace_lengths,
     )
-    keeps = jnp.broadcast_to(keeps.astype(F32)[:, :, None], (KERNEL - 1, ROWS + 8, LANES))
-    grid = labels.reshape(2, STRETCH)
-    before = jnp.stack([wide_labels[7], labels[STRETCH - 1]])
-    last_keep = (grid == grid[:, -1:]).astype(F32)
-    first_keep = (grid == before[:, None]).astype(F32)
-    carry_keep = (grid[:, -1] == before).astype(F32)
-    labr = jnp.broadcast_to(labels[None, :], (8, ROWS))
-    labc = jnp.broadcast_to(labels[:, None], (ROWS, LANES))
-
-    heads_dev = dt_bias.shape[0]
-    dt_in = packed[:, XCOLS + 2 * BCOLS : XCOLS + 2 * BCOLS + heads_dev].astype(F32).T
-    logits = dt_in + dt_bias[:, None]
-    step = jax.nn.softplus(logits)
-    sig = jax.nn.sigmoid(logits)
-    tri = jnp.tril(jnp.ones((STRETCH, STRETCH), F32))
-    folded = step.reshape(heads_dev, 2, STRETCH)
-    cum = exact("hks,rs->hkr", -decay_rate[:, None, None] * folded, tri)
-    to_end = jnp.exp(cum[:, :, -1:] - cum) * last_keep[None]
-    gain = jnp.exp(cum) * first_keep[None]
-    gs = (jnp.exp(cum[:, :, -1]) * carry_keep[None]).reshape(-1)
-    rows = jnp.stack([folded, cum, to_end, gain]).reshape(4, PAIRS, 2, ROWS)
-    rows = jnp.swapaxes(rows, 0, 1).reshape(PAIRS, 8, ROWS)
-
-    bias_bc = bc_bias[:, None, :]
+
     conv_args = (
         packed,
         packed,
@@ -980,10 +1213,10 @@
         x_taps,
         x_bias[None, :],
         bc_taps,
-        bias_bc,
+        bc_bias,
         bc_taps,
-        bias_bc,
-        keep,
+        bc_bias,
+        label,
     )
     ep, xT, gT, bn, cn, e0, t1 = first_pass(gs, rows, conv_args, out_grad)
 
@@ -992,13 +1225,12 @@
     ent = exchange_states(ep.reshape(contexts, per, tall, STATE))
     ent = ent.reshape(PAIRS, 2 * LANES, STATE)
 
-    heads = (step, sig, decay_rate[:, None])
+    heads = (step, sig, decay_rate[None, :])
     y, dx, db, dc, ddt, tails, fronts, sums = main_pass(
         gs,
         skip_gain,
         rows,
         conv_args,
-        keeps,
         out_grad,
         xT,
         gT,
@@ -1008,31 +1240,24 @@
         e0,
         t1,
         labr,
-        labc,
         heads,
     )
-    back = passed_along(fronts, "ctx", -1)
-    x_grad, b_grad, c_grad, dt_grad, whole = route_out(
-        comes[:, None, :], goes[:, None], dx, db, dc, ddt, tails, back, sums
+    x_grad, b_grad, c_grad, dt_grad, xt_grad, bct_grad, xb_grad, bcb_grad, heads_grad = route_out(
+        comes[:, None, :], goes[:, None], dx, db, dc, ddt, tails, fronts, sums
     )
-    whole = jnp.swapaxes(whole, 0, 1).reshape(8, OWNERS * LANES)
-    sum_x = whole[:, :XCOLS]
-    sum_b = whole[:, XCOLS : XCOLS + BCOLS]
-    sum_c = whole[:, XCOLS + BCOLS : CMAIN]
-    tail = whole[:, CMAIN : CMAIN + heads_dev]
     return (
         y,
         x_grad,
         b_grad,
         c_grad,
         dt_grad,
-        sum_x[:4],
-        jnp.stack([sum_b[:4], sum_c[:4]]),
-        sum_x[4],
-        jnp.stack([sum_b[4], sum_c[4]]),
-        tail[0],
-        tail[1],
-        tail[2],
+        xt_grad,
+        bct_grad,
+        xb_grad.reshape(-1),
+        bcb_grad,
+        heads_grad[0],
+        heads_grad[1],
+        heads_grad[2],
     )
 
 

time: 299 us -> 267 us (0.89)
  local copies, waits for them, and re-layouts: 25.6 us -> 12.4 us
  other arithmetic: 6.81 us -> 1.36 us
  starting transfers between devices: 4.66 us -> 0 us
  Pallas kernels: 256 us -> 252 us
    slice x9 -> x0, local copies, waits for them, and re-layouts: 6.25 us -> none  [the longest x1 1.46 us: on_device(): sum_x[:4]]
    broadcast_in_dim x6 -> x0, local copies, waits for them, and re-layouts: 5.08 us -> none  [the longest x1 1.18 us: on_device(): jnp.broadcast_to(keeps.astype(F32)[:, :, None], (KERNEL - 1, ROWS + 8, LA...]
    pallas_call x1, Pallas kernels: 31.8 us -> 26.9 us  [exchange_states(): pl.pallas_call(functools.partial(state_kernel, chips), in_specs=[pl.Block...]
    ppermute x2 -> x0, starting transfers between devices: 4.66 us -> none  [passed_along(): lax.ppermute(value, axis, [(source, source + steps) for source in range(f...]
    unnamed x26 -> x22, local copies, waits for them, and re-layouts: 6.01 us -> 7.58 us
  transfers between devices with their start and end apart: 2 -> 0, of which waited for: 1 -> 0; matrix products, arithmetic and copies ran while one was open for 3% -> 0% of each run, Pallas kernels for 0% -> 0%
where the time goes in v4:
time: 267 us; the launch traced here: 266 us
  Pallas kernels  252 us (94%)
  local copies, waits for them, and re-layouts  12.4 us (5%)
    pallas_call x1, Pallas kernels, route_in(): pl.pallas_call(route_in_kernel, in_specs=[pl.BlockSpec(memory_space=pltpu...  85.3 us
    pallas_call x1, Pallas kernels, route_out(): pl.pallas_call(route_out_kernel, in_specs=[space] * 9, out_specs=[space]...  84.7 us
    pallas_call x1, Pallas kernels, main_pass(): pl.pallas_call(main_kernel, grid=(PAIRS,), in_specs=[pl.BlockSpec(memory_...  39 us
    pallas_call x1, Pallas kernels, exchange_states(): pl.pallas_call(functools.partial(state_kernel, chips), in_specs=[pl.Block...  26.9 us
    pallas_call x1, Pallas kernels, first_pass(): pl.pallas_call(first_kernel, grid=(PAIRS,), in_specs=[pl.BlockSpec(memory...  15.9 us
    unnamed x22, local copies, waits for them, and re-layouts  7.58 us

profile of v4, /device:TPU:1, one launch (start us, length us, event | category | flops | bytes accessed | tf_op | source)
XLA Modules:
  0.0 266.3 jit_solution(5303212403720058087)
XLA Ops:
  0.7 0.8 dynamic_slice.8
  1.4 0.1 reshape.219
  1.5 0.3 convert_reduce_fusion
  1.8 0.1 copy.36
  1.9 0.1 copy.37
  2.0 0.2 add.129
  2.1 0.6 broadcast_add_fusion.q_ref
  2.7 0.8 reshape.218
  3.6 0.1 dynamic-slice_reduce_fusion
  3.7 0.1 eq.20
  3.7 0.2 select_reduce_fusion
  4.0 0.2 convert_reduce_fusion.1
  4.1 0.1 iota_add_fusion
  4.2 0.7 add.123.d_ref
  4.9 85.3 %route_in.1 = (bf16[512,2688]{1,0:T(8,128)(2,1)}, bf16[8,2688]{1,0:T(8,128)(2,1)}, f32[16,8,512]{2,1,0:T(8,128)}, f32[32,512]{1,0:T(8,128)}, f32[32,512]{1,0:T(8...) custom-call(s32[1,128]{1,0:T(1,128)} %add.123.d_ref, s32[4,1,128]{2,1,0:T(1,128)} %broadcast_add_fusion.q_ref, ...), custom_call_target="tpu_custom_call" | custom-call | tf_op jit(solution)/shard_map/route_in/pallas_call | solution.py:274
  90.2 15.9 %first_pass.1 = (bf16[16,272,128]{2,1,0:T(8,128)(2,1)}, bf16[2048,512]{1,0:T(8,128)(2,1)}, bf16[2048,512]{1,0:T(8,128)(2,1)}, bf16[512,256]{1,0:T(8,128)(2,1)}, ...) custom-call(f32[32,128]{1,0:T(8,128)} %get-tuple-element.44.gs_ref, ...), custom_call_target="tpu_custom_call" | custom-call | tf_op jit(solution)/shard_map/first_pass/pallas_call | solution.py:662
  106.1 26.9 %exchange_states.1 = bf16[8,2,256,128]{3,2,1,0:T(8,128)(2,1)} custom-call(bf16[8,2,272,128]{3,2,1,0:T(8,128)(2,1)} %bitcast.14), custom_call_target="tpu_custom_call" | custom-call | tf_op jit(solution)/shard_map/exchange_states/pallas_call | solution.py:827
  133.0 39.0 %main_pass.1 = (bf16[512,2048]{1,0:T(8,128)(2,1)}, bf16[512,2048]{1,0:T(8,128)(2,1)}, bf16[512,256]{1,0:T(8,128)(2,1)}, bf16[512,256]{1,0:T(8,128)(2,1)}, bf16[5...) custom-call(f32[32,128]{1,0:T(8,128)} %get-tuple-element.44.gs_ref, ...), custom_call_target="tpu_custom_call" | custom-call | tf_op jit(solution)/shard_map/main_pass/pallas_call | solution.py:1090
  172.0 0.7 add.133.d_ref
  172.7 84.7 %route_out.1 = (bf16[128,8192]{1,0:T(8,128)(2,1)}, bf16[128,1024]{1,0:T(8,128)(2,1)}, bf16[128,1024]{1,0:T(8,128)(2,1)}, bf16[128,128]{1,0:T(8,128)(2,1)}, f32[4...) custom-call(s32[4,1,128]{2,1,0:T(1,128)} %broadcast_add_fusion.q_ref, ...), custom_call_target="tpu_custom_call" | custom-call | tf_op jit(solution)/shard_map/route_out/pallas_call | solution.py:467
  257.4 1.3 slice_bitcast_fusion
  258.7 0.0 copy-start.2
  258.7 0.0 copy-start.5
  258.7 3.1 %copy.47 = bf16[128,8192]{1,0:T(8,128)(2,1)} copy(bf16[128,8192]{1,0:T(8,128)(2,1)} %get-tuple-element.92) | data formatting | bytes 4194304
  261.8 0.0 copy-done.1
  261.8 0.7 copy.48
  262.6 0.7 copy.49
  263.3 0.6 copy.50
  263.9 0.6 copy.51
  264.5 0.6 copy.52
  265.1 0.6 copy.53
  265.7 0.6 copy.54
  (18 shorter events, 0.1 us)
Async XLA Ops:
  258.7 3.2 %copy-start.1 = (bf16[128,1024]{1,0:T(8,128)(2,1)S(1)}, bf16[128,1024]{1,0:T(8,128)(2,1)}, u32[]{:S(2)}) copy-start(bf16[128,1024]{1,0:T(8,128)(2,1)} %get-tuple-element.93) | copy-start | bytes 786436
  258.7 3.9 %copy-start = (bf16[128,1024]{1,0:T(8,128)(2,1)S(1)}, bf16[128,1024]{1,0:T(8,128)(2,1)}, u32[]{:S(2)}) copy-start(bf16[128,1024]{1,0:T(8,128)(2,1)} %get-tuple-element.94) | copy-start | bytes 786436
  258.7 4.6 %copy-start.3 = (bf16[128,128]{1,0:T(8,128)(2,1)S(1)}, bf16[128,128]{1,0:T(8,128)(2,1)}, u32[]{:S(2)}) copy-start(bf16[128,128]{1,0:T(8,128)(2,1)} %get-tuple-element.95) | copy-start | bytes 98308
  258.7 5.2 %copy-start.2 = (f32[4,2048]{1,0:T(4,128)S(1)}, f32[4,2048]{1,0:T(4,128)}, u32[]{:S(2)}) copy-start(f32[4,2048]{1,0:T(4,128)} %get-tuple-element.96) | copy-start | bytes 98308
  258.7 5.8 %copy-start.5 = (f32[2,4,256]{2,1,0:T(4,128)S(1)}, f32[2,4,256]{2,1,0:T(4,128)}, u32[]{:S(2)}) copy-start(f32[2,4,256]{2,1,0:T(4,128)} %get-tuple-element.97) | copy-start | bytes 24580
  258.7 6.4 %copy-start.4 = (f32[1,2048]{1,0:T(1,128)S(1)}, f32[1,2048]{1,0:T(1,128)}, u32[]{:S(2)}) copy-start(f32[1,2048]{1,0:T(1,128)} %get-tuple-element.73) | copy-start | bytes 24580
  258.7 7.0 %copy-start.6 = (f32[2,256]{1,0:T(2,128)S(1)}, f32[2,256]{1,0:T(2,128)}, u32[]{:S(2)}) copy-start(f32[2,256]{1,0:T(2,128)} %get-tuple-element.99) | copy-start | bytes 6148

commit v5 on v4

--- a/solution.py
+++ b/solution.py
@@ -29,7 +29,7 @@
 CMAIN = XCOLS + 2 * BCOLS
 OWN_HEADS = HEADS // WAYS
 NEG = -1e30
-STRIDE = 37
+STRIDE = 11
 
 F32 = jnp.float32
 BF16 = jnp.bfloat16

time: 267 us -> 269 us (level)
  no operation moved by 1% of the time
where the time goes in v5:
time: 269 us; the launch traced here: 268 us
  Pallas kernels  254 us (94%)
  local copies, waits for them, and re-layouts  12.4 us (5%)
    pallas_call x1, Pallas kernels, route_out(): pl.pallas_call(route_out_kernel, in_specs=[space] * 9, out_specs=[space]...  86.3 us
    pallas_call x1, Pallas kernels, route_in(): pl.pallas_call(route_in_kernel, in_specs=[pl.BlockSpec(memory_space=pltpu...  86.1 us
    pallas_call x1, Pallas kernels, main_pass(): pl.pallas_call(main_kernel, grid=(PAIRS,), in_specs=[pl.BlockSpec(memory_...  39 us
    pallas_call x1, Pallas kernels, exchange_states(): pl.pallas_call(functools.partial(state_kernel, chips), in_specs=[pl.Block...  26.6 us
    pallas_call x1, Pallas kernels, first_pass(): pl.pallas_call(first_kernel, grid=(PAIRS,), in_specs=[pl.BlockSpec(memory...  15.9 us
    unnamed x22, local copies, waits for them, and re-layouts  7.58 us

profile of v5, /device:TPU:1, one launch (start us, length us, event | category | flops | bytes accessed | tf_op | source)
XLA Modules:
  0.0 268.4 jit_solution(8429237076544100935)
XLA Ops:
  0.7 0.8 dynamic_slice.8
  1.4 0.1 reshape.219
  1.5 0.3 convert_reduce_fusion
  1.8 0.1 copy.36
  1.9 0.1 copy.37
  2.0 0.2 add.129
  2.1 0.6 broadcast_add_fusion.q_ref
  2.7 0.8 reshape.218
  3.6 0.1 dynamic-slice_reduce_fusion
  3.7 0.1 eq.20
  3.7 0.2 select_reduce_fusion
  4.0 0.2 convert_reduce_fusion.1
  4.1 0.1 iota_add_fusion
  4.2 0.7 add.123.d_ref
  4.9 86.1 %route_in.1 = (bf16[512,2688]{1,0:T(8,128)(2,1)}, bf16[8,2688]{1,0:T(8,128)(2,1)}, f32[16,8,512]{2,1,0:T(8,128)}, f32[32,512]{1,0:T(8,128)}, f32[32,512]{1,0:T(8...) custom-call(s32[1,128]{1,0:T(1,128)} %add.123.d_ref, s32[4,1,128]{2,1,0:T(1,128)} %broadcast_add_fusion.q_ref, ...), custom_call_target="tpu_custom_call" | custom-call | tf_op jit(solution)/shard_map/route_in/pallas_call | solution.py:274
  91.0 15.9 %first_pass.1 = (bf16[16,272,128]{2,1,0:T(8,128)(2,1)}, bf16[2048,512]{1,0:T(8,128)(2,1)}, bf16[2048,512]{1,0:T(8,128)(2,1)}, bf16[512,256]{1,0:T(8,128)(2,1)}, ...) custom-call(f32[32,128]{1,0:T(8,128)} %get-tuple-element.44.gs_ref, ...), custom_call_target="tpu_custom_call" | custom-call | tf_op jit(solution)/shard_map/first_pass/pallas_call | solution.py:662
  106.9 26.6 %exchange_states.1 = bf16[8,2,256,128]{3,2,1,0:T(8,128)(2,1)} custom-call(bf16[8,2,272,128]{3,2,1,0:T(8,128)(2,1)} %bitcast.14), custom_call_target="tpu_custom_call" | custom-call | tf_op jit(solution)/shard_map/exchange_states/pallas_call | solution.py:827
  133.5 39.0 %main_pass.1 = (bf16[512,2048]{1,0:T(8,128)(2,1)}, bf16[512,2048]{1,0:T(8,128)(2,1)}, bf16[512,256]{1,0:T(8,128)(2,1)}, bf16[512,256]{1,0:T(8,128)(2,1)}, bf16[5...) custom-call(f32[32,128]{1,0:T(8,128)} %get-tuple-element.44.gs_ref, ...), custom_call_target="tpu_custom_call" | custom-call | tf_op jit(solution)/shard_map/main_pass/pallas_call | solution.py:1090
  172.5 0.7 add.133.d_ref
  173.2 86.3 %route_out.1 = (bf16[128,8192]{1,0:T(8,128)(2,1)}, bf16[128,1024]{1,0:T(8,128)(2,1)}, bf16[128,1024]{1,0:T(8,128)(2,1)}, bf16[128,128]{1,0:T(8,128)(2,1)}, f32[4...) custom-call(s32[4,1,128]{2,1,0:T(1,128)} %broadcast_add_fusion.q_ref, ...), custom_call_target="tpu_custom_call" | custom-call | tf_op jit(solution)/shard_map/route_out/pallas_call | solution.py:467
  259.5 1.3 slice_bitcast_fusion
  260.8 3.1 %copy.47 = bf16[128,8192]{1,0:T(8,128)(2,1)} copy(bf16[128,8192]{1,0:T(8,128)(2,1)} %get-tuple-element.92) | data formatting | bytes 4194304
  264.0 0.0 copy-done.1
  264.0 0.7 copy.48
  264.7 0.7 copy.49
  265.4 0.0 copy-done.3
  265.4 0.6 copy.50
  266.0 0.6 copy.51
  266.6 0.6 copy.52
  267.2 0.6 copy.53
  267.8 0.0 copy-done.6
  267.8 0.6 copy.54
  (18 shorter events, 0.1 us)
Async XLA Ops:
  260.8 3.2 %copy-start.1 = (bf16[128,1024]{1,0:T(8,128)(2,1)S(1)}, bf16[128,1024]{1,0:T(8,128)(2,1)}, u32[]{:S(2)}) copy-start(bf16[128,1024]{1,0:T(8,128)(2,1)} %get-tuple-element.93) | copy-start | bytes 786436
  260.8 3.9 %copy-start = (bf16[128,1024]{1,0:T(8,128)(2,1)S(1)}, bf16[128,1024]{1,0:T(8,128)(2,1)}, u32[]{:S(2)}) copy-start(bf16[128,1024]{1,0:T(8,128)(2,1)} %get-tuple-element.94) | copy-start | bytes 786436
  260.8 4.6 %copy-start.3 = (bf16[128,128]{1,0:T(8,128)(2,1)S(1)}, bf16[128,128]{1,0:T(8,128)(2,1)}, u32[]{:S(2)}) copy-start(bf16[128,128]{1,0:T(8,128)(2,1)} %get-tuple-element.95) | copy-start | bytes 98308
  260.8 5.2 %copy-start.2 = (f32[4,2048]{1,0:T(4,128)S(1)}, f32[4,2048]{1,0:T(4,128)}, u32[]{:S(2)}) copy-start(f32[4,2048]{1,0:T(4,128)} %get-tuple-element.96) | copy-start | bytes 98308
  260.8 5.8 %copy-start.5 = (f32[2,4,256]{2,1,0:T(4,128)S(1)}, f32[2,4,256]{2,1,0:T(4,128)}, u32[]{:S(2)}) copy-start(f32[2,4,256]{2,1,0:T(4,128)} %get-tuple-element.97) | copy-start | bytes 24580
  260.8 6.4 %copy-start.4 = (f32[1,2048]{1,0:T(1,128)S(1)}, f32[1,2048]{1,0:T(1,128)}, u32[]{:S(2)}) copy-start(f32[1,2048]{1,0:T(1,128)} %get-tuple-element.73) | copy-start | bytes 24580
  260.8 7.0 %copy-start.6 = (f32[2,256]{1,0:T(2,128)S(1)}, f32[2,256]{1,0:T(2,128)}, u32[]{:S(2)}) copy-start(f32[2,256]{1,0:T(2,128)} %get-tuple-element.99) | copy-start | bytes 6148
